TPU v7x, 32 devices: a whole 2x2x4 slice. The times are simulated.
32 devices in a mesh: grp: 4 (over x, core), row: 8 (over z, y).
Axes of the slice: x: 2, y: 2, z: 4, core: 2. Of those that a mesh axis runs over, the one named last changes fastest.
Arguments:
- features: bfloat16 [2048, 4096], P('row', 'grp'), may hold values from -0.125 to 0.125
- residual: float32 [2048, 576], P('row'), may hold values from -6 to 6
- precond: float32 [4096, 1024], P('grp'), as said below
Outputs:
- coefs: float32 [4096, 576], P('grp')
- section_resid: float32 [4, 2048, 576], P('grp', 'row')
Inputs may be any that keep to these rules, and one draw needn't show every extreme that they name: Each 1024 x 1024 block of precond is symmetric and positive definite.
All inputs are finite; a program needn't handle non-finite values.
Results may differ from a plain program's by a relative error of at most 0.009.
Values may be sent and summed in bfloat16 or wider, within the bound.
No kernel may reach another device: no remote copies, remote signals or barrier semaphores. Data moves between devices by JAX's collectives and lax.ppermute only.
A program may use at most 64 MiB of HBM per device.

v0:
```python
import functools

import jax
import jax.numpy as jnp
from jax import lax
from jax.experimental import pallas as pl
from jax.experimental.pallas import tpu as pltpu
from jax.sharding import PartitionSpec as P


F32 = jnp.float32
BF16 = jnp.bfloat16
CORES = 2
PAIR = 2
TILE = 8
VMEM = pl.BlockSpec(memory_space=pltpu.VMEM)
SCALARS = pl.BlockSpec(memory_space=pltpu.SMEM)
GRANT = 24 * 1024 * 1024


def grouped(refs, layout):
    out, at = [], 0
    for size in layout:
        out.append(refs[at:at + size])
        at += size
    return out


def correlation(r_ref, blocks, c_ref):
    rows, feats = blocks[0][0].shape[0], c_ref.shape[1]
    cut = feats // 2
    whole = [(q, b[0]) for q, b in enumerate(blocks) if len(b) == 1]
    split = [(q, b) for q, b in enumerate(blocks) if len(b) == 2]
    lhs = [r_ref[:, q * rows:(q + 1) * rows].astype(BF16) for q in range(len(blocks))]
    for k in range(2):
        span = pl.ds(k * cut, cut)
        total = None
        for q, block in whole:
            part = jnp.dot(lhs[q], block[:, span], preferred_element_type=F32)
            total = part if total is None else total + part
        for q, block in split:
            total += jnp.dot(lhs[q], block[k][...], preferred_element_type=F32)
        c_ref[:, span] = total.astype(BF16)


def core_is(index):
    return lax.axis_index("grp") % CORES == index


def first_kernel(layout, owner, r_ref, *refs):
    count = sum(layout)

    @pl.when(core_is(owner))
    def _():
        correlation(r_ref, grouped(refs[:count], layout), refs[2 * count])

    @pl.when(core_is(1 - owner))
    def _():
        correlation(r_ref, grouped(refs[count:2 * count], layout), refs[2 * count])


def stage_kernel(layout, owner, r_ref, ca_ref, cb_ref, own_ref, other_ref, *refs):
    count = sum(layout)
    w_ref, rn_ref = refs[2 * count:]
    width = ca_ref.shape[0]
    total = ca_ref[...].astype(F32) + cb_ref[...].astype(F32)
    high = total.astype(BF16)
    low = (total - high.astype(F32)).astype(BF16)
    stacked = jnp.concatenate((high, low), axis=0)

    def run(map_ref, blocks):
        both = jnp.dot(stacked, map_ref[...], preferred_element_type=F32)
        wb = (both[:width] + both[width:]).astype(BF16)
        w_ref[...] = wb
        rows = blocks[0][0].shape[0]
        cut = wb.shape[1] // 2
        for q, block in enumerate(blocks):
            span = pl.ds(q * rows, rows)
            if len(block) == 1:
                change = product(wb, block[0])
            else:
                change = product(wb[:, :cut], block[0]) + product(wb[:, cut:], block[1])
            rn_ref[:, span] = (r_ref[:, span].astype(F32) - change).astype(rn_ref.dtype)

    @pl.when(core_is(owner))
    def _():
        run(own_ref, grouped(refs[:count], layout))

    @pl.when(core_is(1 - owner))
    def _():
        run(other_ref, grouped(refs[count:2 * count], layout))


def product(w, a_ref):
    return lax.dot_general(w, a_ref[...], (((1,), (1,)), ((), ())), preferred_element_type=F32)


def spans(info_ref, count, height):
    if height % TILE:
        return [pl.ds(q * height, height) for q in range(count)]
    return [pl.ds(pl.multiple_of(info_ref[q], TILE), height) for q in range(count)]


def rows_of(ref, q, height):
    return ref[q * height:(q + 1) * height, :]


def both_panels(first_core, own, got):
    return jnp.concatenate((own, got) if first_core else (got, own), axis=0)


def update_kernel(count, info_ref, own_ref, other_ref, base_ref, got_ref, *refs):
    parts, out_ref = refs[:count], refs[count]
    height = parts[0].shape[0]

    def run(first_core, a_ref):
        for q, at in enumerate(spans(info_ref, count, 2 * height)):
            w = both_panels(first_core, parts[q][...], rows_of(got_ref, q, height))
            out_ref[at, :] = base_ref[at, :] - product(w, a_ref)

    pl.when(core_is(0))(functools.partial(run, True, own_ref))
    pl.when(core_is(1))(functools.partial(run, False, other_ref))


def final_kernel(count, early, info_ref, a_ref, after_ref, got_ref, *refs):
    first, second = refs[:count], refs[count:2 * count]
    got_early, got_late = refs[2 * count:2 * count + 2]
    coef_ref, resid_ref = refs[2 * count + 2:]
    height = first[0].shape[0]
    places = spans(info_ref, count, 2 * height)

    @pl.when(core_is(0))
    def _():
        for q, at in enumerate(places):
            w = both_panels(True, first[q][...], rows_of(got_ref, q, height))
            coef_ref[at, :] = w.astype(F32)
        resid_ref[...] = after_ref[...]

    @pl.when(core_is(1))
    def _():
        for q, at in enumerate(places):
            source, k = (got_early, q) if q < early else (got_late, q - early)
            w = both_panels(False, second[q][...], rows_of(source, k, height))
            coef_ref[at, :] = w.astype(F32)
            resid_ref[at, :] = after_ref[at, :] - product(w, a_ref)


def base_kernel(count, info_ref, turned_ref, got_ref, *refs):
    parts, out_ref = refs[:count], refs[count]
    height = parts[0].shape[0]
    first_plane = lax.axis_index("grp") < CORES

    @pl.when(first_plane)
    def _():
        out_ref[...] = turned_ref[...]

    def run(first_core):
        for q, at in enumerate(spans(info_ref, count, 2 * height)):
            r = both_panels(first_core, parts[q][...], rows_of(got_ref, q, height))
            out_ref[at, :] = r.astype(F32)

    later = jnp.logical_not(first_plane)
    pl.when(jnp.logical_and(later, core_is(0)))(functools.partial(run, True))
    pl.when(jnp.logical_and(later, core_is(1)))(functools.partial(run, False))


def local_call(body, out_shape, info, arrays):
    many = isinstance(out_shape, (list, tuple))
    return pl.pallas_call(
        body,
        out_shape=out_shape,
        in_specs=[pl.BlockSpec(memory_space=pltpu.SMEM)] + [VMEM] * len(arrays),
        out_specs=[VMEM] * len(out_shape) if many else VMEM,
        compiler_params=pltpu.CompilerParams(vmem_limit_bytes=GRANT),
    )(info, *arrays)


def first_call(owner, layout, panel, own, other):
    feats = own[0].shape[1]
    width, rows = panel.shape
    return pl.pallas_call(
        functools.partial(first_kernel, layout, owner),
        out_shape=jax.ShapeDtypeStruct((width, feats), BF16),
        in_specs=[VMEM] * (1 + 2 * len(own)),
        out_specs=VMEM,
        cost_estimate=pl.CostEstimate(
            flops=2 * width * rows * feats, bytes_accessed=2 * rows * feats, transcendentals=0
        ),
        compiler_params=pltpu.CompilerParams(vmem_limit_bytes=GRANT),
        name="first_corr",
    )(panel, *own, *other)


def stage_call(owner, layout, panel, ca, cb, squares, own, other, kind):
    feats = own[0].shape[1]
    width, rows = panel.shape
    return pl.pallas_call(
        functools.partial(stage_kernel, layout, owner),
        out_shape=[jax.ShapeDtypeStruct((width, feats), BF16), jax.ShapeDtypeStruct(panel.shape, kind)],
        in_specs=[VMEM] * (5 + 2 * len(own)),
        out_specs=[VMEM] * 2,
        cost_estimate=pl.CostEstimate(
            flops=2 * width * feats * (2 * feats + rows),
            bytes_accessed=2 * feats * (feats + rows),
            transcendentals=0,
        ),
        compiler_params=pltpu.CompilerParams(vmem_limit_bytes=GRANT),
        name="sweep_stage",
    )(panel, ca, cb, *squares, *own, *other)


def sweep(features, residual, precond):
    grp_count, row_count = lax.axis_size("grp"), lax.axis_size("row")
    g, r = lax.axis_index("grp"), lax.axis_index("row")
    core = g % CORES
    plane = g // CORES
    plane_count = grp_count // CORES
    rows, feats = features.shape
    targets = residual.shape[1]
    panel_count = row_count // PAIR * CORES
    width = targets // panel_count

    def permute(x, mask=0, flip=0, keep=None, shift=0):
        route = []
        for a in range(grp_count):
            if keep is not None and a % CORES != keep:
                continue
            b = (a ^ flip) + shift
            if b >= grp_count:
                continue
            for i in range(row_count):
                route.append((a * row_count + i, b * row_count + (i ^ mask)))
        return lax.ppermute(x, ("grp", "row"), route)

    bits = [1 << i for i in range(row_count.bit_length() - 1) if (1 << i) != PAIR]
    masks = [0]
    for bit in reversed(bits):
        masks += [m ^ bit for m in masks]

    def place_of(index):
        return (index // (2 * PAIR)) * PAIR + index % PAIR

    def after(x, *others):
        return lax.optimization_barrier((x,) + others)[0]

    ranks = jnp.stack([place_of(r ^ m) for m in masks])

    def ordered(parts):
        if CORES * width % TILE == 0:
            return parts
        stacked = jnp.take(jnp.stack(parts), jnp.argsort(ranks), axis=0)
        return [stacked[q] for q in range(len(parts))]

    info = jnp.stack(
        [place_of(r ^ m) * CORES * width for m in masks]
    ).astype(jnp.int32)
    starts = [((place_of(r ^ m) * CORES + core) * width).astype(jnp.uint32) for m in masks]
    on_first = core == 0
    at_plane = [plane == step for step in range(plane_count)]
    features, info, starts, on_first, at_plane = lax.optimization_barrier(
        (features, info, starts, on_first, at_plane)
    )
    far = bits[-1]
    near = bits[:-1]
    count = len(masks)
    halves = [features[:, : feats // 2], features[:, feats // 2 :]]

    held = {0: [features]}
    held[far] = [permute(x, mask=far) for x in halves]
    for bit in reversed(near):
        for m in masks:
            if m not in held and (m ^ bit) in held and not m & far:
                held[m] = [permute(x, mask=bit) for x in held[m ^ bit]]
    swapped = permute(features, flip=1)
    square = after(precond, swapped).astype(BF16)
    squares = (square, permute(square, flip=1))

    turned = residual.T
    zero = jnp.uint32(0)

    def slice_for(k):
        return lax.dynamic_slice(turned, (starts[k], zero), (width, rows))

    slices = [slice_for(k).astype(BF16) if m else slice_for(k) for k, m in enumerate(masks)]
    moved = [permute(x, mask=m) for x, m in zip(slices, masks) if m]
    panel = jnp.concatenate([slices[0]] + [x.astype(F32) for x in moved], axis=1)

    held[far][0], squares = lax.optimization_barrier((held[far][0], squares))
    for bit in reversed(near):
        for m in masks:
            if m not in held and (m ^ bit) in held and m & far:
                held[m] = [permute(x, mask=bit) for x in held[m ^ bit]]
    got_blocks = {0: [swapped]}
    for m in masks[1:]:
        got_blocks[m] = [permute(x, flip=1) for x in held[m]]
    layout = [len(held[m]) for m in masks]
    mine = [x for m in masks for x in held[m]]
    theirs = [x for m in masks for x in got_blocks[m]]

    keep_first = keep_second = passed = blocks = None
    for step in range(plane_count):
        end = step + 1 == plane_count
        corr = first_call(0, layout, panel, mine, theirs)
        got = permute(corr, mask=PAIR)
        if end and passed is not None:
            blocks = [passed[:, k * rows:(k + 1) * rows] for k in range(count)]
            blocks = [permute(x, mask=m) if m else x for x, m in zip(blocks, masks)]
        w1, panel1 = stage_call(0, layout, panel, corr, got, squares, mine, theirs, F32)
        keep_first = w1 if keep_first is None else jnp.where(at_plane[step], w1, keep_first)
        corr = first_call(1, layout, panel1, mine, theirs)
        got = permute(corr, mask=PAIR)
        w2, panel2 = stage_call(1, layout, panel1, corr, got, squares, mine, theirs, BF16)
        keep_second = w2 if keep_second is None else jnp.where(at_plane[step], w2, keep_second)
        if not end:
            panel = permute(panel2, shift=CORES)
            passed = panel if passed is None else jnp.where(at_plane[step + 1], panel, passed)

    def gather(pair):
        parts = {0: pair}
        for bit in reversed(bits):
            for m in list(parts):
                parts[m ^ bit] = permute(parts[m], mask=bit)
        return ordered([parts[m] for m in masks])

    first_parts = gather(keep_first)
    second_parts = gather(keep_second)
    first_got = permute(jnp.concatenate(first_parts, axis=0), flip=1)
    early = max(count - 1, 1)
    got_early = permute(jnp.concatenate(second_parts[:early], axis=0), flip=1)
    whole = jax.ShapeDtypeStruct((targets, rows), F32)
    base = turned
    if blocks is not None:
        blocks = ordered(blocks)
        base_got = permute(jnp.concatenate(blocks, axis=0), flip=1)
        base = local_call(
            functools.partial(base_kernel, count), whole, info, [turned, base_got] + blocks
        )
    after_first = local_call(
        functools.partial(update_kernel, count),
        whole,
        info,
        [features, swapped, base, first_got] + first_parts,
    )
    late = second_parts[early:] or second_parts[:1]
    got_late = permute(after(jnp.concatenate(late, axis=0), after_first), flip=1)
    coef_t, resid_t = local_call(
        functools.partial(final_kernel, count, early),
        [jax.ShapeDtypeStruct((targets, feats), F32), whole],
        info,
        [features, after_first, first_got] + first_parts + second_parts + [got_early, got_late],
    )
    return coef_t.T, resid_t.T[None]


def solution(mesh):
    placed = (P("row", "grp"), P("row", None), P("grp", None))

    return jax.shard_map(
        sweep,
        mesh=mesh,
        in_specs=placed,
        out_specs=(P("grp", None), P("grp", "row", None)),
        check_vma=False,
    )
```

profile of v0, /device:TPU:11, one launch (start us, length us, event | category | flops | bytes accessed | tf_op | source)
XLA Modules:
  0.0 109.9 jit_solution(6960469183682873278)
XLA Ops:
  0.9 0.7 collective-permute-start
  1.6 1.7 %collective-permute-done.refs_6_.other_ref = bf16[256,1024]{1,0:T(8,128)(2,1)S(1)} collective-permute-done((bf16[256,1024]{1,0:T(8,128)(2,1)}, bf16[256,1024]{1,0:T(8,128)(2,1)S(1)}, u32[]{:S(2)}, u32[]{:S(2)}) %collective-permute-start) | collective-permute-done | bytes 524320 | tf_op jit(solution)/shard_map/ppermute | solution.py:233
  3.3 2.5 %convert_element_type.55.own_ref = bf16[1024,1024]{1,0:T(8,128)(2,1)S(1)} convert(f32[1024,1024]{1,0:T(8,128)} %param.5) | non-fusion elementwise | flops 1048576 | bytes 6291456 | tf_op jit(solution)/shard_map/convert_element_type | solution.py:275
  6.3 1.2 %collective-permute-start.7 = (bf16[256,1024]{1,0:T(8,128)(2,1)S(1)}, bf16[256,1024]{1,0:T(8,128)(2,1)S(1)}, u32[]{:S(2)}, u32[]{:S(2)}) collective-permute-start(bf16[256,1024]{1,0:T(8,128)(2,1)S(1)} %copy-done), channel_id=1, source_target_pairs={{0,1},{1,0},{2,3},{3,2},{4,5},{5,4},{6,7},{7,6},{8,9},{9,8},{10,11... | collective-permute-start | bytes 1572872 | tf_op jit(solution)/shard_map/ppermute | solution.py:233
  7.5 2.4 %collective-permute-start.6 = (bf16[256,512]{1,0:T(8,128)(2,1)S(1)}, bf16[256,512]{1,0:T(8,128)(2,1)S(1)}, u32[]{:S(2)}, u32[]{:S(2)}) collective-permute-start(bf16[256,512]{1,0:T(8,128)(2,1)S(1)} %get-tuple-element.47), channel_id=1, source_target_pairs={{0,4},{1,5},{2,6},{3,7},{4,0},{5,1},{6,2},{7,3},{8,12},{9,13},{10,... | collective-permute-start | bytes 786440 | tf_op jit(solution)/shard_map/ppermute | solution.py:233
  10.0 17.1 %collective-permute-done.6.refs_2_ = bf16[256,512]{1,0:T(8,128)(2,1)S(1)} collective-permute-done((bf16[256,512]{1,0:T(8,128)(2,1)S(1)}, bf16[256,512]{1,0:T(8,128)(2,1)S(1)}, u32[]{:S(2)}, u32[]{:S(2)}) %collective-permute-start.6) | collective-permute-done | bytes 262176 | tf_op jit(solution)/shard_map/ppermute | solution.py:233
  27.3 0.8 collective-permute-start.12
  28.1 4.6 %collective-permute-done.4.refs_1_ = bf16[256,512]{1,0:T(8,128)(2,1)S(1)} collective-permute-done((bf16[256,512]{1,0:T(8,128)(2,1)S(1)}, bf16[256,512]{1,0:T(8,128)(2,1)S(1)}, u32[]{:S(2)}, u32[]{:S(2)}) %collective-permute-start.4) | collective-permute-done | bytes 262176 | tf_op jit(solution)/shard_map/ppermute | solution.py:233
  33.0 3.2 %collective-permute-start.1 = (bf16[72,256]{1,0:T(8,128)(2,1)S(1)}, bf16[72,256]{1,0:T(8,128)(2,1)S(1)}, u32[]{:S(2)}, u32[]{:S(2)}) collective-permute-start(bf16[72,256]{1,0:T(8,128)(2,1)S(1)} %get-tuple-element.44), channel_id=1, source_target_pairs={{0,4},{1,5},{2,6},{3,7},{4,0},{5,1},{6,2},{7,3},{8,12},{9,13},{10,... | collective-permute-start | bytes 110600 | tf_op jit(solution)/shard_map/ppermute | solution.py:233
  36.1 1.0 collective-permute-start.3
  37.5 1.2 %collective-permute-start.2 = (bf16[72,256]{1,0:T(8,128)(2,1)S(1)}, bf16[72,256]{1,0:T(8,128)(2,1)S(1)}, u32[]{:S(2)}, u32[]{:S(2)}) collective-permute-start(bf16[72,256]{1,0:T(8,128)(2,1)S(1)} %get-tuple-element.46), channel_id=1, source_target_pairs={{0,1},{1,0},{2,3},{3,2},{4,5},{5,4},{6,7},{7,6},{8,9},{9,8},{10,11... | collective-permute-start | bytes 110600 | tf_op jit(solution)/shard_map/ppermute | solution.py:233
  38.7 2.1 %collective-permute-done.3 = bf16[72,256]{1,0:T(8,128)(2,1)S(1)} collective-permute-done((bf16[72,256]{1,0:T(8,128)(2,1)S(1)}, bf16[72,256]{1,0:T(8,128)(2,1)S(1)}, u32[]{:S(2)}, u32[]{:S(2)}) %collective-permute-start.3) | collective-permute-done | bytes 36896 | tf_op jit(solution)/shard_map/ppermute | solution.py:233
  40.8 2.1 %collective-permute-start.11 = (bf16[256,512]{1,0:T(8,128)(2,1)S(1)}, bf16[256,512]{1,0:T(8,128)(2,1)S(1)}, u32[]{:S(2)}, u32[]{:S(2)}) collective-permute-start(bf16[256,512]{1,0:T(8,128)(2,1)S(1)} %collective-permute-done.6.refs_2_), channel_id=1, source_target_pairs={{0,8},{1,9},{2,10},{3,11},{4,12},{5,13},{6,14},{7,15},{8,0},{9,1},... | collective-permute-start | bytes 786440 | tf_op jit(solution)/shard_map/ppermute | solution.py:233
  43.0 0.5 collective-permute-start.10
  43.6 0.5 collective-permute-done.11.refs_8_
  45.2 0.5 first_corr.4.ca_ref
  45.8 5.0 %collective-permute-done.15.cb_ref = bf16[72,1024]{1,0:T(8,128)(2,1)S(1)} collective-permute-done((bf16[72,1024]{1,0:T(8,128)(2,1)S(1)}, bf16[72,1024]{1,0:T(8,128)(2,1)S(1)}, u32[]{:S(2)}, u32[]{:S(2)}) %collective-permute-start.15) | collective-permute-done | bytes 147488 | tf_op jit(solution)/shard_map/ppermute | solution.py:233
  50.8 1.2 %sweep_stage.4 = (bf16[72,1024]{1,0:T(8,128)(2,1)S(1)}, f32[72,1024]{1,0:T(8,128)S(1)}) custom-call(f32[72,1024]{1,0:T(8,128)S(1)} %pad_maximum_fusion.2.r_ref, bf16[72,1024]{1,0:T(8,128)(2,1)S(1)} %first_corr.4.ca_ref, bf16[72,1024]{1,0:T(8,128)(2,1)S(1)} %collective-permute-done.15.cb_ref, bf16[1024,1024]{1,0:T(8,128)(2,1)S(1)} %convert_element_type.55.own_ref, ...), custom_call_target="tpu_custom_call" | custom-call | flops 452984832 | bytes 4194304 | tf_op jit(solution)/shard_map/sweep_stage/pallas_call | solution.py:197
  52.1 0.5 first_corr.5.ca_ref
  52.6 4.0 %collective-permute-done.16.cb_ref = bf16[72,1024]{1,0:T(8,128)(2,1)S(1)} collective-permute-done((bf16[72,1024]{1,0:T(8,128)(2,1)S(1)}, bf16[72,1024]{1,0:T(8,128)(2,1)S(1)}, u32[]{:S(2)}, u32[]{:S(2)}) %collective-permute-start.16) | collective-permute-done | bytes 147488 | tf_op jit(solution)/shard_map/ppermute | solution.py:233
  56.6 1.2 %sweep_stage.5 = (bf16[72,1024]{1,0:T(8,128)(2,1)S(1)}, bf16[72,1024]{1,0:T(8,128)(2,1)S(1)}) custom-call(f32[72,1024]{1,0:T(8,128)S(1)} %get-tuple-element.33.r_ref, bf16[72,1024]{1,0:T(8,128)(2,1)S(1)} %first_corr.5.ca_ref, bf16[72,1024]{1,0:T(8,128)(2,1)S(1)} %collective-permute-done.16.cb_ref, bf16[1024,1024]{1,0:T(8,128)(2,1)S(1)} %convert_element_type.55.own_ref, ...), custom_call_target="tpu_custom_call" | custom-call | flops 452984832 | bytes 4194304 | tf_op jit(solution)/shard_map/sweep_stage/pallas_call | solution.py:197
  57.9 1.3 %collective-permute-start.17 = (bf16[72,1024]{1,0:T(8,128)(2,1)S(1)}, bf16[72,1024]{1,0:T(8,128)(2,1)S(1)}, u32[]{:S(2)}, u32[]{:S(2)}) collective-permute-start(bf16[72,1024]{1,0:T(8,128)(2,1)S(1)} %get-tuple-element.34), channel_id=1, source_target_pairs={{0,16},{1,17},{2,18},{3,19},{4,20},{5,21},{6,22},{7,23},{8,24},{9,... | collective-permute-start | bytes 442376 | tf_op jit(solution)/shard_map/ppermute | solution.py:233
  59.2 4.6 %collective-permute-done.17.r_ref = bf16[72,1024]{1,0:T(8,128)(2,1)S(1)} collective-permute-done((bf16[72,1024]{1,0:T(8,128)(2,1)S(1)}, bf16[72,1024]{1,0:T(8,128)(2,1)S(1)}, u32[]{:S(2)}, u32[]{:S(2)}) %collective-permute-start.17) | collective-permute-done | bytes 147488 | tf_op jit(solution)/shard_map/ppermute | solution.py:233
  63.8 0.5 first_corr.6.ca_ref
  64.3 4.0 %collective-permute-done.22.cb_ref = bf16[72,1024]{1,0:T(8,128)(2,1)S(1)} collective-permute-done((bf16[72,1024]{1,0:T(8,128)(2,1)S(1)}, bf16[72,1024]{1,0:T(8,128)(2,1)S(1)}, u32[]{:S(2)}, u32[]{:S(2)}) %collective-permute-start.22) | collective-permute-done | bytes 147488 | tf_op jit(solution)/shard_map/ppermute | solution.py:233
  68.3 1.2 %sweep_stage.6 = (bf16[72,1024]{1,0:T(8,128)(2,1)S(1)}, f32[72,1024]{1,0:T(8,128)S(1)}) custom-call(bf16[72,1024]{1,0:T(8,128)(2,1)S(1)} %collective-permute-done.17.r_ref, bf16[72,1024]{1,0:T(8,128)(2,1)S(1)} %first_corr.6.ca_ref, bf16[72,1024]{1,0:T(8,128)(2,1)S(1)} %collective-permute-done.22.cb_ref, bf16[1024,1024]{1,0:T(8,128)(2,1)S(1)} %convert_element_type.55.own_ref, ...), custom_call_target="tpu_custom_call" | custom-call | flops 452984832 | bytes 4194304 | tf_op jit(solution)/shard_map/sweep_stage/pallas_call | solution.py:197
  69.6 0.5 first_corr.7.ca_ref
  70.2 3.2 %collective-permute-start.23 = (bf16[72,1024]{1,0:T(8,128)(2,1)S(1)}, bf16[72,1024]{1,0:T(8,128)(2,1)S(1)}, u32[]{:S(2)}, u32[]{:S(2)}) collective-permute-start(bf16[72,1024]{1,0:T(8,128)(2,1)S(1)} %broadcast_select_fusion.1.refs_0_), channel_id=1, source_target_pairs={{0,4},{1,5},{2,6},{3,7},{4,0},{5,1},{6,2},{7,3},{8,12},{9,13},{10,... | collective-permute-start | bytes 442376 | tf_op jit(solution)/shard_map/ppermute | solution.py:233
  73.4 1.2 %collective-permute-start.24 = (bf16[72,1024]{1,0:T(8,128)(2,1)S(1)}, bf16[72,1024]{1,0:T(8,128)(2,1)S(1)}, u32[]{:S(2)}, u32[]{:S(2)}) collective-permute-start(bf16[72,1024]{1,0:T(8,128)(2,1)S(1)} %broadcast_select_fusion.1.refs_0_), channel_id=1, source_target_pairs={{0,1},{1,0},{2,3},{3,2},{4,5},{5,4},{6,7},{7,6},{8,9},{9,8},{10,11... | collective-permute-start | bytes 442376 | tf_op jit(solution)/shard_map/ppermute | solution.py:233
  74.6 1.9 %sweep_stage.7 = (bf16[72,1024]{1,0:T(8,128)(2,1)S(1)}, bf16[72,1024]{1,0:T(8,128)(2,1)}) custom-call(f32[72,1024]{1,0:T(8,128)S(1)} %get-tuple-element.38.r_ref, bf16[72,1024]{1,0:T(8,128)(2,1)S(1)} %first_corr.7.ca_ref, bf16[72,1024]{1,0:T(8,128)(2,1)S(1)} %collective-permute-done.27.cb_ref, bf16[1024,1024]{1,0:T(8,128)(2,1)S(1)} %convert_element_type.55.own_ref, ...), custom_call_target="tpu_custom_call" | custom-call | flops 452984832 | bytes 4194304 | tf_op jit(solution)/shard_map/sweep_stage/pallas_call | solution.py:197
  76.5 0.9 collective-permute-done.23.refs_1_
  77.4 1.2 %collective-permute-start.25 = (bf16[72,1024]{1,0:T(8,128)(2,1)S(1)}, bf16[72,1024]{1,0:T(8,128)(2,1)S(1)}, u32[]{:S(2)}, u32[]{:S(2)}) collective-permute-start(bf16[72,1024]{1,0:T(8,128)(2,1)S(1)} %collective-permute-done.23.refs_1_), channel_id=1, source_target_pairs={{0,1},{1,0},{2,3},{3,2},{4,5},{5,4},{6,7},{7,6},{8,9},{9,8},{10,11... | collective-permute-start | bytes 442376 | tf_op jit(solution)/shard_map/ppermute | solution.py:233
  78.9 2.5 %collective-permute-start.28 = (bf16[72,1024]{1,0:T(8,128)(2,1)S(1)}, bf16[72,1024]{1,0:T(8,128)(2,1)S(1)}, u32[]{:S(2)}, u32[]{:S(2)}) collective-permute-start(bf16[72,1024]{1,0:T(8,128)(2,1)S(1)} %broadcast_select_fusion.refs_4_), channel_id=1, source_target_pairs={{0,4},{1,5},{2,6},{3,7},{4,0},{5,1},{6,2},{7,3},{8,12},{9,13},{10,... | collective-permute-start | bytes 442376 | tf_op jit(solution)/shard_map/ppermute | solution.py:233
  81.4 0.7 collective-permute-done.25.refs_3_
  82.2 7.9 %collective-permute-start.26 = (bf16[288,1024]{1,0:T(8,128)(2,1)S(1)}, bf16[288,1024]{1,0:T(8,128)(2,1)S(1)}, u32[]{:S(2)}, u32[]{:S(2)}) collective-permute-start(bf16[288,1024]{1,0:T(8,128)(2,1)S(1)} %pad_maximum_fusion), channel_id=1, source_target_pairs={{0,8},{1,9},{2,10},{3,11},{4,12},{5,13},{6,14},{7,15},{8,0},{9,1},... | collective-permute-start | bytes 1769480 | tf_op jit(solution)/shard_map/ppermute | solution.py:233
  90.0 3.8 %collective-permute-start.20 = (bf16[72,256]{1,0:T(8,128)(2,1)S(1)}, bf16[72,256]{1,0:T(8,128)(2,1)S(1)}, u32[]{:S(2)}, u32[]{:S(2)}) collective-permute-start(bf16[72,256]{1,0:T(8,128)(2,1)S(1)} %get-tuple-element.50), channel_id=1, source_target_pairs={{0,5},{1,4},{2,7},{3,6},{4,1},{5,0},{6,3},{7,2},{8,13},{9,12},{10,... | collective-permute-start | bytes 110600 | tf_op jit(solution)/shard_map/ppermute | solution.py:233
  94.2 0.6 collective-permute-start.31
  94.9 0.8 collective-permute-done.20.refs_3_
  95.6 1.0 collective-permute-done.19.refs_2_
  96.6 1.1 %collective-permute-done.18.refs_1_ = bf16[72,256]{1,0:T(8,128)(2,1)S(1)} collective-permute-done((bf16[72,256]{1,0:T(8,128)(2,1)S(1)}, bf16[72,256]{1,0:T(8,128)(2,1)S(1)}, u32[]{:S(2)}, u32[]{:S(2)}) %collective-permute-start.18) | collective-permute-done | bytes 36896 | tf_op jit(solution)/shard_map/ppermute | solution.py:233
  97.8 1.8 %collective-permute-start.21 = (bf16[288,256]{1,0:T(8,128)(2,1)S(1)}, bf16[288,256]{1,0:T(8,128)(2,1)S(1)}, u32[]{:S(2)}, u32[]{:S(2)}) collective-permute-start(bf16[288,256]{1,0:T(8,128)(2,1)S(1)} %pad_maximum_fusion.3), channel_id=1, source_target_pairs={{0,8},{1,9},{2,10},{3,11},{4,12},{5,13},{6,14},{7,15},{8,0},{9,1},... | collective-permute-start | bytes 442376 | tf_op jit(solution)/shard_map/ppermute | solution.py:233
  99.6 1.2 %collective-permute-start.30 = (bf16[72,1024]{1,0:T(8,128)(2,1)S(1)}, bf16[72,1024]{1,0:T(8,128)(2,1)S(1)}, u32[]{:S(2)}, u32[]{:S(2)}) collective-permute-start(bf16[72,1024]{1,0:T(8,128)(2,1)S(1)} %collective-permute-done.28.refs_5_), channel_id=1, source_target_pairs={{0,1},{1,0},{2,3},{3,2},{4,5},{5,4},{6,7},{7,6},{8,9},{9,8},{10,11... | collective-permute-start | bytes 442376 | tf_op jit(solution)/shard_map/ppermute | solution.py:233
  100.8 0.6 shard_map.50.base_ref
  101.4 1.4 %shard_map.51.after_ref = f32[576,256]{1,0:T(8,128)S(1)} custom-call(s32[4]{0:T(128)S(1)} %pad_add_fusion.info_ref, bf16[256,1024]{1,0:T(8,128)(2,1)S(1)} %copy-done, bf16[256,1024]{1,0:T(8,128)(2,1)S(1)} %collective-permute-done.refs_6_.other_ref, f32[576,256]{1,0:T(8,128)S(1)} %shard_map.50.base_ref, ...), custom_call_target="tpu_custom_call" | custom-call | tf_op jit(solution)/shard_map/pallas_call | solution.py:169
  102.9 2.0 %collective-permute-done.30.refs_7_ = bf16[72,1024]{1,0:T(8,128)(2,1)S(1)} collective-permute-done((bf16[72,1024]{1,0:T(8,128)(2,1)S(1)}, bf16[72,1024]{1,0:T(8,128)(2,1)S(1)}, u32[]{:S(2)}, u32[]{:S(2)}) %collective-permute-start.30) | collective-permute-done | bytes 147488 | tf_op jit(solution)/shard_map/ppermute | solution.py:233
  104.9 0.9 collective-permute-start.32
  105.8 1.0 collective-permute-done.32.refs_9_
  106.8 3.1 %shard_map.52 = (f32[576,1024]{1,0:T(8,128)}, f32[576,256]{1,0:T(8,128)}) custom-call(s32[4]{0:T(128)S(1)} %pad_add_fusion.info_ref, bf16[256,1024]{1,0:T(8,128)(2,1)S(1)} %copy-done, f32[576,256]{1,0:T(8,128)S(1)} %shard_map.51.after_ref, bf16[288,1024]{1,0:T(8,128)(2,1)S(1)} %collective-permute-done.26.got_ref, ...), custom_call_target="tpu_custom_call" | custom-call | tf_op jit(solution)/shard_map/pallas_call | solution.py:169
  (48 shorter events, 3.8 us)
Async XLA Ops:
  0.9 5.4 %copy-start = (bf16[256,1024]{1,0:T(8,128)(2,1)S(1)}, bf16[256,1024]{1,0:T(8,128)(2,1)}, u32[]{:S(2)}) copy-start(bf16[256,1024]{1,0:T(8,128)(2,1)} %a_ref) | copy-start | bytes 1572868
  0.9 32.1 %copy-start.1 = (f32[256,576]{0,1:T(8,128)S(1)}, f32[256,576]{0,1:T(8,128)}, u32[]{:S(2)}) copy-start(f32[256,576]{0,1:T(8,128)} %param.4) | copy-start | bytes 1769476
  0.9 2.4 %collective-permute-start = (bf16[256,1024]{1,0:T(8,128)(2,1)}, bf16[256,1024]{1,0:T(8,128)(2,1)S(1)}, u32[]{:S(2)}, u32[]{:S(2)}) collective-permute-start(bf16[256,1024]{1,0:T(8,128)(2,1)} %a_ref), channel_id=1, source_target_pairs={{0,8},{1,9},{2,10},{3,11},{4,12},{5,13},{6,14},{7,15},{8,0},{9,1},... | collective-permute-start | bytes 1572872 | tf_op jit(solution)/shard_map/ppermute | solution.py:233
  5.8 26.9 %collective-permute-start.5 = (bf16[1024,1024]{1,0:T(8,128)(2,1)S(1)}, bf16[1024,1024]{1,0:T(8,128)(2,1)S(1)}, u32[]{:S(2)}, u32[]{:S(2)}) collective-permute-start(bf16[1024,1024]{1,0:T(8,128)(2,1)S(1)} %convert_element_type.55.own_ref), channel_id=1, source_target_pairs={{0,8},{1,9},{2,10},{3,11},{4,12},{5,13},{6,14},{7,15},{8,0},{9,1},... | collective-permute-start | bytes 6291464 | tf_op jit(solution)/shard_map/ppermute | solution.py:233
  6.3 21.1 %collective-permute-start.7 = (bf16[256,1024]{1,0:T(8,128)(2,1)S(1)}, bf16[256,1024]{1,0:T(8,128)(2,1)S(1)}, u32[]{:S(2)}, u32[]{:S(2)}) collective-permute-start(bf16[256,1024]{1,0:T(8,128)(2,1)S(1)} %copy-done), channel_id=1, source_target_pairs={{0,1},{1,0},{2,3},{3,2},{4,5},{5,4},{6,7},{7,6},{8,9},{9,8},{10,11... | collective-permute-start | bytes 1572872 | tf_op jit(solution)/shard_map/ppermute | solution.py:233
  7.5 19.5 %collective-permute-start.6 = (bf16[256,512]{1,0:T(8,128)(2,1)S(1)}, bf16[256,512]{1,0:T(8,128)(2,1)S(1)}, u32[]{:S(2)}, u32[]{:S(2)}) collective-permute-start(bf16[256,512]{1,0:T(8,128)(2,1)S(1)} %get-tuple-element.47), channel_id=1, source_target_pairs={{0,4},{1,5},{2,6},{3,7},{4,0},{5,1},{6,2},{7,3},{8,12},{9,13},{10,... | collective-permute-start | bytes 786440 | tf_op jit(solution)/shard_map/ppermute | solution.py:233
  9.9 22.8 %collective-permute-start.4 = (bf16[256,512]{1,0:T(8,128)(2,1)S(1)}, bf16[256,512]{1,0:T(8,128)(2,1)S(1)}, u32[]{:S(2)}, u32[]{:S(2)}) collective-permute-start(bf16[256,512]{1,0:T(8,128)(2,1)S(1)} %get-tuple-element.48), channel_id=1, source_target_pairs={{0,4},{1,5},{2,6},{3,7},{4,0},{5,1},{6,2},{7,3},{8,12},{9,13},{10,... | collective-permute-start | bytes 786440 | tf_op jit(solution)/shard_map/ppermute | solution.py:233
  27.1 15.9 %collective-permute-start.9 = (bf16[256,512]{1,0:T(8,128)(2,1)S(1)}, bf16[256,512]{1,0:T(8,128)(2,1)S(1)}, u32[]{:S(2)}, u32[]{:S(2)}) collective-permute-start(bf16[256,512]{1,0:T(8,128)(2,1)S(1)} %collective-permute-done.6.refs_2_), channel_id=1, source_target_pairs={{0,1},{1,0},{2,3},{3,2},{4,5},{5,4},{6,7},{7,6},{8,9},{9,8},{10,11... | collective-permute-start | bytes 786440 | tf_op jit(solution)/shard_map/ppermute | solution.py:233
  27.3 17.2 %collective-permute-start.12 = (bf16[256,1024]{1,0:T(8,128)(2,1)S(1)}, bf16[256,1024]{1,0:T(8,128)(2,1)S(1)}, u32[]{:S(2)}, u32[]{:S(2)}) collective-permute-start(bf16[256,1024]{1,0:T(8,128)(2,1)S(1)} %collective-permute-done.7.refs_3_), channel_id=1, source_target_pairs={{0,8},{1,9},{2,10},{3,11},{4,12},{5,13},{6,14},{7,15},{8,0},{9,1},... | collective-permute-start | bytes 1572872 | tf_op jit(solution)/shard_map/ppermute | solution.py:233
  32.7 10.8 %collective-permute-start.8 = (bf16[256,512]{1,0:T(8,128)(2,1)S(1)}, bf16[256,512]{1,0:T(8,128)(2,1)S(1)}, u32[]{:S(2)}, u32[]{:S(2)}) collective-permute-start(bf16[256,512]{1,0:T(8,128)(2,1)S(1)} %collective-permute-done.4.refs_1_), channel_id=1, source_target_pairs={{0,1},{1,0},{2,3},{3,2},{4,5},{5,4},{6,7},{7,6},{8,9},{9,8},{10,11... | collective-permute-start | bytes 786440 | tf_op jit(solution)/shard_map/ppermute | solution.py:233
  33.0 4.5 %collective-permute-start.1 = (bf16[72,256]{1,0:T(8,128)(2,1)S(1)}, bf16[72,256]{1,0:T(8,128)(2,1)S(1)}, u32[]{:S(2)}, u32[]{:S(2)}) collective-permute-start(bf16[72,256]{1,0:T(8,128)(2,1)S(1)} %get-tuple-element.44), channel_id=1, source_target_pairs={{0,4},{1,5},{2,6},{3,7},{4,0},{5,1},{6,2},{7,3},{8,12},{9,13},{10,... | collective-permute-start | bytes 110600 | tf_op jit(solution)/shard_map/ppermute | solution.py:233
  36.1 4.7 %collective-permute-start.3 = (bf16[72,256]{1,0:T(8,128)(2,1)S(1)}, bf16[72,256]{1,0:T(8,128)(2,1)S(1)}, u32[]{:S(2)}, u32[]{:S(2)}) collective-permute-start(bf16[72,256]{1,0:T(8,128)(2,1)S(1)} %get-tuple-element.45), channel_id=1, source_target_pairs={{0,5},{1,4},{2,7},{3,6},{4,1},{5,0},{6,3},{7,2},{8,13},{9,12},{10,... | collective-permute-start | bytes 110600 | tf_op jit(solution)/shard_map/ppermute | solution.py:233
  37.5 5.5 %collective-permute-start.2 = (bf16[72,256]{1,0:T(8,128)(2,1)S(1)}, bf16[72,256]{1,0:T(8,128)(2,1)S(1)}, u32[]{:S(2)}, u32[]{:S(2)}) collective-permute-start(bf16[72,256]{1,0:T(8,128)(2,1)S(1)} %get-tuple-element.46), channel_id=1, source_target_pairs={{0,1},{1,0},{2,3},{3,2},{4,5},{5,4},{6,7},{7,6},{8,9},{9,8},{10,11... | collective-permute-start | bytes 110600 | tf_op jit(solution)/shard_map/ppermute | solution.py:233
  40.8 3.3 %collective-permute-start.11 = (bf16[256,512]{1,0:T(8,128)(2,1)S(1)}, bf16[256,512]{1,0:T(8,128)(2,1)S(1)}, u32[]{:S(2)}, u32[]{:S(2)}) collective-permute-start(bf16[256,512]{1,0:T(8,128)(2,1)S(1)} %collective-permute-done.6.refs_2_), channel_id=1, source_target_pairs={{0,8},{1,9},{2,10},{3,11},{4,12},{5,13},{6,14},{7,15},{8,0},{9,1},... | collective-permute-start | bytes 786440 | tf_op jit(solution)/shard_map/ppermute | solution.py:233
  43.0 1.5 %collective-permute-start.14 = (bf16[256,512]{1,0:T(8,128)(2,1)S(1)}, bf16[256,512]{1,0:T(8,128)(2,1)S(1)}, u32[]{:S(2)}, u32[]{:S(2)}) collective-permute-start(bf16[256,512]{1,0:T(8,128)(2,1)S(1)} %collective-permute-done.9.refs_5_), channel_id=1, source_target_pairs={{0,8},{1,9},{2,10},{3,11},{4,12},{5,13},{6,14},{7,15},{8,0},{9,1},... | collective-permute-start | bytes 786440 | tf_op jit(solution)/shard_map/ppermute | solution.py:233
  43.0 1.9 %collective-permute-start.10 = (bf16[256,512]{1,0:T(8,128)(2,1)S(1)}, bf16[256,512]{1,0:T(8,128)(2,1)S(1)}, u32[]{:S(2)}, u32[]{:S(2)}) collective-permute-start(bf16[256,512]{1,0:T(8,128)(2,1)S(1)} %collective-permute-done.4.refs_1_), channel_id=1, source_target_pairs={{0,8},{1,9},{2,10},{3,11},{4,12},{5,13},{6,14},{7,15},{8,0},{9,1},... | collective-permute-start | bytes 786440 | tf_op jit(solution)/shard_map/ppermute | solution.py:233
  43.5 1.8 %collective-permute-start.13 = (bf16[256,512]{1,0:T(8,128)(2,1)S(1)}, bf16[256,512]{1,0:T(8,128)(2,1)S(1)}, u32[]{:S(2)}, u32[]{:S(2)}) collective-permute-start(bf16[256,512]{1,0:T(8,128)(2,1)S(1)} %collective-permute-done.8.refs_4_), channel_id=1, source_target_pairs={{0,8},{1,9},{2,10},{3,11},{4,12},{5,13},{6,14},{7,15},{8,0},{9,1},... | collective-permute-start | bytes 786440 | tf_op jit(solution)/shard_map/ppermute | solution.py:233
  45.7 5.1 %collective-permute-start.15 = (bf16[72,1024]{1,0:T(8,128)(2,1)S(1)}, bf16[72,1024]{1,0:T(8,128)(2,1)S(1)}, u32[]{:S(2)}, u32[]{:S(2)}) collective-permute-start(bf16[72,1024]{1,0:T(8,128)(2,1)S(1)} %first_corr.4.ca_ref), channel_id=1, source_target_pairs={{0,2},{1,3},{2,0},{3,1},{4,6},{5,7},{6,4},{7,5},{8,10},{9,11},{10,... | collective-permute-start | bytes 442376 | tf_op jit(solution)/shard_map/ppermute | solution.py:233
  52.6 4.1 %collective-permute-start.16 = (bf16[72,1024]{1,0:T(8,128)(2,1)S(1)}, bf16[72,1024]{1,0:T(8,128)(2,1)S(1)}, u32[]{:S(2)}, u32[]{:S(2)}) collective-permute-start(bf16[72,1024]{1,0:T(8,128)(2,1)S(1)} %first_corr.5.ca_ref), channel_id=1, source_target_pairs={{0,2},{1,3},{2,0},{3,1},{4,6},{5,7},{6,4},{7,5},{8,10},{9,11},{10,... | collective-permute-start | bytes 442376 | tf_op jit(solution)/shard_map/ppermute | solution.py:233
  57.9 5.9 %collective-permute-start.17 = (bf16[72,1024]{1,0:T(8,128)(2,1)S(1)}, bf16[72,1024]{1,0:T(8,128)(2,1)S(1)}, u32[]{:S(2)}, u32[]{:S(2)}) collective-permute-start(bf16[72,1024]{1,0:T(8,128)(2,1)S(1)} %get-tuple-element.34), channel_id=1, source_target_pairs={{0,16},{1,17},{2,18},{3,19},{4,20},{5,21},{6,22},{7,23},{8,24},{9,... | collective-permute-start | bytes 442376 | tf_op jit(solution)/shard_map/ppermute | solution.py:233
  64.2 4.1 %collective-permute-start.22 = (bf16[72,1024]{1,0:T(8,128)(2,1)S(1)}, bf16[72,1024]{1,0:T(8,128)(2,1)S(1)}, u32[]{:S(2)}, u32[]{:S(2)}) collective-permute-start(bf16[72,1024]{1,0:T(8,128)(2,1)S(1)} %first_corr.6.ca_ref), channel_id=1, source_target_pairs={{0,2},{1,3},{2,0},{3,1},{4,6},{5,7},{6,4},{7,5},{8,10},{9,11},{10,... | collective-permute-start | bytes 442376 | tf_op jit(solution)/shard_map/ppermute | solution.py:233
  70.1 4.5 %collective-permute-start.27 = (bf16[72,1024]{1,0:T(8,128)(2,1)S(1)}, bf16[72,1024]{1,0:T(8,128)(2,1)S(1)}, u32[]{:S(2)}, u32[]{:S(2)}) collective-permute-start(bf16[72,1024]{1,0:T(8,128)(2,1)S(1)} %first_corr.7.ca_ref), channel_id=1, source_target_pairs={{0,2},{1,3},{2,0},{3,1},{4,6},{5,7},{6,4},{7,5},{8,10},{9,11},{10,... | collective-permute-start | bytes 442376 | tf_op jit(solution)/shard_map/ppermute | solution.py:233
  70.2 7.2 %collective-permute-start.23 = (bf16[72,1024]{1,0:T(8,128)(2,1)S(1)}, bf16[72,1024]{1,0:T(8,128)(2,1)S(1)}, u32[]{:S(2)}, u32[]{:S(2)}) collective-permute-start(bf16[72,1024]{1,0:T(8,128)(2,1)S(1)} %broadcast_select_fusion.1.refs_0_), channel_id=1, source_target_pairs={{0,4},{1,5},{2,6},{3,7},{4,0},{5,1},{6,2},{7,3},{8,12},{9,13},{10,... | collective-permute-start | bytes 442376 | tf_op jit(solution)/shard_map/ppermute | solution.py:233
  73.4 8.0 %collective-permute-start.24 = (bf16[72,1024]{1,0:T(8,128)(2,1)S(1)}, bf16[72,1024]{1,0:T(8,128)(2,1)S(1)}, u32[]{:S(2)}, u32[]{:S(2)}) collective-permute-start(bf16[72,1024]{1,0:T(8,128)(2,1)S(1)} %broadcast_select_fusion.1.refs_0_), channel_id=1, source_target_pairs={{0,1},{1,0},{2,3},{3,2},{4,5},{5,4},{6,7},{7,6},{8,9},{9,8},{10,11... | collective-permute-start | bytes 442376 | tf_op jit(solution)/shard_map/ppermute | solution.py:233
  77.4 4.7 %collective-permute-start.25 = (bf16[72,1024]{1,0:T(8,128)(2,1)S(1)}, bf16[72,1024]{1,0:T(8,128)(2,1)S(1)}, u32[]{:S(2)}, u32[]{:S(2)}) collective-permute-start(bf16[72,1024]{1,0:T(8,128)(2,1)S(1)} %collective-permute-done.23.refs_1_), channel_id=1, source_target_pairs={{0,1},{1,0},{2,3},{3,2},{4,5},{5,4},{6,7},{7,6},{8,9},{9,8},{10,11... | collective-permute-start | bytes 442376 | tf_op jit(solution)/shard_map/ppermute | solution.py:233
  78.6 15.4 %collective-permute-start.29 = (bf16[72,1024]{1,0:T(8,128)(2,1)S(1)}, bf16[72,1024]{1,0:T(8,128)(2,1)S(1)}, u32[]{:S(2)}, u32[]{:S(2)}) collective-permute-start(bf16[72,1024]{1,0:T(8,128)(2,1)S(1)} %broadcast_select_fusion.refs_4_), channel_id=1, source_target_pairs={{0,1},{1,0},{2,3},{3,2},{4,5},{5,4},{6,7},{7,6},{8,9},{9,8},{10,11... | collective-permute-start | bytes 442376 | tf_op jit(solution)/shard_map/ppermute | solution.py:233
  78.9 15.2 %collective-permute-start.28 = (bf16[72,1024]{1,0:T(8,128)(2,1)S(1)}, bf16[72,1024]{1,0:T(8,128)(2,1)S(1)}, u32[]{:S(2)}, u32[]{:S(2)}) collective-permute-start(bf16[72,1024]{1,0:T(8,128)(2,1)S(1)} %broadcast_select_fusion.refs_4_), channel_id=1, source_target_pairs={{0,4},{1,5},{2,6},{3,7},{4,0},{5,1},{6,2},{7,3},{8,12},{9,13},{10,... | collective-permute-start | bytes 442376 | tf_op jit(solution)/shard_map/ppermute | solution.py:233
  82.2 19.2 %collective-permute-start.26 = (bf16[288,1024]{1,0:T(8,128)(2,1)S(1)}, bf16[288,1024]{1,0:T(8,128)(2,1)S(1)}, u32[]{:S(2)}, u32[]{:S(2)}) collective-permute-start(bf16[288,1024]{1,0:T(8,128)(2,1)S(1)} %pad_maximum_fusion), channel_id=1, source_target_pairs={{0,8},{1,9},{2,10},{3,11},{4,12},{5,13},{6,14},{7,15},{8,0},{9,1},... | collective-permute-start | bytes 1769480 | tf_op jit(solution)/shard_map/ppermute | solution.py:233
  90.0 5.6 %collective-permute-start.20 = (bf16[72,256]{1,0:T(8,128)(2,1)S(1)}, bf16[72,256]{1,0:T(8,128)(2,1)S(1)}, u32[]{:S(2)}, u32[]{:S(2)}) collective-permute-start(bf16[72,256]{1,0:T(8,128)(2,1)S(1)} %get-tuple-element.50), channel_id=1, source_target_pairs={{0,5},{1,4},{2,7},{3,6},{4,1},{5,0},{6,3},{7,2},{8,13},{9,12},{10,... | collective-permute-start | bytes 110600 | tf_op jit(solution)/shard_map/ppermute | solution.py:233
  93.8 2.8 %collective-permute-start.19 = (bf16[72,256]{1,0:T(8,128)(2,1)S(1)}, bf16[72,256]{1,0:T(8,128)(2,1)S(1)}, u32[]{:S(2)}, u32[]{:S(2)}) collective-permute-start(bf16[72,256]{1,0:T(8,128)(2,1)S(1)} %get-tuple-element.51), channel_id=1, source_target_pairs={{0,1},{1,0},{2,3},{3,2},{4,5},{5,4},{6,7},{7,6},{8,9},{9,8},{10,11... | collective-permute-start | bytes 110600 | tf_op jit(solution)/shard_map/ppermute | solution.py:233
  94.0 3.7 %collective-permute-start.18 = (bf16[72,256]{1,0:T(8,128)(2,1)S(1)}, bf16[72,256]{1,0:T(8,128)(2,1)S(1)}, u32[]{:S(2)}, u32[]{:S(2)}) collective-permute-start(bf16[72,256]{1,0:T(8,128)(2,1)S(1)} %get-tuple-element.52), channel_id=1, source_target_pairs={{0,4},{1,5},{2,6},{3,7},{4,0},{5,1},{6,2},{7,3},{8,12},{9,13},{10,... | collective-permute-start | bytes 110600 | tf_op jit(solution)/shard_map/ppermute | solution.py:233
  94.2 11.6 %collective-permute-start.31 = (bf16[216,1024]{1,0:T(8,128)(2,1)S(1)}, bf16[216,1024]{1,0:T(8,128)(2,1)S(1)}, u32[]{:S(2)}, u32[]{:S(2)}) collective-permute-start(bf16[216,1024]{1,0:T(8,128)(2,1)S(1)} %pad_maximum_fusion.1), channel_id=1, source_target_pairs={{0,8},{1,9},{2,10},{3,11},{4,12},{5,13},{6,14},{7,15},{8,0},{9,1},... | collective-permute-start | bytes 1327112 | tf_op jit(solution)/shard_map/ppermute | solution.py:233
  97.8 3.0 %collective-permute-start.21 = (bf16[288,256]{1,0:T(8,128)(2,1)S(1)}, bf16[288,256]{1,0:T(8,128)(2,1)S(1)}, u32[]{:S(2)}, u32[]{:S(2)}) collective-permute-start(bf16[288,256]{1,0:T(8,128)(2,1)S(1)} %pad_maximum_fusion.3), channel_id=1, source_target_pairs={{0,8},{1,9},{2,10},{3,11},{4,12},{5,13},{6,14},{7,15},{8,0},{9,1},... | collective-permute-start | bytes 442376 | tf_op jit(solution)/shard_map/ppermute | solution.py:233
  99.6 5.3 %collective-permute-start.30 = (bf16[72,1024]{1,0:T(8,128)(2,1)S(1)}, bf16[72,1024]{1,0:T(8,128)(2,1)S(1)}, u32[]{:S(2)}, u32[]{:S(2)}) collective-permute-start(bf16[72,1024]{1,0:T(8,128)(2,1)S(1)} %collective-permute-done.28.refs_5_), channel_id=1, source_target_pairs={{0,1},{1,0},{2,3},{3,2},{4,5},{5,4},{6,7},{7,6},{8,9},{9,8},{10,11... | collective-permute-start | bytes 442376 | tf_op jit(solution)/shard_map/ppermute | solution.py:233
  104.9 1.9 %collective-permute-start.32 = (bf16[72,1024]{1,0:T(8,128)(2,1)S(1)}, bf16[72,1024]{1,0:T(8,128)(2,1)S(1)}, u32[]{:S(2)}, u32[]{:S(2)}) collective-permute-start(bf16[72,1024]{1,0:T(8,128)(2,1)S(1)} %collective-permute-done.30.refs_7_), channel_id=1, source_target_pairs={{0,8},{1,9},{2,10},{3,11},{4,12},{5,13},{6,14},{7,15},{8,0},{9,1},... | collective-permute-start | bytes 442376 | tf_op jit(solution)/shard_map/ppermute | solution.py:233
where the time goes:
time: 110 us
  waiting for transfers between devices  52.6 us (48%)
  starting transfers between devices  40.8 us (37%)
  Pallas kernels  12.7 us (12%)
  other arithmetic  2.75 us (2%)
    ppermute x33, waiting for transfers between devices, permute(): return lax.ppermute(x, ('grp', 'row'), route)  52.6 us
    ppermute x33, starting transfers between devices, permute(): return lax.ppermute(x, ('grp', 'row'), route)  40.8 us
    pallas_call x4, Pallas kernels, stage_call(): pl.pallas_call(functools.partial(stage_kernel, layout, owner), out_shape=...  5.62 us
    pallas_call x3, Pallas kernels, local_call(): pl.pallas_call(body, out_shape=out_shape, in_specs=[pl.BlockSpec(memory_s...  5.1 us
    convert_element_type x1, other arithmetic, sweep(): square = after(precond, swapped).astype(BF16)  2.51 us
  transfers between devices with their start and end apart: 33, of which 20 were waited for; matrix products, arithmetic and copies ran while one was open for 0% of the time, Pallas kernels for 4%

commit v1 on v0

--- a/solution.py
+++ b/solution.py
@@ -13,8 +13,8 @@
 CORES = 2
 PAIR = 2
 TILE = 8
+ANY = pl.BlockSpec(memory_space=pl.ANY)
 VMEM = pl.BlockSpec(memory_space=pltpu.VMEM)
-SCALARS = pl.BlockSpec(memory_space=pltpu.SMEM)
 GRANT = 24 * 1024 * 1024
 
 
@@ -61,7 +61,7 @@
 
 def stage_kernel(layout, owner, r_ref, ca_ref, cb_ref, own_ref, other_ref, *refs):
     count = sum(layout)
-    w_ref, rn_ref = refs[2 * count:]
+    w_ref, rn_ref = refs[2 * count], refs[2 * count + 1:]
     width = ca_ref.shape[0]
     total = ca_ref[...].astype(F32) + cb_ref[...].astype(F32)
     high = total.astype(BF16)
@@ -72,6 +72,8 @@
         both = jnp.dot(stacked, map_ref[...], preferred_element_type=F32)
         wb = (both[:width] + both[width:]).astype(BF16)
         w_ref[...] = wb
+        if not rn_ref:
+            return
         rows = blocks[0][0].shape[0]
         cut = wb.shape[1] // 2
         for q, block in enumerate(blocks):
@@ -80,7 +82,7 @@
                 change = product(wb, block[0])
             else:
                 change = product(wb[:, :cut], block[0]) + product(wb[:, cut:], block[1])
-            rn_ref[:, span] = (r_ref[:, span].astype(F32) - change).astype(rn_ref.dtype)
+            rn_ref[0][:, span] = (r_ref[:, span].astype(F32) - change).astype(rn_ref[0].dtype)
 
     @pl.when(core_is(owner))
     def _():
@@ -95,10 +97,16 @@
     return lax.dot_general(w, a_ref[...], (((1,), (1,)), ((), ())), preferred_element_type=F32)
 
 
-def spans(info_ref, count, height):
+def place_of(index):
+    return (index // (2 * PAIR)) * PAIR + index % PAIR
+
+
+def spans(masks, height):
     if height % TILE:
-        return [pl.ds(q * height, height) for q in range(count)]
-    return [pl.ds(pl.multiple_of(info_ref[q], TILE), height) for q in range(count)]
+        return [pl.ds(q * height, height) for q in range(len(masks))]
+    shard = lax.axis_index("row")
+    places = [place_of(lax.bitwise_xor(shard, jnp.int32(m))) for m in masks]
+    return [pl.ds(pl.multiple_of(place * height, TILE), height) for place in places]
 
 
 def rows_of(ref, q, height):
@@ -109,12 +117,12 @@
     return jnp.concatenate((own, got) if first_core else (got, own), axis=0)
 
 
-def update_kernel(count, info_ref, own_ref, other_ref, base_ref, got_ref, *refs):
-    parts, out_ref = refs[:count], refs[count]
+def update_kernel(masks, own_ref, other_ref, base_ref, got_ref, *refs):
+    parts, out_ref = refs[:-1], refs[-1]
     height = parts[0].shape[0]
 
     def run(first_core, a_ref):
-        for q, at in enumerate(spans(info_ref, count, 2 * height)):
+        for q, at in enumerate(spans(masks, 2 * height)):
             w = both_panels(first_core, parts[q][...], rows_of(got_ref, q, height))
             out_ref[at, :] = base_ref[at, :] - product(w, a_ref)
 
@@ -122,31 +130,63 @@
     pl.when(core_is(1))(functools.partial(run, False, other_ref))
 
 
-def final_kernel(count, early, info_ref, a_ref, after_ref, got_ref, *refs):
+def write_kernel(masks, chosen, resume, a_ref, after_ref, got_ref, got_late_ref, *refs):
+    count = len(masks)
     first, second = refs[:count], refs[count:2 * count]
-    got_early, got_late = refs[2 * count:2 * count + 2]
-    coef_ref, resid_ref = refs[2 * count + 2:]
+    refs = refs[2 * count + (2 if resume else 0):]
+    coef_ref, resid_ref, coefs, resids, sems = refs
     height = first[0].shape[0]
-    places = spans(info_ref, count, 2 * height)
-
-    @pl.when(core_is(0))
-    def _():
-        for q, at in enumerate(places):
+    places = spans(masks, 2 * height)
+
+    def copies(k):
+        at = places[chosen[k]]
+        return (
+            pltpu.make_async_copy(coefs.at[k], coef_ref.at[at, :], sems.at[0, k]),
+            pltpu.make_async_copy(resids.at[k], resid_ref.at[at, :], sems.at[1, k]),
+        )
+
+    for k, q in enumerate(chosen):
+        @pl.when(core_is(0))
+        def _():
             w = both_panels(True, first[q][...], rows_of(got_ref, q, height))
-            coef_ref[at, :] = w.astype(F32)
-        resid_ref[...] = after_ref[...]
-
-    @pl.when(core_is(1))
-    def _():
-        for q, at in enumerate(places):
-            source, k = (got_early, q) if q < early else (got_late, q - early)
-            w = both_panels(False, second[q][...], rows_of(source, k, height))
-            coef_ref[at, :] = w.astype(F32)
-            resid_ref[at, :] = after_ref[at, :] - product(w, a_ref)
-
-
-def base_kernel(count, info_ref, turned_ref, got_ref, *refs):
-    parts, out_ref = refs[:count], refs[count]
+            coefs[k] = w.astype(F32)
+            resids[k] = after_ref[places[q], :]
+
+        @pl.when(core_is(1))
+        def _():
+            w = both_panels(False, second[q][...], rows_of(got_late_ref, k, height))
+            coefs[k] = w.astype(F32)
+            resids[k] = after_ref[places[q], :] - product(w, a_ref)
+
+        for copy in copies(k):
+            copy.start()
+    for k in range(len(chosen)):
+        for copy in copies(k):
+            copy.wait()
+
+
+def write_call(masks, chosen, shapes, arrays, resume=()):
+    height = 2 * arrays[4].shape[0]
+    feats, rows = shapes[0].shape[1], shapes[1].shape[1]
+    size = len(chosen)
+    return pl.pallas_call(
+        functools.partial(write_kernel, masks, chosen, len(resume) > 0),
+        out_shape=shapes,
+        in_specs=[VMEM] * len(arrays) + [ANY] * len(resume),
+        out_specs=[ANY] * 2,
+        scratch_shapes=[
+            pltpu.VMEM((size, height, feats), F32),
+            pltpu.VMEM((size, height, rows), F32),
+            pltpu.SemaphoreType.DMA((2, size)),
+        ],
+        input_output_aliases={len(arrays) + k: k for k in range(len(resume))},
+        compiler_params=pltpu.CompilerParams(vmem_limit_bytes=GRANT),
+        name="write_rest" if resume else "write_early",
+    )(*arrays, *resume)
+
+
+def base_kernel(masks, turned_ref, got_ref, *refs):
+    parts, out_ref = refs[:-1], refs[-1]
     height = parts[0].shape[0]
     first_plane = lax.axis_index("grp") < CORES
 
@@ -155,7 +195,7 @@
         out_ref[...] = turned_ref[...]
 
     def run(first_core):
-        for q, at in enumerate(spans(info_ref, count, 2 * height)):
+        for q, at in enumerate(spans(masks, 2 * height)):
             r = both_panels(first_core, parts[q][...], rows_of(got_ref, q, height))
             out_ref[at, :] = r.astype(F32)
 
@@ -164,15 +204,15 @@
     pl.when(jnp.logical_and(later, core_is(1)))(functools.partial(run, False))
 
 
-def local_call(body, out_shape, info, arrays):
+def local_call(body, out_shape, arrays):
     many = isinstance(out_shape, (list, tuple))
     return pl.pallas_call(
         body,
         out_shape=out_shape,
-        in_specs=[pl.BlockSpec(memory_space=pltpu.SMEM)] + [VMEM] * len(arrays),
+        in_specs=[VMEM] * len(arrays),
         out_specs=[VMEM] * len(out_shape) if many else VMEM,
         compiler_params=pltpu.CompilerParams(vmem_limit_bytes=GRANT),
-    )(info, *arrays)
+    )(*arrays)
 
 
 def first_call(owner, layout, panel, own, other):
@@ -194,11 +234,16 @@
 def stage_call(owner, layout, panel, ca, cb, squares, own, other, kind):
     feats = own[0].shape[1]
     width, rows = panel.shape
+    out_shape = [jax.ShapeDtypeStruct((width, feats), BF16)]
+    if kind is None:
+        own, other, layout = [panel], [panel], [1]
+    else:
+        out_shape.append(jax.ShapeDtypeStruct(panel.shape, kind))
     return pl.pallas_call(
         functools.partial(stage_kernel, layout, owner),
-        out_shape=[jax.ShapeDtypeStruct((width, feats), BF16), jax.ShapeDtypeStruct(panel.shape, kind)],
+        out_shape=out_shape,
         in_specs=[VMEM] * (5 + 2 * len(own)),
-        out_specs=[VMEM] * 2,
+        out_specs=[VMEM] * len(out_shape),
         cost_estimate=pl.CostEstimate(
             flops=2 * width * feats * (2 * feats + rows),
             bytes_accessed=2 * feats * (feats + rows),
@@ -237,9 +282,6 @@
     for bit in reversed(bits):
         masks += [m ^ bit for m in masks]
 
-    def place_of(index):
-        return (index // (2 * PAIR)) * PAIR + index % PAIR
-
     def after(x, *others):
         return lax.optimization_barrier((x,) + others)[0]
 
@@ -251,14 +293,11 @@
         stacked = jnp.take(jnp.stack(parts), jnp.argsort(ranks), axis=0)
         return [stacked[q] for q in range(len(parts))]
 
-    info = jnp.stack(
-        [place_of(r ^ m) * CORES * width for m in masks]
-    ).astype(jnp.int32)
     starts = [((place_of(r ^ m) * CORES + core) * width).astype(jnp.uint32) for m in masks]
     on_first = core == 0
     at_plane = [plane == step for step in range(plane_count)]
-    features, info, starts, on_first, at_plane = lax.optimization_barrier(
-        (features, info, starts, on_first, at_plane)
+    features, starts, on_first, at_plane = lax.optimization_barrier(
+        (features, starts, on_first, at_plane)
     )
     far = bits[-1]
     near = bits[:-1]
@@ -309,10 +348,12 @@
         keep_first = w1 if keep_first is None else jnp.where(at_plane[step], w1, keep_first)
         corr = first_call(1, layout, panel1, mine, theirs)
         got = permute(corr, mask=PAIR)
-        w2, panel2 = stage_call(1, layout, panel1, corr, got, squares, mine, theirs, BF16)
+        w2, *panel2 = stage_call(
+            1, layout, panel1, corr, got, squares, mine, theirs, None if end else BF16
+        )
         keep_second = w2 if keep_second is None else jnp.where(at_plane[step], w2, keep_second)
         if not end:
-            panel = permute(panel2, shift=CORES)
+            panel = permute(panel2[0], shift=CORES)
             passed = panel if passed is None else jnp.where(at_plane[step + 1], panel, passed)
 
     def gather(pair):
@@ -332,23 +373,44 @@
     if blocks is not None:
         blocks = ordered(blocks)
         base_got = permute(jnp.concatenate(blocks, axis=0), flip=1)
-        base = local_call(
-            functools.partial(base_kernel, count), whole, info, [turned, base_got] + blocks
-        )
+        base = local_call(functools.partial(base_kernel, masks), whole, [turned, base_got] + blocks)
     after_first = local_call(
-        functools.partial(update_kernel, count),
+        functools.partial(update_kernel, masks),
         whole,
-        info,
         [features, swapped, base, first_got] + first_parts,
     )
-    late = second_parts[early:] or second_parts[:1]
-    got_late = permute(after(jnp.concatenate(late, axis=0), after_first), flip=1)
-    coef_t, resid_t = local_call(
-        functools.partial(final_kernel, count, early),
-        [jax.ShapeDtypeStruct((targets, feats), F32), whole],
-        info,
-        [features, after_first, first_got] + first_parts + second_parts + [got_early, got_late],
-    )
+    if CORES * width % TILE:
+        def assembled(parts, got):
+            got = [got[q * width:(q + 1) * width] for q in range(len(parts))]
+            pairs = [
+                jnp.where(on_first, jnp.concatenate((x, y), axis=0), jnp.concatenate((y, x), axis=0))
+                for x, y in zip(parts, got)
+            ]
+            return jnp.concatenate(pairs, axis=0)
+
+        got_all = [got_early]
+        if early < count:
+            late = jnp.concatenate(second_parts[early:], axis=0)
+            got_all.append(permute(late, flip=1))
+        second = assembled(second_parts, jnp.concatenate(got_all, axis=0))
+        coef_t = jnp.where(on_first, assembled(first_parts, first_got), second).astype(F32)
+        change = product(second, features)
+        return coef_t.T, jnp.where(on_first, after_first, after_first - change).T[None]
+    shapes = [jax.ShapeDtypeStruct((targets, feats), F32), whole]
+    parts = [features, after_first, first_got]
+    known = second_parts[:early] + second_parts[:1] * (count - early)
+    done = write_call(masks, tuple(range(early)), shapes, parts + [got_early] + first_parts + known)
+    if early < count:
+        late = jnp.concatenate(second_parts[early:], axis=0)
+        got_late = permute(late, flip=1)
+        done = write_call(
+            masks,
+            tuple(range(early, count)),
+            shapes,
+            parts + [got_late] + first_parts + second_parts,
+            done,
+        )
+    coef_t, resid_t = done
     return coef_t.T, resid_t.T[None]
 
 

time: 110 us -> 112 us (1.018)
  the two profiles are of different devices: /device:TPU:11 before, /device:TPU:1 now
where the time goes in v1:
time: 112 us; the launch traced here: 111 us
  starting transfers between devices  52.4 us (47%)
  waiting for transfers between devices  44.9 us (40%)
  Pallas kernels  10.3 us (9%)
  other arithmetic  2.67 us (2%)
    ppermute x33, starting transfers between devices, permute(): return lax.ppermute(x, ('grp', 'row'), route)  52.4 us
    ppermute x33, waiting for transfers between devices, permute(): return lax.ppermute(x, ('grp', 'row'), route)  44.9 us
    pallas_call x4, Pallas kernels, stage_call(): pl.pallas_call(functools.partial(stage_kernel, layout, owner), out_shape=...  4.29 us
    pallas_call x2, Pallas kernels, write_call(): pl.pallas_call(functools.partial(write_kernel, masks, chosen, len(resume)...  3.13 us
    convert_element_type x1, other arithmetic, sweep(): square = after(precond, swapped).astype(BF16)  2.51 us
  transfers between devices with their start and end apart: 33, of which 16 were waited for; matrix products, arithmetic and copies ran while one was open for 0% of the time, Pallas kernels for 3%

profile of v1, /device:TPU:1, one launch (start us, length us, event | category | flops | bytes accessed | tf_op | source)
XLA Modules:
  0.0 111.4 jit_solution(3391869490230382349)
XLA Ops:
  0.9 2.1 %collective-permute-done.refs_6_.other_ref = bf16[256,1024]{1,0:T(8,128)(2,1)S(1)} collective-permute-done((bf16[256,1024]{1,0:T(8,128)(2,1)}, bf16[256,1024]{1,0:T(8,128)(2,1)S(1)}, u32[]{:S(2)}, u32[]{:S(2)}) %collective-permute-start) | collective-permute-done | bytes 524320 | tf_op jit(solution)/shard_map/ppermute | solution.py:278
  3.0 2.5 %convert_element_type.55.own_ref = bf16[1024,1024]{1,0:T(8,128)(2,1)S(1)} convert(f32[1024,1024]{1,0:T(8,128)} %param.5) | non-fusion elementwise | flops 1048576 | bytes 6291456 | tf_op jit(solution)/shard_map/convert_element_type | solution.py:314
  5.7 2.6 %collective-permute-start.7 = (bf16[256,1024]{1,0:T(8,128)(2,1)S(1)}, bf16[256,1024]{1,0:T(8,128)(2,1)S(1)}, u32[]{:S(2)}, u32[]{:S(2)}) collective-permute-start(bf16[256,1024]{1,0:T(8,128)(2,1)S(1)} %copy-done), channel_id=1, source_target_pairs={{0,1},{1,0},{2,3},{3,2},{4,5},{5,4},{6,7},{7,6},{8,9},{9,8},{10,11... | collective-permute-start | bytes 1572872 | tf_op jit(solution)/shard_map/ppermute | solution.py:278
  8.4 2.4 %collective-permute-start.6 = (bf16[256,512]{1,0:T(8,128)(2,1)S(1)}, bf16[256,512]{1,0:T(8,128)(2,1)S(1)}, u32[]{:S(2)}, u32[]{:S(2)}) collective-permute-start(bf16[256,512]{1,0:T(8,128)(2,1)S(1)} %get-tuple-element.45), channel_id=1, source_target_pairs={{0,4},{1,5},{2,6},{3,7},{4,0},{5,1},{6,2},{7,3},{8,12},{9,13},{10,... | collective-permute-start | bytes 786440 | tf_op jit(solution)/shard_map/ppermute | solution.py:278
  10.8 17.2 %collective-permute-done.6.refs_2_ = bf16[256,512]{1,0:T(8,128)(2,1)S(1)} collective-permute-done((bf16[256,512]{1,0:T(8,128)(2,1)S(1)}, bf16[256,512]{1,0:T(8,128)(2,1)S(1)}, u32[]{:S(2)}, u32[]{:S(2)}) %collective-permute-start.6) | collective-permute-done | bytes 262176 | tf_op jit(solution)/shard_map/ppermute | solution.py:278
  28.5 1.9 %collective-permute-start.12 = (bf16[256,1024]{1,0:T(8,128)(2,1)S(1)}, bf16[256,1024]{1,0:T(8,128)(2,1)S(1)}, u32[]{:S(2)}, u32[]{:S(2)}) collective-permute-start(bf16[256,1024]{1,0:T(8,128)(2,1)S(1)} %collective-permute-done.7.refs_3_), channel_id=1, source_target_pairs={{0,8},{1,9},{2,10},{3,11},{4,12},{5,13},{6,14},{7,15},{8,0},{9,1},... | collective-permute-start | bytes 1572872 | tf_op jit(solution)/shard_map/ppermute | solution.py:278
  30.3 3.3 %collective-permute-done.4.refs_1_ = bf16[256,512]{1,0:T(8,128)(2,1)S(1)} collective-permute-done((bf16[256,512]{1,0:T(8,128)(2,1)S(1)}, bf16[256,512]{1,0:T(8,128)(2,1)S(1)}, u32[]{:S(2)}, u32[]{:S(2)}) %collective-permute-start.4) | collective-permute-done | bytes 262176 | tf_op jit(solution)/shard_map/ppermute | solution.py:278
  33.6 0.5 collective-permute-start.8
  34.2 1.1 collective-permute-start.2
  35.3 2.6 %collective-permute-done.1 = bf16[72,256]{1,0:T(8,128)(2,1)S(1)} collective-permute-done((bf16[72,256]{1,0:T(8,128)(2,1)S(1)}, bf16[72,256]{1,0:T(8,128)(2,1)S(1)}, u32[]{:S(2)}, u32[]{:S(2)}) %collective-permute-start.1) | collective-permute-done | bytes 36896 | tf_op jit(solution)/shard_map/ppermute | solution.py:278
  37.9 0.7 collective-permute-start.3
  38.6 2.4 %collective-permute-done.2 = bf16[72,256]{1,0:T(8,128)(2,1)S(1)} collective-permute-done((bf16[72,256]{1,0:T(8,128)(2,1)S(1)}, bf16[72,256]{1,0:T(8,128)(2,1)S(1)}, u32[]{:S(2)}, u32[]{:S(2)}) %collective-permute-start.2) | collective-permute-done | bytes 36896 | tf_op jit(solution)/shard_map/ppermute | solution.py:278
  41.0 2.5 %collective-permute-start.11 = (bf16[256,512]{1,0:T(8,128)(2,1)S(1)}, bf16[256,512]{1,0:T(8,128)(2,1)S(1)}, u32[]{:S(2)}, u32[]{:S(2)}) collective-permute-start(bf16[256,512]{1,0:T(8,128)(2,1)S(1)} %collective-permute-done.6.refs_2_), channel_id=1, source_target_pairs={{0,8},{1,9},{2,10},{3,11},{4,12},{5,13},{6,14},{7,15},{8,0},{9,1},... | collective-permute-start | bytes 786440 | tf_op jit(solution)/shard_map/ppermute | solution.py:278
  43.5 2.6 %collective-permute-start.10 = (bf16[256,512]{1,0:T(8,128)(2,1)S(1)}, bf16[256,512]{1,0:T(8,128)(2,1)S(1)}, u32[]{:S(2)}, u32[]{:S(2)}) collective-permute-start(bf16[256,512]{1,0:T(8,128)(2,1)S(1)} %collective-permute-done.4.refs_1_), channel_id=1, source_target_pairs={{0,8},{1,9},{2,10},{3,11},{4,12},{5,13},{6,14},{7,15},{8,0},{9,1},... | collective-permute-start | bytes 786440 | tf_op jit(solution)/shard_map/ppermute | solution.py:278
  46.3 1.0 collective-permute-done.10.refs_7_
  47.7 0.5 first_corr.4.ca_ref
  48.2 0.9 collective-permute-start.15
  49.1 4.2 %collective-permute-done.15.cb_ref = bf16[72,1024]{1,0:T(8,128)(2,1)S(1)} collective-permute-done((bf16[72,1024]{1,0:T(8,128)(2,1)S(1)}, bf16[72,1024]{1,0:T(8,128)(2,1)S(1)}, u32[]{:S(2)}, u32[]{:S(2)}) %collective-permute-start.15) | collective-permute-done | bytes 147488 | tf_op jit(solution)/shard_map/ppermute | solution.py:278
  53.3 1.2 %sweep_stage.4 = (bf16[72,1024]{1,0:T(8,128)(2,1)S(1)}, f32[72,1024]{1,0:T(8,128)S(1)}) custom-call(f32[72,1024]{1,0:T(8,128)S(1)} %pad_maximum_fusion.2.r_ref, bf16[72,1024]{1,0:T(8,128)(2,1)S(1)} %first_corr.4.ca_ref, bf16[72,1024]{1,0:T(8,128)(2,1)S(1)} %collective-permute-done.15.cb_ref, bf16[1024,1024]{1,0:T(8,128)(2,1)S(1)} %convert_element_type.55.own_ref, ...), custom_call_target="tpu_custom_call" | custom-call | flops 452984832 | bytes 4194304 | tf_op jit(solution)/shard_map/sweep_stage/pallas_call | solution.py:242
  54.5 0.5 first_corr.5.ca_ref
  55.0 0.9 collective-permute-start.16
  56.0 3.1 %collective-permute-done.16.cb_ref = bf16[72,1024]{1,0:T(8,128)(2,1)S(1)} collective-permute-done((bf16[72,1024]{1,0:T(8,128)(2,1)S(1)}, bf16[72,1024]{1,0:T(8,128)(2,1)S(1)}, u32[]{:S(2)}, u32[]{:S(2)}) %collective-permute-start.16) | collective-permute-done | bytes 147488 | tf_op jit(solution)/shard_map/ppermute | solution.py:278
  59.1 1.2 %sweep_stage.5 = (bf16[72,1024]{1,0:T(8,128)(2,1)S(1)}, bf16[72,1024]{1,0:T(8,128)(2,1)S(1)}) custom-call(f32[72,1024]{1,0:T(8,128)S(1)} %get-tuple-element.31.r_ref, bf16[72,1024]{1,0:T(8,128)(2,1)S(1)} %first_corr.5.ca_ref, bf16[72,1024]{1,0:T(8,128)(2,1)S(1)} %collective-permute-done.16.cb_ref, bf16[1024,1024]{1,0:T(8,128)(2,1)S(1)} %convert_element_type.55.own_ref, ...), custom_call_target="tpu_custom_call" | custom-call | flops 452984832 | bytes 4194304 | tf_op jit(solution)/shard_map/sweep_stage/pallas_call | solution.py:242
  60.3 3.1 %collective-permute-start.17 = (bf16[72,1024]{1,0:T(8,128)(2,1)S(1)}, bf16[72,1024]{1,0:T(8,128)(2,1)S(1)}, u32[]{:S(2)}, u32[]{:S(2)}) collective-permute-start(bf16[72,1024]{1,0:T(8,128)(2,1)S(1)} %get-tuple-element.32), channel_id=1, source_target_pairs={{0,16},{1,17},{2,18},{3,19},{4,20},{5,21},{6,22},{7,23},{8,24},{9,... | collective-permute-start | bytes 442376 | tf_op jit(solution)/shard_map/ppermute | solution.py:278
  63.5 2.1 %collective-permute-done.17.r_ref = bf16[72,1024]{1,0:T(8,128)(2,1)S(1)} collective-permute-done((bf16[72,1024]{1,0:T(8,128)(2,1)S(1)}, bf16[72,1024]{1,0:T(8,128)(2,1)S(1)}, u32[]{:S(2)}, u32[]{:S(2)}) %collective-permute-start.17) | collective-permute-done | bytes 147488 | tf_op jit(solution)/shard_map/ppermute | solution.py:278
  65.5 0.5 first_corr.6.ca_ref
  66.0 0.9 collective-permute-start.22
  67.0 3.1 %collective-permute-done.22.cb_ref = bf16[72,1024]{1,0:T(8,128)(2,1)S(1)} collective-permute-done((bf16[72,1024]{1,0:T(8,128)(2,1)S(1)}, bf16[72,1024]{1,0:T(8,128)(2,1)S(1)}, u32[]{:S(2)}, u32[]{:S(2)}) %collective-permute-start.22) | collective-permute-done | bytes 147488 | tf_op jit(solution)/shard_map/ppermute | solution.py:278
  70.1 1.2 %sweep_stage.6 = (bf16[72,1024]{1,0:T(8,128)(2,1)S(1)}, f32[72,1024]{1,0:T(8,128)S(1)}) custom-call(bf16[72,1024]{1,0:T(8,128)(2,1)S(1)} %collective-permute-done.17.r_ref, bf16[72,1024]{1,0:T(8,128)(2,1)S(1)} %first_corr.6.ca_ref, bf16[72,1024]{1,0:T(8,128)(2,1)S(1)} %collective-permute-done.22.cb_ref, bf16[1024,1024]{1,0:T(8,128)(2,1)S(1)} %convert_element_type.55.own_ref, ...), custom_call_target="tpu_custom_call" | custom-call | flops 452984832 | bytes 4194304 | tf_op jit(solution)/shard_map/sweep_stage/pallas_call | solution.py:242
  71.3 0.5 first_corr.7.ca_ref
  71.8 0.9 collective-permute-start.27
  72.8 2.7 %collective-permute-start.23 = (bf16[72,1024]{1,0:T(8,128)(2,1)S(1)}, bf16[72,1024]{1,0:T(8,128)(2,1)S(1)}, u32[]{:S(2)}, u32[]{:S(2)}) collective-permute-start(bf16[72,1024]{1,0:T(8,128)(2,1)S(1)} %broadcast_select_fusion.1.refs_0_), channel_id=1, source_target_pairs={{0,4},{1,5},{2,6},{3,7},{4,0},{5,1},{6,2},{7,3},{8,12},{9,13},{10,... | collective-permute-start | bytes 442376 | tf_op jit(solution)/shard_map/ppermute | solution.py:278
  75.5 1.2 %collective-permute-start.24 = (bf16[72,1024]{1,0:T(8,128)(2,1)S(1)}, bf16[72,1024]{1,0:T(8,128)(2,1)S(1)}, u32[]{:S(2)}, u32[]{:S(2)}) collective-permute-start(bf16[72,1024]{1,0:T(8,128)(2,1)S(1)} %broadcast_select_fusion.1.refs_0_), channel_id=1, source_target_pairs={{0,1},{1,0},{2,3},{3,2},{4,5},{5,4},{6,7},{7,6},{8,9},{9,8},{10,11... | collective-permute-start | bytes 442376 | tf_op jit(solution)/shard_map/ppermute | solution.py:278
  76.7 0.6 sweep_stage.7
  77.3 0.7 collective-permute-done.23.refs_1_
  78.0 1.2 %collective-permute-start.25 = (bf16[72,1024]{1,0:T(8,128)(2,1)S(1)}, bf16[72,1024]{1,0:T(8,128)(2,1)S(1)}, u32[]{:S(2)}, u32[]{:S(2)}) collective-permute-start(bf16[72,1024]{1,0:T(8,128)(2,1)S(1)} %collective-permute-done.23.refs_1_), channel_id=1, source_target_pairs={{0,1},{1,0},{2,3},{3,2},{4,5},{5,4},{6,7},{7,6},{8,9},{9,8},{10,11... | collective-permute-start | bytes 442376 | tf_op jit(solution)/shard_map/ppermute | solution.py:278
  79.2 2.5 %collective-permute-start.28 = (bf16[72,1024]{1,0:T(8,128)(2,1)S(1)}, bf16[72,1024]{1,0:T(8,128)(2,1)S(1)}, u32[]{:S(2)}, u32[]{:S(2)}) collective-permute-start(bf16[72,1024]{1,0:T(8,128)(2,1)S(1)} %broadcast_select_fusion.refs_4_.refs_7_), channel_id=1, source_target_pairs={{0,4},{1,5},{2,6},{3,7},{4,0},{5,1},{6,2},{7,3},{8,12},{9,13},{10,... | collective-permute-start | bytes 442376 | tf_op jit(solution)/shard_map/ppermute | solution.py:278
  82.3 10.2 %collective-permute-start.26 = (bf16[288,1024]{1,0:T(8,128)(2,1)S(1)}, bf16[288,1024]{1,0:T(8,128)(2,1)S(1)}, u32[]{:S(2)}, u32[]{:S(2)}) collective-permute-start(bf16[288,1024]{1,0:T(8,128)(2,1)S(1)} %pad_maximum_fusion), channel_id=1, source_target_pairs={{0,8},{1,9},{2,10},{3,11},{4,12},{5,13},{6,14},{7,15},{8,0},{9,1},... | collective-permute-start | bytes 1769480 | tf_op jit(solution)/shard_map/ppermute | solution.py:278
  92.6 3.9 %collective-permute-start.32 = (bf16[216,1024]{1,0:T(8,128)(2,1)S(1)}, bf16[216,1024]{1,0:T(8,128)(2,1)S(1)}, u32[]{:S(2)}, u32[]{:S(2)}) collective-permute-start(bf16[216,1024]{1,0:T(8,128)(2,1)S(1)} %pad_maximum_fusion.1), channel_id=1, source_target_pairs={{0,8},{1,9},{2,10},{3,11},{4,12},{5,13},{6,14},{7,15},{8,0},{9,1},... | collective-permute-start | bytes 1327112 | tf_op jit(solution)/shard_map/ppermute | solution.py:278
  96.5 0.9 collective-permute-start.18
  97.4 2.7 %collective-permute-start.20 = (bf16[72,256]{1,0:T(8,128)(2,1)S(1)}, bf16[72,256]{1,0:T(8,128)(2,1)S(1)}, u32[]{:S(2)}, u32[]{:S(2)}) collective-permute-start(bf16[72,256]{1,0:T(8,128)(2,1)S(1)} %get-tuple-element.48), channel_id=1, source_target_pairs={{0,5},{1,4},{2,7},{3,6},{4,1},{5,0},{6,3},{7,2},{8,13},{9,12},{10,... | collective-permute-start | bytes 110600 | tf_op jit(solution)/shard_map/ppermute | solution.py:278
  100.5 1.5 %collective-permute-done.20.refs_3_ = bf16[72,256]{1,0:T(8,128)(2,1)S(1)} collective-permute-done((bf16[72,256]{1,0:T(8,128)(2,1)S(1)}, bf16[72,256]{1,0:T(8,128)(2,1)S(1)}, u32[]{:S(2)}, u32[]{:S(2)}) %collective-permute-start.20) | collective-permute-done | bytes 36896 | tf_op jit(solution)/shard_map/ppermute | solution.py:278
  102.0 1.8 %collective-permute-start.21 = (bf16[288,256]{1,0:T(8,128)(2,1)S(1)}, bf16[288,256]{1,0:T(8,128)(2,1)S(1)}, u32[]{:S(2)}, u32[]{:S(2)}) collective-permute-start(bf16[288,256]{1,0:T(8,128)(2,1)S(1)} %pad_maximum_fusion.3), channel_id=1, source_target_pairs={{0,8},{1,9},{2,10},{3,11},{4,12},{5,13},{6,14},{7,15},{8,0},{9,1},... | collective-permute-start | bytes 442376 | tf_op jit(solution)/shard_map/ppermute | solution.py:278
  103.8 0.8 collective-permute-done.29.refs_7_
  104.6 2.8 %collective-permute-start.30 = (bf16[72,1024]{1,0:T(8,128)(2,1)S(1)}, bf16[72,1024]{1,0:T(8,128)(2,1)S(1)}, u32[]{:S(2)}, u32[]{:S(2)}) collective-permute-start(bf16[72,1024]{1,0:T(8,128)(2,1)S(1)} %collective-permute-done.29.refs_7_), channel_id=1, source_target_pairs={{0,8},{1,9},{2,10},{3,11},{4,12},{5,13},{6,14},{7,15},{8,0},{9,1},... | collective-permute-start | bytes 442376 | tf_op jit(solution)/shard_map/ppermute | solution.py:278
  107.4 0.9 shard_map.51.after_ref
  108.3 1.9 %write_early.1 = (f32[576,1024]{1,0:T(8,128)}, f32[576,256]{1,0:T(8,128)}) custom-call(bf16[256,1024]{1,0:T(8,128)(2,1)S(1)} %copy-done, f32[576,256]{1,0:T(8,128)S(1)} %shard_map.51.after_ref, bf16[288,1024]{1,0:T(8,128)(2,1)S(1)} %collective-permute-done.26.got_ref, bf16[216,1024]{1,0:T(8,128)(2,1)S(1)} %collective-permute-done.32.got_late_ref, ...), custom_call_target="tpu_custom_call" | custom-call | tf_op jit(solution)/shard_map/write_early/pallas_call | solution.py:172
  110.2 1.2 %write_rest.1 = (f32[576,1024]{1,0:T(8,128)}, f32[576,256]{1,0:T(8,128)}) custom-call(bf16[256,1024]{1,0:T(8,128)(2,1)S(1)} %copy-done, f32[576,256]{1,0:T(8,128)S(1)} %shard_map.51.after_ref, bf16[288,1024]{1,0:T(8,128)(2,1)S(1)} %collective-permute-done.26.got_ref, ...), custom_call_target="tpu_custom_call", output_to_operand_aliasing={{0}: (12, {}), {1}: (13, {})} | custom-call | tf_op jit(solution)/shard_map/write_rest/pallas_call | solution.py:172
  (48 shorter events, 2.5 us)
Async XLA Ops:
  0.8 4.9 %copy-start = (bf16[256,1024]{1,0:T(8,128)(2,1)S(1)}, bf16[256,1024]{1,0:T(8,128)(2,1)}, u32[]{:S(2)}) copy-start(bf16[256,1024]{1,0:T(8,128)(2,1)} %a_ref.1) | copy-start | bytes 1572868
  0.8 33.3 %copy-start.1 = (f32[256,576]{0,1:T(8,128)S(1)}, f32[256,576]{0,1:T(8,128)}, u32[]{:S(2)}) copy-start(f32[256,576]{0,1:T(8,128)} %param.4) | copy-start | bytes 1769476
  0.8 2.2 %collective-permute-start = (bf16[256,1024]{1,0:T(8,128)(2,1)}, bf16[256,1024]{1,0:T(8,128)(2,1)S(1)}, u32[]{:S(2)}, u32[]{:S(2)}) collective-permute-start(bf16[256,1024]{1,0:T(8,128)(2,1)} %a_ref.1), channel_id=1, source_target_pairs={{0,8},{1,9},{2,10},{3,11},{4,12},{5,13},{6,14},{7,15},{8,0},{9,1},... | collective-permute-start | bytes 1572872 | tf_op jit(solution)/shard_map/ppermute | solution.py:278
  5.5 28.1 %collective-permute-start.5 = (bf16[1024,1024]{1,0:T(8,128)(2,1)S(1)}, bf16[1024,1024]{1,0:T(8,128)(2,1)S(1)}, u32[]{:S(2)}, u32[]{:S(2)}) collective-permute-start(bf16[1024,1024]{1,0:T(8,128)(2,1)S(1)} %convert_element_type.55.own_ref), channel_id=1, source_target_pairs={{0,8},{1,9},{2,10},{3,11},{4,12},{5,13},{6,14},{7,15},{8,0},{9,1},... | collective-permute-start | bytes 6291464 | tf_op jit(solution)/shard_map/ppermute | solution.py:278
  5.7 22.7 %collective-permute-start.7 = (bf16[256,1024]{1,0:T(8,128)(2,1)S(1)}, bf16[256,1024]{1,0:T(8,128)(2,1)S(1)}, u32[]{:S(2)}, u32[]{:S(2)}) collective-permute-start(bf16[256,1024]{1,0:T(8,128)(2,1)S(1)} %copy-done), channel_id=1, source_target_pairs={{0,1},{1,0},{2,3},{3,2},{4,5},{5,4},{6,7},{7,6},{8,9},{9,8},{10,11... | collective-permute-start | bytes 1572872 | tf_op jit(solution)/shard_map/ppermute | solution.py:278
  8.4 19.6 %collective-permute-start.6 = (bf16[256,512]{1,0:T(8,128)(2,1)S(1)}, bf16[256,512]{1,0:T(8,128)(2,1)S(1)}, u32[]{:S(2)}, u32[]{:S(2)}) collective-permute-start(bf16[256,512]{1,0:T(8,128)(2,1)S(1)} %get-tuple-element.45), channel_id=1, source_target_pairs={{0,4},{1,5},{2,6},{3,7},{4,0},{5,1},{6,2},{7,3},{8,12},{9,13},{10,... | collective-permute-start | bytes 786440 | tf_op jit(solution)/shard_map/ppermute | solution.py:278
  10.7 22.9 %collective-permute-start.4 = (bf16[256,512]{1,0:T(8,128)(2,1)S(1)}, bf16[256,512]{1,0:T(8,128)(2,1)S(1)}, u32[]{:S(2)}, u32[]{:S(2)}) collective-permute-start(bf16[256,512]{1,0:T(8,128)(2,1)S(1)} %get-tuple-element.46), channel_id=1, source_target_pairs={{0,4},{1,5},{2,6},{3,7},{4,0},{5,1},{6,2},{7,3},{8,12},{9,13},{10,... | collective-permute-start | bytes 786440 | tf_op jit(solution)/shard_map/ppermute | solution.py:278
  28.0 15.5 %collective-permute-start.9 = (bf16[256,512]{1,0:T(8,128)(2,1)S(1)}, bf16[256,512]{1,0:T(8,128)(2,1)S(1)}, u32[]{:S(2)}, u32[]{:S(2)}) collective-permute-start(bf16[256,512]{1,0:T(8,128)(2,1)S(1)} %collective-permute-done.6.refs_2_), channel_id=1, source_target_pairs={{0,1},{1,0},{2,3},{3,2},{4,5},{5,4},{6,7},{7,6},{8,9},{9,8},{10,11... | collective-permute-start | bytes 786440 | tf_op jit(solution)/shard_map/ppermute | solution.py:278
  28.5 17.8 %collective-permute-start.12 = (bf16[256,1024]{1,0:T(8,128)(2,1)S(1)}, bf16[256,1024]{1,0:T(8,128)(2,1)S(1)}, u32[]{:S(2)}, u32[]{:S(2)}) collective-permute-start(bf16[256,1024]{1,0:T(8,128)(2,1)S(1)} %collective-permute-done.7.refs_3_), channel_id=1, source_target_pairs={{0,8},{1,9},{2,10},{3,11},{4,12},{5,13},{6,14},{7,15},{8,0},{9,1},... | collective-permute-start | bytes 1572872 | tf_op jit(solution)/shard_map/ppermute | solution.py:278
  33.6 12.5 %collective-permute-start.8 = (bf16[256,512]{1,0:T(8,128)(2,1)S(1)}, bf16[256,512]{1,0:T(8,128)(2,1)S(1)}, u32[]{:S(2)}, u32[]{:S(2)}) collective-permute-start(bf16[256,512]{1,0:T(8,128)(2,1)S(1)} %collective-permute-done.4.refs_1_), channel_id=1, source_target_pairs={{0,1},{1,0},{2,3},{3,2},{4,5},{5,4},{6,7},{7,6},{8,9},{9,8},{10,11... | collective-permute-start | bytes 786440 | tf_op jit(solution)/shard_map/ppermute | solution.py:278
  34.1 3.8 %collective-permute-start.1 = (bf16[72,256]{1,0:T(8,128)(2,1)S(1)}, bf16[72,256]{1,0:T(8,128)(2,1)S(1)}, u32[]{:S(2)}, u32[]{:S(2)}) collective-permute-start(bf16[72,256]{1,0:T(8,128)(2,1)S(1)} %get-tuple-element.42), channel_id=1, source_target_pairs={{0,4},{1,5},{2,6},{3,7},{4,0},{5,1},{6,2},{7,3},{8,12},{9,13},{10,... | collective-permute-start | bytes 110600 | tf_op jit(solution)/shard_map/ppermute | solution.py:278
  34.2 6.8 %collective-permute-start.2 = (bf16[72,256]{1,0:T(8,128)(2,1)S(1)}, bf16[72,256]{1,0:T(8,128)(2,1)S(1)}, u32[]{:S(2)}, u32[]{:S(2)}) collective-permute-start(bf16[72,256]{1,0:T(8,128)(2,1)S(1)} %get-tuple-element.44), channel_id=1, source_target_pairs={{0,1},{1,0},{2,3},{3,2},{4,5},{5,4},{6,7},{7,6},{8,9},{9,8},{10,11... | collective-permute-start | bytes 110600 | tf_op jit(solution)/shard_map/ppermute | solution.py:278
  37.9 5.7 %collective-permute-start.3 = (bf16[72,256]{1,0:T(8,128)(2,1)S(1)}, bf16[72,256]{1,0:T(8,128)(2,1)S(1)}, u32[]{:S(2)}, u32[]{:S(2)}) collective-permute-start(bf16[72,256]{1,0:T(8,128)(2,1)S(1)} %get-tuple-element.43), channel_id=1, source_target_pairs={{0,5},{1,4},{2,7},{3,6},{4,1},{5,0},{6,3},{7,2},{8,13},{9,12},{10,... | collective-permute-start | bytes 110600 | tf_op jit(solution)/shard_map/ppermute | solution.py:278
  41.0 5.2 %collective-permute-start.11 = (bf16[256,512]{1,0:T(8,128)(2,1)S(1)}, bf16[256,512]{1,0:T(8,128)(2,1)S(1)}, u32[]{:S(2)}, u32[]{:S(2)}) collective-permute-start(bf16[256,512]{1,0:T(8,128)(2,1)S(1)} %collective-permute-done.6.refs_2_), channel_id=1, source_target_pairs={{0,8},{1,9},{2,10},{3,11},{4,12},{5,13},{6,14},{7,15},{8,0},{9,1},... | collective-permute-start | bytes 786440 | tf_op jit(solution)/shard_map/ppermute | solution.py:278
  43.5 2.7 %collective-permute-start.14 = (bf16[256,512]{1,0:T(8,128)(2,1)S(1)}, bf16[256,512]{1,0:T(8,128)(2,1)S(1)}, u32[]{:S(2)}, u32[]{:S(2)}) collective-permute-start(bf16[256,512]{1,0:T(8,128)(2,1)S(1)} %collective-permute-done.9.refs_5_), channel_id=1, source_target_pairs={{0,8},{1,9},{2,10},{3,11},{4,12},{5,13},{6,14},{7,15},{8,0},{9,1},... | collective-permute-start | bytes 786440 | tf_op jit(solution)/shard_map/ppermute | solution.py:278
  43.5 3.8 %collective-permute-start.10 = (bf16[256,512]{1,0:T(8,128)(2,1)S(1)}, bf16[256,512]{1,0:T(8,128)(2,1)S(1)}, u32[]{:S(2)}, u32[]{:S(2)}) collective-permute-start(bf16[256,512]{1,0:T(8,128)(2,1)S(1)} %collective-permute-done.4.refs_1_), channel_id=1, source_target_pairs={{0,8},{1,9},{2,10},{3,11},{4,12},{5,13},{6,14},{7,15},{8,0},{9,1},... | collective-permute-start | bytes 786440 | tf_op jit(solution)/shard_map/ppermute | solution.py:278
  46.1 1.5 %collective-permute-start.13 = (bf16[256,512]{1,0:T(8,128)(2,1)S(1)}, bf16[256,512]{1,0:T(8,128)(2,1)S(1)}, u32[]{:S(2)}, u32[]{:S(2)}) collective-permute-start(bf16[256,512]{1,0:T(8,128)(2,1)S(1)} %collective-permute-done.8.refs_4_), channel_id=1, source_target_pairs={{0,8},{1,9},{2,10},{3,11},{4,12},{5,13},{6,14},{7,15},{8,0},{9,1},... | collective-permute-start | bytes 786440 | tf_op jit(solution)/shard_map/ppermute | solution.py:278
  48.2 5.1 %collective-permute-start.15 = (bf16[72,1024]{1,0:T(8,128)(2,1)S(1)}, bf16[72,1024]{1,0:T(8,128)(2,1)S(1)}, u32[]{:S(2)}, u32[]{:S(2)}) collective-permute-start(bf16[72,1024]{1,0:T(8,128)(2,1)S(1)} %first_corr.4.ca_ref), channel_id=1, source_target_pairs={{0,2},{1,3},{2,0},{3,1},{4,6},{5,7},{6,4},{7,5},{8,10},{9,11},{10,... | collective-permute-start | bytes 442376 | tf_op jit(solution)/shard_map/ppermute | solution.py:278
  55.0 4.1 %collective-permute-start.16 = (bf16[72,1024]{1,0:T(8,128)(2,1)S(1)}, bf16[72,1024]{1,0:T(8,128)(2,1)S(1)}, u32[]{:S(2)}, u32[]{:S(2)}) collective-permute-start(bf16[72,1024]{1,0:T(8,128)(2,1)S(1)} %first_corr.5.ca_ref), channel_id=1, source_target_pairs={{0,2},{1,3},{2,0},{3,1},{4,6},{5,7},{6,4},{7,5},{8,10},{9,11},{10,... | collective-permute-start | bytes 442376 | tf_op jit(solution)/shard_map/ppermute | solution.py:278
  60.3 5.2 %collective-permute-start.17 = (bf16[72,1024]{1,0:T(8,128)(2,1)S(1)}, bf16[72,1024]{1,0:T(8,128)(2,1)S(1)}, u32[]{:S(2)}, u32[]{:S(2)}) collective-permute-start(bf16[72,1024]{1,0:T(8,128)(2,1)S(1)} %get-tuple-element.32), channel_id=1, source_target_pairs={{0,16},{1,17},{2,18},{3,19},{4,20},{5,21},{6,22},{7,23},{8,24},{9,... | collective-permute-start | bytes 442376 | tf_op jit(solution)/shard_map/ppermute | solution.py:278
  66.0 4.1 %collective-permute-start.22 = (bf16[72,1024]{1,0:T(8,128)(2,1)S(1)}, bf16[72,1024]{1,0:T(8,128)(2,1)S(1)}, u32[]{:S(2)}, u32[]{:S(2)}) collective-permute-start(bf16[72,1024]{1,0:T(8,128)(2,1)S(1)} %first_corr.6.ca_ref), channel_id=1, source_target_pairs={{0,2},{1,3},{2,0},{3,1},{4,6},{5,7},{6,4},{7,5},{8,10},{9,11},{10,... | collective-permute-start | bytes 442376 | tf_op jit(solution)/shard_map/ppermute | solution.py:278
  71.8 4.9 %collective-permute-start.27 = (bf16[72,1024]{1,0:T(8,128)(2,1)S(1)}, bf16[72,1024]{1,0:T(8,128)(2,1)S(1)}, u32[]{:S(2)}, u32[]{:S(2)}) collective-permute-start(bf16[72,1024]{1,0:T(8,128)(2,1)S(1)} %first_corr.7.ca_ref), channel_id=1, source_target_pairs={{0,2},{1,3},{2,0},{3,1},{4,6},{5,7},{6,4},{7,5},{8,10},{9,11},{10,... | collective-permute-start | bytes 442376 | tf_op jit(solution)/shard_map/ppermute | solution.py:278
  72.8 5.2 %collective-permute-start.23 = (bf16[72,1024]{1,0:T(8,128)(2,1)S(1)}, bf16[72,1024]{1,0:T(8,128)(2,1)S(1)}, u32[]{:S(2)}, u32[]{:S(2)}) collective-permute-start(bf16[72,1024]{1,0:T(8,128)(2,1)S(1)} %broadcast_select_fusion.1.refs_0_), channel_id=1, source_target_pairs={{0,4},{1,5},{2,6},{3,7},{4,0},{5,1},{6,2},{7,3},{8,12},{9,13},{10,... | collective-permute-start | bytes 442376 | tf_op jit(solution)/shard_map/ppermute | solution.py:278
  75.5 6.5 %collective-permute-start.24 = (bf16[72,1024]{1,0:T(8,128)(2,1)S(1)}, bf16[72,1024]{1,0:T(8,128)(2,1)S(1)}, u32[]{:S(2)}, u32[]{:S(2)}) collective-permute-start(bf16[72,1024]{1,0:T(8,128)(2,1)S(1)} %broadcast_select_fusion.1.refs_0_), channel_id=1, source_target_pairs={{0,1},{1,0},{2,3},{3,2},{4,5},{5,4},{6,7},{7,6},{8,9},{9,8},{10,11... | collective-permute-start | bytes 442376 | tf_op jit(solution)/shard_map/ppermute | solution.py:278
  78.0 4.3 %collective-permute-start.25 = (bf16[72,1024]{1,0:T(8,128)(2,1)S(1)}, bf16[72,1024]{1,0:T(8,128)(2,1)S(1)}, u32[]{:S(2)}, u32[]{:S(2)}) collective-permute-start(bf16[72,1024]{1,0:T(8,128)(2,1)S(1)} %collective-permute-done.23.refs_1_), channel_id=1, source_target_pairs={{0,1},{1,0},{2,3},{3,2},{4,5},{5,4},{6,7},{7,6},{8,9},{9,8},{10,11... | collective-permute-start | bytes 442376 | tf_op jit(solution)/shard_map/ppermute | solution.py:278
  79.2 13.3 %collective-permute-start.28 = (bf16[72,1024]{1,0:T(8,128)(2,1)S(1)}, bf16[72,1024]{1,0:T(8,128)(2,1)S(1)}, u32[]{:S(2)}, u32[]{:S(2)}) collective-permute-start(bf16[72,1024]{1,0:T(8,128)(2,1)S(1)} %broadcast_select_fusion.refs_4_.refs_7_), channel_id=1, source_target_pairs={{0,4},{1,5},{2,6},{3,7},{4,0},{5,1},{6,2},{7,3},{8,12},{9,13},{10,... | collective-permute-start | bytes 442376 | tf_op jit(solution)/shard_map/ppermute | solution.py:278
  81.8 10.8 %collective-permute-start.31 = (bf16[72,1024]{1,0:T(8,128)(2,1)S(1)}, bf16[72,1024]{1,0:T(8,128)(2,1)S(1)}, u32[]{:S(2)}, u32[]{:S(2)}) collective-permute-start(bf16[72,1024]{1,0:T(8,128)(2,1)S(1)} %broadcast_select_fusion.refs_4_.refs_7_), channel_id=1, source_target_pairs={{0,1},{1,0},{2,3},{3,2},{4,5},{5,4},{6,7},{7,6},{8,9},{9,8},{10,11... | collective-permute-start | bytes 442376 | tf_op jit(solution)/shard_map/ppermute | solution.py:278
  82.3 25.0 %collective-permute-start.26 = (bf16[288,1024]{1,0:T(8,128)(2,1)S(1)}, bf16[288,1024]{1,0:T(8,128)(2,1)S(1)}, u32[]{:S(2)}, u32[]{:S(2)}) collective-permute-start(bf16[288,1024]{1,0:T(8,128)(2,1)S(1)} %pad_maximum_fusion), channel_id=1, source_target_pairs={{0,8},{1,9},{2,10},{3,11},{4,12},{5,13},{6,14},{7,15},{8,0},{9,1},... | collective-permute-start | bytes 1769480 | tf_op jit(solution)/shard_map/ppermute | solution.py:278
  92.6 15.7 %collective-permute-start.32 = (bf16[216,1024]{1,0:T(8,128)(2,1)S(1)}, bf16[216,1024]{1,0:T(8,128)(2,1)S(1)}, u32[]{:S(2)}, u32[]{:S(2)}) collective-permute-start(bf16[216,1024]{1,0:T(8,128)(2,1)S(1)} %pad_maximum_fusion.1), channel_id=1, source_target_pairs={{0,8},{1,9},{2,10},{3,11},{4,12},{5,13},{6,14},{7,15},{8,0},{9,1},... | collective-permute-start | bytes 1327112 | tf_op jit(solution)/shard_map/ppermute | solution.py:278
  96.5 3.8 %collective-permute-start.18 = (bf16[72,256]{1,0:T(8,128)(2,1)S(1)}, bf16[72,256]{1,0:T(8,128)(2,1)S(1)}, u32[]{:S(2)}, u32[]{:S(2)}) collective-permute-start(bf16[72,256]{1,0:T(8,128)(2,1)S(1)} %get-tuple-element.50), channel_id=1, source_target_pairs={{0,4},{1,5},{2,6},{3,7},{4,0},{5,1},{6,2},{7,3},{8,12},{9,13},{10,... | collective-permute-start | bytes 110600 | tf_op jit(solution)/shard_map/ppermute | solution.py:278
  97.4 3.1 %collective-permute-start.19 = (bf16[72,256]{1,0:T(8,128)(2,1)S(1)}, bf16[72,256]{1,0:T(8,128)(2,1)S(1)}, u32[]{:S(2)}, u32[]{:S(2)}) collective-permute-start(bf16[72,256]{1,0:T(8,128)(2,1)S(1)} %get-tuple-element.49), channel_id=1, source_target_pairs={{0,1},{1,0},{2,3},{3,2},{4,5},{5,4},{6,7},{7,6},{8,9},{9,8},{10,11... | collective-permute-start | bytes 110600 | tf_op jit(solution)/shard_map/ppermute | solution.py:278
  97.4 4.6 %collective-permute-start.20 = (bf16[72,256]{1,0:T(8,128)(2,1)S(1)}, bf16[72,256]{1,0:T(8,128)(2,1)S(1)}, u32[]{:S(2)}, u32[]{:S(2)}) collective-permute-start(bf16[72,256]{1,0:T(8,128)(2,1)S(1)} %get-tuple-element.48), channel_id=1, source_target_pairs={{0,5},{1,4},{2,7},{3,6},{4,1},{5,0},{6,3},{7,2},{8,13},{9,12},{10,... | collective-permute-start | bytes 110600 | tf_op jit(solution)/shard_map/ppermute | solution.py:278
  100.2 4.3 %collective-permute-start.29 = (bf16[72,1024]{1,0:T(8,128)(2,1)S(1)}, bf16[72,1024]{1,0:T(8,128)(2,1)S(1)}, u32[]{:S(2)}, u32[]{:S(2)}) collective-permute-start(bf16[72,1024]{1,0:T(8,128)(2,1)S(1)} %collective-permute-done.28.refs_5_), channel_id=1, source_target_pairs={{0,1},{1,0},{2,3},{3,2},{4,5},{5,4},{6,7},{7,6},{8,9},{9,8},{10,11... | collective-permute-start | bytes 442376 | tf_op jit(solution)/shard_map/ppermute | solution.py:278
  102.0 5.3 %collective-permute-start.21 = (bf16[288,256]{1,0:T(8,128)(2,1)S(1)}, bf16[288,256]{1,0:T(8,128)(2,1)S(1)}, u32[]{:S(2)}, u32[]{:S(2)}) collective-permute-start(bf16[288,256]{1,0:T(8,128)(2,1)S(1)} %pad_maximum_fusion.3), channel_id=1, source_target_pairs={{0,8},{1,9},{2,10},{3,11},{4,12},{5,13},{6,14},{7,15},{8,0},{9,1},... | collective-permute-start | bytes 442376 | tf_op jit(solution)/shard_map/ppermute | solution.py:278
  104.6 5.6 %collective-permute-start.30 = (bf16[72,1024]{1,0:T(8,128)(2,1)S(1)}, bf16[72,1024]{1,0:T(8,128)(2,1)S(1)}, u32[]{:S(2)}, u32[]{:S(2)}) collective-permute-start(bf16[72,1024]{1,0:T(8,128)(2,1)S(1)} %collective-permute-done.29.refs_7_), channel_id=1, source_target_pairs={{0,8},{1,9},{2,10},{3,11},{4,12},{5,13},{6,14},{7,15},{8,0},{9,1},... | collective-permute-start | bytes 442376 | tf_op jit(solution)/shard_map/ppermute | solution.py:278

commit v2 on v1

--- a/solution.py
+++ b/solution.py
@@ -12,6 +12,7 @@
 BF16 = jnp.bfloat16
 CORES = 2
 PAIR = 2
+CUTS = (0, 2, 4, 6, 8)
 TILE = 8
 ANY = pl.BlockSpec(memory_space=pl.ANY)
 VMEM = pl.BlockSpec(memory_space=pltpu.VMEM)
@@ -27,20 +28,19 @@
 
 
 def correlation(r_ref, blocks, c_ref):
-    rows, feats = blocks[0][0].shape[0], c_ref.shape[1]
-    cut = feats // 2
-    whole = [(q, b[0]) for q, b in enumerate(blocks) if len(b) == 1]
-    split = [(q, b) for q, b in enumerate(blocks) if len(b) == 2]
+    rows = blocks[0][0].shape[0]
+    split = max(blocks, key=len)
     lhs = [r_ref[:, q * rows:(q + 1) * rows].astype(BF16) for q in range(len(blocks))]
-    for k in range(2):
-        span = pl.ds(k * cut, cut)
+    start = 0
+    for k, piece in enumerate(split):
+        span = pl.ds(start, piece.shape[1])
         total = None
-        for q, block in whole:
-            part = jnp.dot(lhs[q], block[:, span], preferred_element_type=F32)
+        for x, block in zip(lhs, blocks):
+            part = block[0][:, span] if len(block) == 1 else block[k][...]
+            part = jnp.dot(x, part, preferred_element_type=F32)
             total = part if total is None else total + part
-        for q, block in split:
-            total += jnp.dot(lhs[q], block[k][...], preferred_element_type=F32)
         c_ref[:, span] = total.astype(BF16)
+        start += piece.shape[1]
 
 
 def core_is(index):
@@ -75,13 +75,14 @@
         if not rn_ref:
             return
         rows = blocks[0][0].shape[0]
-        cut = wb.shape[1] // 2
         for q, block in enumerate(blocks):
             span = pl.ds(q * rows, rows)
-            if len(block) == 1:
-                change = product(wb, block[0])
-            else:
-                change = product(wb[:, :cut], block[0]) + product(wb[:, cut:], block[1])
+            change, start = None, 0
+            for piece in block:
+                size = piece.shape[1]
+                part = product(wb[:, start:start + size], piece)
+                change = part if change is None else change + part
+                start += size
             rn_ref[0][:, span] = (r_ref[:, span].astype(F32) - change).astype(rn_ref[0].dtype)
 
     @pl.when(core_is(owner))
@@ -302,10 +303,11 @@
     far = bits[-1]
     near = bits[:-1]
     count = len(masks)
-    halves = [features[:, : feats // 2], features[:, feats // 2 :]]
+    edges = [feats * e // CUTS[-1] for e in CUTS]
+    parts_of_a = [features[:, low:high] for low, high in zip(edges[:-1], edges[1:])]
 
     held = {0: [features]}
-    held[far] = [permute(x, mask=far) for x in halves]
+    held[far] = [permute(x, mask=far) for x in parts_of_a]
     for bit in reversed(near):
         for m in masks:
             if m not in held and (m ^ bit) in held and not m & far:

time: 112 us -> 119 us (1.062)
  starting transfers between devices: 52.4 us -> 60.6 us
    ppermute x33 -> x41, starting transfers between devices: 52.4 us -> 60.6 us  [permute(): return lax.ppermute(x, ('grp', 'row'), route)]
    ppermute x33 -> x41, waiting for transfers between devices: 44.9 us -> 43.9 us  [permute(): return lax.ppermute(x, ('grp', 'row'), route)]
  transfers between devices with their start and end apart: 33 -> 41, of which waited for: 16 -> 19; matrix products, arithmetic and copies ran while one was open for 0% -> 0% of each run, Pallas kernels for 3% -> 3%
where the time goes in v2:
time: 119 us; the launch traced here: 118 us
  starting transfers between devices  60.6 us (51%)
  waiting for transfers between devices  43.9 us (37%)
  Pallas kernels  10.2 us (9%)
  other arithmetic  2.67 us (2%)
    ppermute x41, starting transfers between devices, permute(): return lax.ppermute(x, ('grp', 'row'), route)  60.6 us
    ppermute x41, waiting for transfers between devices, permute(): return lax.ppermute(x, ('grp', 'row'), route)  43.9 us
    pallas_call x4, Pallas kernels, stage_call(): pl.pallas_call(functools.partial(stage_kernel, layout, owner), out_shape=...  4.12 us
    pallas_call x2, Pallas kernels, write_call(): pl.pallas_call(functools.partial(write_kernel, masks, chosen, len(resume)...  3.13 us
    convert_element_type x1, other arithmetic, sweep(): square = after(precond, swapped).astype(BF16)  2.51 us
  transfers between devices with their start and end apart: 41, of which 19 were waited for; matrix products, arithmetic and copies ran while one was open for 0% of the time, Pallas kernels for 3%

profile of v2, /device:TPU:1, one launch (start us, length us, event | category | flops | bytes accessed | tf_op | source)
XLA Modules:
  0.0 118.4 jit_solution(15199367580984105797)
XLA Ops:
  0.9 2.1 %collective-permute-done.refs_10_.other_ref = bf16[256,1024]{1,0:T(8,128)(2,1)S(1)} collective-permute-done((bf16[256,1024]{1,0:T(8,128)(2,1)}, bf16[256,1024]{1,0:T(8,128)(2,1)S(1)}, u32[]{:S(2)}, u32[]{:S(2)}) %collective-permute-start) | collective-permute-done | bytes 524320 | tf_op jit(solution)/shard_map/ppermute | solution.py:279
  3.0 2.5 %convert_element_type.55.own_ref = bf16[1024,1024]{1,0:T(8,128)(2,1)S(1)} convert(f32[1024,1024]{1,0:T(8,128)} %param.5) | non-fusion elementwise | flops 1048576 | bytes 6291456 | tf_op jit(solution)/shard_map/convert_element_type | solution.py:316
  5.7 2.6 %collective-permute-start.9 = (bf16[256,1024]{1,0:T(8,128)(2,1)S(1)}, bf16[256,1024]{1,0:T(8,128)(2,1)S(1)}, u32[]{:S(2)}, u32[]{:S(2)}) collective-permute-start(bf16[256,1024]{1,0:T(8,128)(2,1)S(1)} %copy-done), channel_id=1, source_target_pairs={{0,1},{1,0},{2,3},{3,2},{4,5},{5,4},{6,7},{7,6},{8,9},{9,8},{10,11... | collective-permute-start | bytes 1572872 | tf_op jit(solution)/shard_map/ppermute | solution.py:279
  8.4 2.4 %collective-permute-start.4 = (bf16[256,256]{1,0:T(8,128)(2,1)S(1)}, bf16[256,256]{1,0:T(8,128)(2,1)S(1)}, u32[]{:S(2)}, u32[]{:S(2)}) collective-permute-start(bf16[256,256]{1,0:T(8,128)(2,1)S(1)} %get-tuple-element.48), channel_id=1, source_target_pairs={{0,4},{1,5},{2,6},{3,7},{4,0},{5,1},{6,2},{7,3},{8,12},{9,13},{10,... | collective-permute-start | bytes 393224 | tf_op jit(solution)/shard_map/ppermute | solution.py:279
  11.1 7.2 %collective-permute-done.1 = bf16[72,256]{1,0:T(8,128)(2,1)S(1)} collective-permute-done((bf16[72,256]{1,0:T(8,128)(2,1)S(1)}, bf16[72,256]{1,0:T(8,128)(2,1)S(1)}, u32[]{:S(2)}, u32[]{:S(2)}) %collective-permute-start.1) | collective-permute-done | bytes 36896 | tf_op jit(solution)/shard_map/ppermute | solution.py:279
  18.3 2.9 %collective-permute-done.2 = bf16[72,256]{1,0:T(8,128)(2,1)S(1)} collective-permute-done((bf16[72,256]{1,0:T(8,128)(2,1)S(1)}, bf16[72,256]{1,0:T(8,128)(2,1)S(1)}, u32[]{:S(2)}, u32[]{:S(2)}) %collective-permute-start.2) | collective-permute-done | bytes 36896 | tf_op jit(solution)/shard_map/ppermute | solution.py:279
  21.3 2.7 %collective-permute-start.6 = (bf16[256,256]{1,0:T(8,128)(2,1)S(1)}, bf16[256,256]{1,0:T(8,128)(2,1)S(1)}, u32[]{:S(2)}, u32[]{:S(2)}) collective-permute-start(bf16[256,256]{1,0:T(8,128)(2,1)S(1)} %get-tuple-element.47), channel_id=1, source_target_pairs={{0,4},{1,5},{2,6},{3,7},{4,0},{5,1},{6,2},{7,3},{8,12},{9,13},{10,... | collective-permute-start | bytes 393224 | tf_op jit(solution)/shard_map/ppermute | solution.py:279
  23.9 2.3 %collective-permute-start.8 = (bf16[256,256]{1,0:T(8,128)(2,1)S(1)}, bf16[256,256]{1,0:T(8,128)(2,1)S(1)}, u32[]{:S(2)}, u32[]{:S(2)}) collective-permute-start(bf16[256,256]{1,0:T(8,128)(2,1)S(1)} %get-tuple-element.45), channel_id=1, source_target_pairs={{0,4},{1,5},{2,6},{3,7},{4,0},{5,1},{6,2},{7,3},{8,12},{9,13},{10,... | collective-permute-start | bytes 393224 | tf_op jit(solution)/shard_map/ppermute | solution.py:279
  26.3 2.4 %collective-permute-start.18 = (bf16[256,1024]{1,0:T(8,128)(2,1)S(1)}, bf16[256,1024]{1,0:T(8,128)(2,1)S(1)}, u32[]{:S(2)}, u32[]{:S(2)}) collective-permute-start(bf16[256,1024]{1,0:T(8,128)(2,1)S(1)} %collective-permute-done.9.refs_5_), channel_id=1, source_target_pairs={{0,8},{1,9},{2,10},{3,11},{4,12},{5,13},{6,14},{7,15},{8,0},{9,1},... | collective-permute-start | bytes 1572872 | tf_op jit(solution)/shard_map/ppermute | solution.py:279
  28.7 6.9 %collective-permute-done.6.refs_2_ = bf16[256,256]{1,0:T(8,128)(2,1)S(1)} collective-permute-done((bf16[256,256]{1,0:T(8,128)(2,1)S(1)}, bf16[256,256]{1,0:T(8,128)(2,1)S(1)}, u32[]{:S(2)}, u32[]{:S(2)}) %collective-permute-start.6) | collective-permute-done | bytes 131104 | tf_op jit(solution)/shard_map/ppermute | solution.py:279
  35.6 2.0 %collective-permute-start.11 = (bf16[256,256]{1,0:T(8,128)(2,1)S(1)}, bf16[256,256]{1,0:T(8,128)(2,1)S(1)}, u32[]{:S(2)}, u32[]{:S(2)}) collective-permute-start(bf16[256,256]{1,0:T(8,128)(2,1)S(1)} %collective-permute-done.6.refs_2_), channel_id=1, source_target_pairs={{0,1},{1,0},{2,3},{3,2},{4,5},{5,4},{6,7},{7,6},{8,9},{9,8},{10,11... | collective-permute-start | bytes 393224 | tf_op jit(solution)/shard_map/ppermute | solution.py:279
  37.6 0.8 collective-permute-done.7.refs_3_
  38.4 2.0 %collective-permute-start.12 = (bf16[256,256]{1,0:T(8,128)(2,1)S(1)}, bf16[256,256]{1,0:T(8,128)(2,1)S(1)}, u32[]{:S(2)}, u32[]{:S(2)}) collective-permute-start(bf16[256,256]{1,0:T(8,128)(2,1)S(1)} %collective-permute-done.7.refs_3_), channel_id=1, source_target_pairs={{0,1},{1,0},{2,3},{3,2},{4,5},{5,4},{6,7},{7,6},{8,9},{9,8},{10,11... | collective-permute-start | bytes 393224 | tf_op jit(solution)/shard_map/ppermute | solution.py:279
  40.4 0.8 collective-permute-done.8.refs_4_
  41.2 2.0 %collective-permute-start.13 = (bf16[256,256]{1,0:T(8,128)(2,1)S(1)}, bf16[256,256]{1,0:T(8,128)(2,1)S(1)}, u32[]{:S(2)}, u32[]{:S(2)}) collective-permute-start(bf16[256,256]{1,0:T(8,128)(2,1)S(1)} %collective-permute-done.8.refs_4_), channel_id=1, source_target_pairs={{0,1},{1,0},{2,3},{3,2},{4,5},{5,4},{6,7},{7,6},{8,9},{9,8},{10,11... | collective-permute-start | bytes 393224 | tf_op jit(solution)/shard_map/ppermute | solution.py:279
  43.2 1.1 collective-permute-start.15
  44.4 1.6 %collective-permute-start.17 = (bf16[256,256]{1,0:T(8,128)(2,1)S(1)}, bf16[256,256]{1,0:T(8,128)(2,1)S(1)}, u32[]{:S(2)}, u32[]{:S(2)}) collective-permute-start(bf16[256,256]{1,0:T(8,128)(2,1)S(1)} %collective-permute-done.8.refs_4_), channel_id=1, source_target_pairs={{0,8},{1,9},{2,10},{3,11},{4,12},{5,13},{6,14},{7,15},{8,0},{9,1},... | collective-permute-start | bytes 393224 | tf_op jit(solution)/shard_map/ppermute | solution.py:279
  46.0 1.3 %collective-permute-done.13.refs_9_ = bf16[256,256]{1,0:T(8,128)(2,1)S(1)} collective-permute-done((bf16[256,256]{1,0:T(8,128)(2,1)S(1)}, bf16[256,256]{1,0:T(8,128)(2,1)S(1)}, u32[]{:S(2)}, u32[]{:S(2)}) %collective-permute-start.13) | collective-permute-done | bytes 131104 | tf_op jit(solution)/shard_map/ppermute | solution.py:279
  47.2 1.0 collective-permute-start.20
  48.2 1.2 %collective-permute-start.10 = (bf16[256,256]{1,0:T(8,128)(2,1)S(1)}, bf16[256,256]{1,0:T(8,128)(2,1)S(1)}, u32[]{:S(2)}, u32[]{:S(2)}) collective-permute-start(bf16[256,256]{1,0:T(8,128)(2,1)S(1)} %collective-permute-done.4.refs_1_), channel_id=1, source_target_pairs={{0,1},{1,0},{2,3},{3,2},{4,5},{5,4},{6,7},{7,6},{8,9},{9,8},{10,11... | collective-permute-start | bytes 393224 | tf_op jit(solution)/shard_map/ppermute | solution.py:279
  50.3 3.0 %collective-permute-done.10.refs_6_ = bf16[256,256]{1,0:T(8,128)(2,1)S(1)} collective-permute-done((bf16[256,256]{1,0:T(8,128)(2,1)S(1)}, bf16[256,256]{1,0:T(8,128)(2,1)S(1)}, u32[]{:S(2)}, u32[]{:S(2)}) %collective-permute-start.10) | collective-permute-done | bytes 131104 | tf_op jit(solution)/shard_map/ppermute | solution.py:279
  53.3 0.9 collective-permute-start.19
  54.3 0.9 collective-permute-done.19.refs_16_
  55.7 5.0 %collective-permute-done.23.cb_ref = bf16[72,1024]{1,0:T(8,128)(2,1)S(1)} collective-permute-done((bf16[72,1024]{1,0:T(8,128)(2,1)S(1)}, bf16[72,1024]{1,0:T(8,128)(2,1)S(1)}, u32[]{:S(2)}, u32[]{:S(2)}) %collective-permute-start.23) | collective-permute-done | bytes 147488 | tf_op jit(solution)/shard_map/ppermute | solution.py:279
  60.7 1.2 sweep_stage.4
  62.6 3.9 %collective-permute-done.24.cb_ref = bf16[72,1024]{1,0:T(8,128)(2,1)S(1)} collective-permute-done((bf16[72,1024]{1,0:T(8,128)(2,1)S(1)}, bf16[72,1024]{1,0:T(8,128)(2,1)S(1)}, u32[]{:S(2)}, u32[]{:S(2)}) %collective-permute-start.24) | collective-permute-done | bytes 147488 | tf_op jit(solution)/shard_map/ppermute | solution.py:279
  66.5 1.2 %sweep_stage.5 = (bf16[72,1024]{1,0:T(8,128)(2,1)S(1)}, bf16[72,1024]{1,0:T(8,128)(2,1)S(1)}) custom-call(f32[72,1024]{1,0:T(8,128)S(1)} %get-tuple-element.31.r_ref, bf16[72,1024]{1,0:T(8,128)(2,1)S(1)} %first_corr.5.ca_ref, bf16[72,1024]{1,0:T(8,128)(2,1)S(1)} %collective-permute-done.24.cb_ref, bf16[1024,1024]{1,0:T(8,128)(2,1)S(1)} %convert_element_type.55.own_ref, ...), custom_call_target="tpu_custom_call" | custom-call | flops 452984832 | bytes 4194304 | tf_op jit(solution)/shard_map/sweep_stage/pallas_call | solution.py:243
  67.7 3.1 %collective-permute-start.25 = (bf16[72,1024]{1,0:T(8,128)(2,1)S(1)}, bf16[72,1024]{1,0:T(8,128)(2,1)S(1)}, u32[]{:S(2)}, u32[]{:S(2)}) collective-permute-start(bf16[72,1024]{1,0:T(8,128)(2,1)S(1)} %get-tuple-element.32), channel_id=1, source_target_pairs={{0,16},{1,17},{2,18},{3,19},{4,20},{5,21},{6,22},{7,23},{8,24},{9,... | collective-permute-start | bytes 442376 | tf_op jit(solution)/shard_map/ppermute | solution.py:279
  70.8 2.1 %collective-permute-done.25.r_ref = bf16[72,1024]{1,0:T(8,128)(2,1)S(1)} collective-permute-done((bf16[72,1024]{1,0:T(8,128)(2,1)S(1)}, bf16[72,1024]{1,0:T(8,128)(2,1)S(1)}, u32[]{:S(2)}, u32[]{:S(2)}) %collective-permute-start.25) | collective-permute-done | bytes 147488 | tf_op jit(solution)/shard_map/ppermute | solution.py:279
  73.9 3.5 %collective-permute-done.30.cb_ref = bf16[72,1024]{1,0:T(8,128)(2,1)S(1)} collective-permute-done((bf16[72,1024]{1,0:T(8,128)(2,1)S(1)}, bf16[72,1024]{1,0:T(8,128)(2,1)S(1)}, u32[]{:S(2)}, u32[]{:S(2)}) %collective-permute-start.30) | collective-permute-done | bytes 147488 | tf_op jit(solution)/shard_map/ppermute | solution.py:279
  77.4 1.2 sweep_stage.6
  79.1 0.5 collective-permute-start.35
  79.6 2.6 %collective-permute-start.31 = (bf16[72,1024]{1,0:T(8,128)(2,1)S(1)}, bf16[72,1024]{1,0:T(8,128)(2,1)S(1)}, u32[]{:S(2)}, u32[]{:S(2)}) collective-permute-start(bf16[72,1024]{1,0:T(8,128)(2,1)S(1)} %broadcast_select_fusion.1.refs_0_), channel_id=1, source_target_pairs={{0,4},{1,5},{2,6},{3,7},{4,0},{5,1},{6,2},{7,3},{8,12},{9,13},{10,... | collective-permute-start | bytes 442376 | tf_op jit(solution)/shard_map/ppermute | solution.py:279
  82.2 1.5 %collective-permute-start.32 = (bf16[72,1024]{1,0:T(8,128)(2,1)S(1)}, bf16[72,1024]{1,0:T(8,128)(2,1)S(1)}, u32[]{:S(2)}, u32[]{:S(2)}) collective-permute-start(bf16[72,1024]{1,0:T(8,128)(2,1)S(1)} %broadcast_select_fusion.1.refs_0_), channel_id=1, source_target_pairs={{0,1},{1,0},{2,3},{3,2},{4,5},{5,4},{6,7},{7,6},{8,9},{9,8},{10,11... | collective-permute-start | bytes 442376 | tf_op jit(solution)/shard_map/ppermute | solution.py:279
  83.7 0.6 sweep_stage.7
  84.8 1.5 %collective-permute-start.33 = (bf16[72,1024]{1,0:T(8,128)(2,1)S(1)}, bf16[72,1024]{1,0:T(8,128)(2,1)S(1)}, u32[]{:S(2)}, u32[]{:S(2)}) collective-permute-start(bf16[72,1024]{1,0:T(8,128)(2,1)S(1)} %collective-permute-done.31.refs_1_), channel_id=1, source_target_pairs={{0,1},{1,0},{2,3},{3,2},{4,5},{5,4},{6,7},{7,6},{8,9},{9,8},{10,11... | collective-permute-start | bytes 442376 | tf_op jit(solution)/shard_map/ppermute | solution.py:279
  86.2 2.5 %collective-permute-start.36 = (bf16[72,1024]{1,0:T(8,128)(2,1)S(1)}, bf16[72,1024]{1,0:T(8,128)(2,1)S(1)}, u32[]{:S(2)}, u32[]{:S(2)}) collective-permute-start(bf16[72,1024]{1,0:T(8,128)(2,1)S(1)} %broadcast_select_fusion.refs_4_.refs_7_), channel_id=1, source_target_pairs={{0,4},{1,5},{2,6},{3,7},{4,0},{5,1},{6,2},{7,3},{8,12},{9,13},{10,... | collective-permute-start | bytes 442376 | tf_op jit(solution)/shard_map/ppermute | solution.py:279
  89.1 10.6 %collective-permute-start.34 = (bf16[288,1024]{1,0:T(8,128)(2,1)S(1)}, bf16[288,1024]{1,0:T(8,128)(2,1)S(1)}, u32[]{:S(2)}, u32[]{:S(2)}) collective-permute-start(bf16[288,1024]{1,0:T(8,128)(2,1)S(1)} %pad_maximum_fusion), channel_id=1, source_target_pairs={{0,8},{1,9},{2,10},{3,11},{4,12},{5,13},{6,14},{7,15},{8,0},{9,1},... | collective-permute-start | bytes 1769480 | tf_op jit(solution)/shard_map/ppermute | solution.py:279
  99.8 3.6 %collective-permute-start.40 = (bf16[216,1024]{1,0:T(8,128)(2,1)S(1)}, bf16[216,1024]{1,0:T(8,128)(2,1)S(1)}, u32[]{:S(2)}, u32[]{:S(2)}) collective-permute-start(bf16[216,1024]{1,0:T(8,128)(2,1)S(1)} %pad_maximum_fusion.1), channel_id=1, source_target_pairs={{0,8},{1,9},{2,10},{3,11},{4,12},{5,13},{6,14},{7,15},{8,0},{9,1},... | collective-permute-start | bytes 1327112 | tf_op jit(solution)/shard_map/ppermute | solution.py:279
  103.4 1.1 collective-permute-start.26
  104.6 2.5 %collective-permute-start.28 = (bf16[72,256]{1,0:T(8,128)(2,1)S(1)}, bf16[72,256]{1,0:T(8,128)(2,1)S(1)}, u32[]{:S(2)}, u32[]{:S(2)}) collective-permute-start(bf16[72,256]{1,0:T(8,128)(2,1)S(1)} %get-tuple-element.50), channel_id=1, source_target_pairs={{0,5},{1,4},{2,7},{3,6},{4,1},{5,0},{6,3},{7,2},{8,13},{9,12},{10,... | collective-permute-start | bytes 110600 | tf_op jit(solution)/shard_map/ppermute | solution.py:279
  107.7 1.5 %collective-permute-done.28.refs_3_ = bf16[72,256]{1,0:T(8,128)(2,1)S(1)} collective-permute-done((bf16[72,256]{1,0:T(8,128)(2,1)S(1)}, bf16[72,256]{1,0:T(8,128)(2,1)S(1)}, u32[]{:S(2)}, u32[]{:S(2)}) %collective-permute-start.28) | collective-permute-done | bytes 36896 | tf_op jit(solution)/shard_map/ppermute | solution.py:279
  109.2 1.8 %collective-permute-start.29 = (bf16[288,256]{1,0:T(8,128)(2,1)S(1)}, bf16[288,256]{1,0:T(8,128)(2,1)S(1)}, u32[]{:S(2)}, u32[]{:S(2)}) collective-permute-start(bf16[288,256]{1,0:T(8,128)(2,1)S(1)} %pad_maximum_fusion.3), channel_id=1, source_target_pairs={{0,8},{1,9},{2,10},{3,11},{4,12},{5,13},{6,14},{7,15},{8,0},{9,1},... | collective-permute-start | bytes 442376 | tf_op jit(solution)/shard_map/ppermute | solution.py:279
  111.0 0.6 collective-permute-done.37.refs_7_
  111.6 2.7 %collective-permute-start.38 = (bf16[72,1024]{1,0:T(8,128)(2,1)S(1)}, bf16[72,1024]{1,0:T(8,128)(2,1)S(1)}, u32[]{:S(2)}, u32[]{:S(2)}) collective-permute-start(bf16[72,1024]{1,0:T(8,128)(2,1)S(1)} %collective-permute-done.37.refs_7_), channel_id=1, source_target_pairs={{0,8},{1,9},{2,10},{3,11},{4,12},{5,13},{6,14},{7,15},{8,0},{9,1},... | collective-permute-start | bytes 442376 | tf_op jit(solution)/shard_map/ppermute | solution.py:279
  114.3 0.9 shard_map.51.after_ref
  115.2 1.9 %write_early.1 = (f32[576,1024]{1,0:T(8,128)}, f32[576,256]{1,0:T(8,128)}) custom-call(bf16[256,1024]{1,0:T(8,128)(2,1)S(1)} %copy-done, f32[576,256]{1,0:T(8,128)S(1)} %shard_map.51.after_ref, bf16[288,1024]{1,0:T(8,128)(2,1)S(1)} %collective-permute-done.34.got_ref, bf16[216,1024]{1,0:T(8,128)(2,1)S(1)} %collective-permute-done.40.got_late_ref, ...), custom_call_target="tpu_custom_call" | custom-call | tf_op jit(solution)/shard_map/write_early/pallas_call | solution.py:173
  117.2 1.2 %write_rest.1 = (f32[576,1024]{1,0:T(8,128)}, f32[576,256]{1,0:T(8,128)}) custom-call(bf16[256,1024]{1,0:T(8,128)(2,1)S(1)} %copy-done, f32[576,256]{1,0:T(8,128)S(1)} %shard_map.51.after_ref, bf16[288,1024]{1,0:T(8,128)(2,1)S(1)} %collective-permute-done.34.got_ref, ...), custom_call_target="tpu_custom_call", output_to_operand_aliasing={{0}: (12, {}), {1}: (13, {})} | custom-call | tf_op jit(solution)/shard_map/write_rest/pallas_call | solution.py:173
  (64 shorter events, 6.1 us)
Async XLA Ops:
  0.8 4.9 %copy-start = (bf16[256,1024]{1,0:T(8,128)(2,1)S(1)}, bf16[256,1024]{1,0:T(8,128)(2,1)}, u32[]{:S(2)}) copy-start(bf16[256,1024]{1,0:T(8,128)(2,1)} %a_ref.1) | copy-start | bytes 1572868
  0.8 9.9 %copy-start.1 = (f32[256,576]{0,1:T(8,128)S(1)}, f32[256,576]{0,1:T(8,128)}, u32[]{:S(2)}) copy-start(f32[256,576]{0,1:T(8,128)} %param.4) | copy-start | bytes 1769476
  0.8 2.2 %collective-permute-start = (bf16[256,1024]{1,0:T(8,128)(2,1)}, bf16[256,1024]{1,0:T(8,128)(2,1)S(1)}, u32[]{:S(2)}, u32[]{:S(2)}) collective-permute-start(bf16[256,1024]{1,0:T(8,128)(2,1)} %a_ref.1), channel_id=1, source_target_pairs={{0,8},{1,9},{2,10},{3,11},{4,12},{5,13},{6,14},{7,15},{8,0},{9,1},... | collective-permute-start | bytes 1572872 | tf_op jit(solution)/shard_map/ppermute | solution.py:279
  5.5 37.7 %collective-permute-start.5 = (bf16[1024,1024]{1,0:T(8,128)(2,1)S(1)}, bf16[1024,1024]{1,0:T(8,128)(2,1)S(1)}, u32[]{:S(2)}, u32[]{:S(2)}) collective-permute-start(bf16[1024,1024]{1,0:T(8,128)(2,1)S(1)} %convert_element_type.55.own_ref), channel_id=1, source_target_pairs={{0,8},{1,9},{2,10},{3,11},{4,12},{5,13},{6,14},{7,15},{8,0},{9,1},... | collective-permute-start | bytes 6291464 | tf_op jit(solution)/shard_map/ppermute | solution.py:279
  5.7 20.6 %collective-permute-start.9 = (bf16[256,1024]{1,0:T(8,128)(2,1)S(1)}, bf16[256,1024]{1,0:T(8,128)(2,1)S(1)}, u32[]{:S(2)}, u32[]{:S(2)}) collective-permute-start(bf16[256,1024]{1,0:T(8,128)(2,1)S(1)} %copy-done), channel_id=1, source_target_pairs={{0,1},{1,0},{2,3},{3,2},{4,5},{5,4},{6,7},{7,6},{8,9},{9,8},{10,11... | collective-permute-start | bytes 1572872 | tf_op jit(solution)/shard_map/ppermute | solution.py:279
  8.4 15.6 %collective-permute-start.4 = (bf16[256,256]{1,0:T(8,128)(2,1)S(1)}, bf16[256,256]{1,0:T(8,128)(2,1)S(1)}, u32[]{:S(2)}, u32[]{:S(2)}) collective-permute-start(bf16[256,256]{1,0:T(8,128)(2,1)S(1)} %get-tuple-element.48), channel_id=1, source_target_pairs={{0,4},{1,5},{2,6},{3,7},{4,0},{5,1},{6,2},{7,3},{8,12},{9,13},{10,... | collective-permute-start | bytes 393224 | tf_op jit(solution)/shard_map/ppermute | solution.py:279
  10.8 7.6 %collective-permute-start.1 = (bf16[72,256]{1,0:T(8,128)(2,1)S(1)}, bf16[72,256]{1,0:T(8,128)(2,1)S(1)}, u32[]{:S(2)}, u32[]{:S(2)}) collective-permute-start(bf16[72,256]{1,0:T(8,128)(2,1)S(1)} %get-tuple-element.42), channel_id=1, source_target_pairs={{0,4},{1,5},{2,6},{3,7},{4,0},{5,1},{6,2},{7,3},{8,12},{9,13},{10,... | collective-permute-start | bytes 110600 | tf_op jit(solution)/shard_map/ppermute | solution.py:279
  10.9 10.4 %collective-permute-start.2 = (bf16[72,256]{1,0:T(8,128)(2,1)S(1)}, bf16[72,256]{1,0:T(8,128)(2,1)S(1)}, u32[]{:S(2)}, u32[]{:S(2)}) collective-permute-start(bf16[72,256]{1,0:T(8,128)(2,1)S(1)} %get-tuple-element.44), channel_id=1, source_target_pairs={{0,1},{1,0},{2,3},{3,2},{4,5},{5,4},{6,7},{7,6},{8,9},{9,8},{10,11... | collective-permute-start | bytes 110600 | tf_op jit(solution)/shard_map/ppermute | solution.py:279
  18.3 5.6 %collective-permute-start.3 = (bf16[72,256]{1,0:T(8,128)(2,1)S(1)}, bf16[72,256]{1,0:T(8,128)(2,1)S(1)}, u32[]{:S(2)}, u32[]{:S(2)}) collective-permute-start(bf16[72,256]{1,0:T(8,128)(2,1)S(1)} %get-tuple-element.43), channel_id=1, source_target_pairs={{0,5},{1,4},{2,7},{3,6},{4,1},{5,0},{6,3},{7,2},{8,13},{9,12},{10,... | collective-permute-start | bytes 110600 | tf_op jit(solution)/shard_map/ppermute | solution.py:279
  21.3 14.3 %collective-permute-start.6 = (bf16[256,256]{1,0:T(8,128)(2,1)S(1)}, bf16[256,256]{1,0:T(8,128)(2,1)S(1)}, u32[]{:S(2)}, u32[]{:S(2)}) collective-permute-start(bf16[256,256]{1,0:T(8,128)(2,1)S(1)} %get-tuple-element.47), channel_id=1, source_target_pairs={{0,4},{1,5},{2,6},{3,7},{4,0},{5,1},{6,2},{7,3},{8,12},{9,13},{10,... | collective-permute-start | bytes 393224 | tf_op jit(solution)/shard_map/ppermute | solution.py:279
  23.9 14.5 %collective-permute-start.7 = (bf16[256,256]{1,0:T(8,128)(2,1)S(1)}, bf16[256,256]{1,0:T(8,128)(2,1)S(1)}, u32[]{:S(2)}, u32[]{:S(2)}) collective-permute-start(bf16[256,256]{1,0:T(8,128)(2,1)S(1)} %get-tuple-element.46), channel_id=1, source_target_pairs={{0,4},{1,5},{2,6},{3,7},{4,0},{5,1},{6,2},{7,3},{8,12},{9,13},{10,... | collective-permute-start | bytes 393224 | tf_op jit(solution)/shard_map/ppermute | solution.py:279
  23.9 17.2 %collective-permute-start.8 = (bf16[256,256]{1,0:T(8,128)(2,1)S(1)}, bf16[256,256]{1,0:T(8,128)(2,1)S(1)}, u32[]{:S(2)}, u32[]{:S(2)}) collective-permute-start(bf16[256,256]{1,0:T(8,128)(2,1)S(1)} %get-tuple-element.45), channel_id=1, source_target_pairs={{0,4},{1,5},{2,6},{3,7},{4,0},{5,1},{6,2},{7,3},{8,12},{9,13},{10,... | collective-permute-start | bytes 393224 | tf_op jit(solution)/shard_map/ppermute | solution.py:279
  26.3 27.9 %collective-permute-start.18 = (bf16[256,1024]{1,0:T(8,128)(2,1)S(1)}, bf16[256,1024]{1,0:T(8,128)(2,1)S(1)}, u32[]{:S(2)}, u32[]{:S(2)}) collective-permute-start(bf16[256,1024]{1,0:T(8,128)(2,1)S(1)} %collective-permute-done.9.refs_5_), channel_id=1, source_target_pairs={{0,8},{1,9},{2,10},{3,11},{4,12},{5,13},{6,14},{7,15},{8,0},{9,1},... | collective-permute-start | bytes 1572872 | tf_op jit(solution)/shard_map/ppermute | solution.py:279
  35.6 8.8 %collective-permute-start.11 = (bf16[256,256]{1,0:T(8,128)(2,1)S(1)}, bf16[256,256]{1,0:T(8,128)(2,1)S(1)}, u32[]{:S(2)}, u32[]{:S(2)}) collective-permute-start(bf16[256,256]{1,0:T(8,128)(2,1)S(1)} %collective-permute-done.6.refs_2_), channel_id=1, source_target_pairs={{0,1},{1,0},{2,3},{3,2},{4,5},{5,4},{6,7},{7,6},{8,9},{9,8},{10,11... | collective-permute-start | bytes 393224 | tf_op jit(solution)/shard_map/ppermute | solution.py:279
  38.4 6.0 %collective-permute-start.12 = (bf16[256,256]{1,0:T(8,128)(2,1)S(1)}, bf16[256,256]{1,0:T(8,128)(2,1)S(1)}, u32[]{:S(2)}, u32[]{:S(2)}) collective-permute-start(bf16[256,256]{1,0:T(8,128)(2,1)S(1)} %collective-permute-done.7.refs_3_), channel_id=1, source_target_pairs={{0,1},{1,0},{2,3},{3,2},{4,5},{5,4},{6,7},{7,6},{8,9},{9,8},{10,11... | collective-permute-start | bytes 393224 | tf_op jit(solution)/shard_map/ppermute | solution.py:279
  41.2 6.1 %collective-permute-start.13 = (bf16[256,256]{1,0:T(8,128)(2,1)S(1)}, bf16[256,256]{1,0:T(8,128)(2,1)S(1)}, u32[]{:S(2)}, u32[]{:S(2)}) collective-permute-start(bf16[256,256]{1,0:T(8,128)(2,1)S(1)} %collective-permute-done.8.refs_4_), channel_id=1, source_target_pairs={{0,1},{1,0},{2,3},{3,2},{4,5},{5,4},{6,7},{7,6},{8,9},{9,8},{10,11... | collective-permute-start | bytes 393224 | tf_op jit(solution)/shard_map/ppermute | solution.py:279
  43.2 5.0 %collective-permute-start.15 = (bf16[256,256]{1,0:T(8,128)(2,1)S(1)}, bf16[256,256]{1,0:T(8,128)(2,1)S(1)}, u32[]{:S(2)}, u32[]{:S(2)}) collective-permute-start(bf16[256,256]{1,0:T(8,128)(2,1)S(1)} %collective-permute-done.6.refs_2_), channel_id=1, source_target_pairs={{0,8},{1,9},{2,10},{3,11},{4,12},{5,13},{6,14},{7,15},{8,0},{9,1},... | collective-permute-start | bytes 393224 | tf_op jit(solution)/shard_map/ppermute | solution.py:279
  44.3 5.1 %collective-permute-start.16 = (bf16[256,256]{1,0:T(8,128)(2,1)S(1)}, bf16[256,256]{1,0:T(8,128)(2,1)S(1)}, u32[]{:S(2)}, u32[]{:S(2)}) collective-permute-start(bf16[256,256]{1,0:T(8,128)(2,1)S(1)} %collective-permute-done.7.refs_3_), channel_id=1, source_target_pairs={{0,8},{1,9},{2,10},{3,11},{4,12},{5,13},{6,14},{7,15},{8,0},{9,1},... | collective-permute-start | bytes 393224 | tf_op jit(solution)/shard_map/ppermute | solution.py:279
  44.4 5.3 %collective-permute-start.17 = (bf16[256,256]{1,0:T(8,128)(2,1)S(1)}, bf16[256,256]{1,0:T(8,128)(2,1)S(1)}, u32[]{:S(2)}, u32[]{:S(2)}) collective-permute-start(bf16[256,256]{1,0:T(8,128)(2,1)S(1)} %collective-permute-done.8.refs_4_), channel_id=1, source_target_pairs={{0,8},{1,9},{2,10},{3,11},{4,12},{5,13},{6,14},{7,15},{8,0},{9,1},... | collective-permute-start | bytes 393224 | tf_op jit(solution)/shard_map/ppermute | solution.py:279
  47.2 2.7 %collective-permute-start.20 = (bf16[256,256]{1,0:T(8,128)(2,1)S(1)}, bf16[256,256]{1,0:T(8,128)(2,1)S(1)}, u32[]{:S(2)}, u32[]{:S(2)}) collective-permute-start(bf16[256,256]{1,0:T(8,128)(2,1)S(1)} %collective-permute-done.11.refs_7_), channel_id=1, source_target_pairs={{0,8},{1,9},{2,10},{3,11},{4,12},{5,13},{6,14},{7,15},{8,0},{9,1},... | collective-permute-start | bytes 393224 | tf_op jit(solution)/shard_map/ppermute | solution.py:279
  48.2 5.1 %collective-permute-start.10 = (bf16[256,256]{1,0:T(8,128)(2,1)S(1)}, bf16[256,256]{1,0:T(8,128)(2,1)S(1)}, u32[]{:S(2)}, u32[]{:S(2)}) collective-permute-start(bf16[256,256]{1,0:T(8,128)(2,1)S(1)} %collective-permute-done.4.refs_1_), channel_id=1, source_target_pairs={{0,1},{1,0},{2,3},{3,2},{4,5},{5,4},{6,7},{7,6},{8,9},{9,8},{10,11... | collective-permute-start | bytes 393224 | tf_op jit(solution)/shard_map/ppermute | solution.py:279
  49.5 4.8 %collective-permute-start.21 = (bf16[256,256]{1,0:T(8,128)(2,1)S(1)}, bf16[256,256]{1,0:T(8,128)(2,1)S(1)}, u32[]{:S(2)}, u32[]{:S(2)}) collective-permute-start(bf16[256,256]{1,0:T(8,128)(2,1)S(1)} %collective-permute-done.12.refs_8_), channel_id=1, source_target_pairs={{0,8},{1,9},{2,10},{3,11},{4,12},{5,13},{6,14},{7,15},{8,0},{9,1},... | collective-permute-start | bytes 393224 | tf_op jit(solution)/shard_map/ppermute | solution.py:279
  49.8 4.5 %collective-permute-start.22 = (bf16[256,256]{1,0:T(8,128)(2,1)S(1)}, bf16[256,256]{1,0:T(8,128)(2,1)S(1)}, u32[]{:S(2)}, u32[]{:S(2)}) collective-permute-start(bf16[256,256]{1,0:T(8,128)(2,1)S(1)} %collective-permute-done.13.refs_9_), channel_id=1, source_target_pairs={{0,8},{1,9},{2,10},{3,11},{4,12},{5,13},{6,14},{7,15},{8,0},{9,1},... | collective-permute-start | bytes 393224 | tf_op jit(solution)/shard_map/ppermute | solution.py:279
  50.0 4.3 %collective-permute-start.14 = (bf16[256,256]{1,0:T(8,128)(2,1)S(1)}, bf16[256,256]{1,0:T(8,128)(2,1)S(1)}, u32[]{:S(2)}, u32[]{:S(2)}) collective-permute-start(bf16[256,256]{1,0:T(8,128)(2,1)S(1)} %collective-permute-done.4.refs_1_), channel_id=1, source_target_pairs={{0,8},{1,9},{2,10},{3,11},{4,12},{5,13},{6,14},{7,15},{8,0},{9,1},... | collective-permute-start | bytes 393224 | tf_op jit(solution)/shard_map/ppermute | solution.py:279
  53.3 1.8 %collective-permute-start.19 = (bf16[256,256]{1,0:T(8,128)(2,1)S(1)}, bf16[256,256]{1,0:T(8,128)(2,1)S(1)}, u32[]{:S(2)}, u32[]{:S(2)}) collective-permute-start(bf16[256,256]{1,0:T(8,128)(2,1)S(1)} %collective-permute-done.10.refs_6_), channel_id=1, source_target_pairs={{0,8},{1,9},{2,10},{3,11},{4,12},{5,13},{6,14},{7,15},{8,0},{9,1},... | collective-permute-start | bytes 393224 | tf_op jit(solution)/shard_map/ppermute | solution.py:279
  55.6 5.1 %collective-permute-start.23 = (bf16[72,1024]{1,0:T(8,128)(2,1)S(1)}, bf16[72,1024]{1,0:T(8,128)(2,1)S(1)}, u32[]{:S(2)}, u32[]{:S(2)}) collective-permute-start(bf16[72,1024]{1,0:T(8,128)(2,1)S(1)} %first_corr.4.ca_ref), channel_id=1, source_target_pairs={{0,2},{1,3},{2,0},{3,1},{4,6},{5,7},{6,4},{7,5},{8,10},{9,11},{10,... | collective-permute-start | bytes 442376 | tf_op jit(solution)/shard_map/ppermute | solution.py:279
  62.4 4.1 %collective-permute-start.24 = (bf16[72,1024]{1,0:T(8,128)(2,1)S(1)}, bf16[72,1024]{1,0:T(8,128)(2,1)S(1)}, u32[]{:S(2)}, u32[]{:S(2)}) collective-permute-start(bf16[72,1024]{1,0:T(8,128)(2,1)S(1)} %first_corr.5.ca_ref), channel_id=1, source_target_pairs={{0,2},{1,3},{2,0},{3,1},{4,6},{5,7},{6,4},{7,5},{8,10},{9,11},{10,... | collective-permute-start | bytes 442376 | tf_op jit(solution)/shard_map/ppermute | solution.py:279
  67.7 5.2 %collective-permute-start.25 = (bf16[72,1024]{1,0:T(8,128)(2,1)S(1)}, bf16[72,1024]{1,0:T(8,128)(2,1)S(1)}, u32[]{:S(2)}, u32[]{:S(2)}) collective-permute-start(bf16[72,1024]{1,0:T(8,128)(2,1)S(1)} %get-tuple-element.32), channel_id=1, source_target_pairs={{0,16},{1,17},{2,18},{3,19},{4,20},{5,21},{6,22},{7,23},{8,24},{9,... | collective-permute-start | bytes 442376 | tf_op jit(solution)/shard_map/ppermute | solution.py:279
  73.3 4.1 %collective-permute-start.30 = (bf16[72,1024]{1,0:T(8,128)(2,1)S(1)}, bf16[72,1024]{1,0:T(8,128)(2,1)S(1)}, u32[]{:S(2)}, u32[]{:S(2)}) collective-permute-start(bf16[72,1024]{1,0:T(8,128)(2,1)S(1)} %first_corr.6.ca_ref), channel_id=1, source_target_pairs={{0,2},{1,3},{2,0},{3,1},{4,6},{5,7},{6,4},{7,5},{8,10},{9,11},{10,... | collective-permute-start | bytes 442376 | tf_op jit(solution)/shard_map/ppermute | solution.py:279
  79.1 4.6 %collective-permute-start.35 = (bf16[72,1024]{1,0:T(8,128)(2,1)S(1)}, bf16[72,1024]{1,0:T(8,128)(2,1)S(1)}, u32[]{:S(2)}, u32[]{:S(2)}) collective-permute-start(bf16[72,1024]{1,0:T(8,128)(2,1)S(1)} %first_corr.7.ca_ref), channel_id=1, source_target_pairs={{0,2},{1,3},{2,0},{3,1},{4,6},{5,7},{6,4},{7,5},{8,10},{9,11},{10,... | collective-permute-start | bytes 442376 | tf_op jit(solution)/shard_map/ppermute | solution.py:279
  79.6 5.1 %collective-permute-start.31 = (bf16[72,1024]{1,0:T(8,128)(2,1)S(1)}, bf16[72,1024]{1,0:T(8,128)(2,1)S(1)}, u32[]{:S(2)}, u32[]{:S(2)}) collective-permute-start(bf16[72,1024]{1,0:T(8,128)(2,1)S(1)} %broadcast_select_fusion.1.refs_0_), channel_id=1, source_target_pairs={{0,4},{1,5},{2,6},{3,7},{4,0},{5,1},{6,2},{7,3},{8,12},{9,13},{10,... | collective-permute-start | bytes 442376 | tf_op jit(solution)/shard_map/ppermute | solution.py:279
  82.2 6.6 %collective-permute-start.32 = (bf16[72,1024]{1,0:T(8,128)(2,1)S(1)}, bf16[72,1024]{1,0:T(8,128)(2,1)S(1)}, u32[]{:S(2)}, u32[]{:S(2)}) collective-permute-start(bf16[72,1024]{1,0:T(8,128)(2,1)S(1)} %broadcast_select_fusion.1.refs_0_), channel_id=1, source_target_pairs={{0,1},{1,0},{2,3},{3,2},{4,5},{5,4},{6,7},{7,6},{8,9},{9,8},{10,11... | collective-permute-start | bytes 442376 | tf_op jit(solution)/shard_map/ppermute | solution.py:279
  84.8 4.3 %collective-permute-start.33 = (bf16[72,1024]{1,0:T(8,128)(2,1)S(1)}, bf16[72,1024]{1,0:T(8,128)(2,1)S(1)}, u32[]{:S(2)}, u32[]{:S(2)}) collective-permute-start(bf16[72,1024]{1,0:T(8,128)(2,1)S(1)} %collective-permute-done.31.refs_1_), channel_id=1, source_target_pairs={{0,1},{1,0},{2,3},{3,2},{4,5},{5,4},{6,7},{7,6},{8,9},{9,8},{10,11... | collective-permute-start | bytes 442376 | tf_op jit(solution)/shard_map/ppermute | solution.py:279
  86.2 13.5 %collective-permute-start.36 = (bf16[72,1024]{1,0:T(8,128)(2,1)S(1)}, bf16[72,1024]{1,0:T(8,128)(2,1)S(1)}, u32[]{:S(2)}, u32[]{:S(2)}) collective-permute-start(bf16[72,1024]{1,0:T(8,128)(2,1)S(1)} %broadcast_select_fusion.refs_4_.refs_7_), channel_id=1, source_target_pairs={{0,4},{1,5},{2,6},{3,7},{4,0},{5,1},{6,2},{7,3},{8,12},{9,13},{10,... | collective-permute-start | bytes 442376 | tf_op jit(solution)/shard_map/ppermute | solution.py:279
  88.8 11.0 %collective-permute-start.39 = (bf16[72,1024]{1,0:T(8,128)(2,1)S(1)}, bf16[72,1024]{1,0:T(8,128)(2,1)S(1)}, u32[]{:S(2)}, u32[]{:S(2)}) collective-permute-start(bf16[72,1024]{1,0:T(8,128)(2,1)S(1)} %broadcast_select_fusion.refs_4_.refs_7_), channel_id=1, source_target_pairs={{0,1},{1,0},{2,3},{3,2},{4,5},{5,4},{6,7},{7,6},{8,9},{9,8},{10,11... | collective-permute-start | bytes 442376 | tf_op jit(solution)/shard_map/ppermute | solution.py:279
  89.1 25.2 %collective-permute-start.34 = (bf16[288,1024]{1,0:T(8,128)(2,1)S(1)}, bf16[288,1024]{1,0:T(8,128)(2,1)S(1)}, u32[]{:S(2)}, u32[]{:S(2)}) collective-permute-start(bf16[288,1024]{1,0:T(8,128)(2,1)S(1)} %pad_maximum_fusion), channel_id=1, source_target_pairs={{0,8},{1,9},{2,10},{3,11},{4,12},{5,13},{6,14},{7,15},{8,0},{9,1},... | collective-permute-start | bytes 1769480 | tf_op jit(solution)/shard_map/ppermute | solution.py:279
  99.8 15.4 %collective-permute-start.40 = (bf16[216,1024]{1,0:T(8,128)(2,1)S(1)}, bf16[216,1024]{1,0:T(8,128)(2,1)S(1)}, u32[]{:S(2)}, u32[]{:S(2)}) collective-permute-start(bf16[216,1024]{1,0:T(8,128)(2,1)S(1)} %pad_maximum_fusion.1), channel_id=1, source_target_pairs={{0,8},{1,9},{2,10},{3,11},{4,12},{5,13},{6,14},{7,15},{8,0},{9,1},... | collective-permute-start | bytes 1327112 | tf_op jit(solution)/shard_map/ppermute | solution.py:279
  103.4 3.8 %collective-permute-start.26 = (bf16[72,256]{1,0:T(8,128)(2,1)S(1)}, bf16[72,256]{1,0:T(8,128)(2,1)S(1)}, u32[]{:S(2)}, u32[]{:S(2)}) collective-permute-start(bf16[72,256]{1,0:T(8,128)(2,1)S(1)} %get-tuple-element.52), channel_id=1, source_target_pairs={{0,4},{1,5},{2,6},{3,7},{4,0},{5,1},{6,2},{7,3},{8,12},{9,13},{10,... | collective-permute-start | bytes 110600 | tf_op jit(solution)/shard_map/ppermute | solution.py:279
  104.6 3.1 %collective-permute-start.27 = (bf16[72,256]{1,0:T(8,128)(2,1)S(1)}, bf16[72,256]{1,0:T(8,128)(2,1)S(1)}, u32[]{:S(2)}, u32[]{:S(2)}) collective-permute-start(bf16[72,256]{1,0:T(8,128)(2,1)S(1)} %get-tuple-element.51), channel_id=1, source_target_pairs={{0,1},{1,0},{2,3},{3,2},{4,5},{5,4},{6,7},{7,6},{8,9},{9,8},{10,11... | collective-permute-start | bytes 110600 | tf_op jit(solution)/shard_map/ppermute | solution.py:279
  104.6 4.6 %collective-permute-start.28 = (bf16[72,256]{1,0:T(8,128)(2,1)S(1)}, bf16[72,256]{1,0:T(8,128)(2,1)S(1)}, u32[]{:S(2)}, u32[]{:S(2)}) collective-permute-start(bf16[72,256]{1,0:T(8,128)(2,1)S(1)} %get-tuple-element.50), channel_id=1, source_target_pairs={{0,5},{1,4},{2,7},{3,6},{4,1},{5,0},{6,3},{7,2},{8,13},{9,12},{10,... | collective-permute-start | bytes 110600 | tf_op jit(solution)/shard_map/ppermute | solution.py:279
  107.2 4.4 %collective-permute-start.37 = (bf16[72,1024]{1,0:T(8,128)(2,1)S(1)}, bf16[72,1024]{1,0:T(8,128)(2,1)S(1)}, u32[]{:S(2)}, u32[]{:S(2)}) collective-permute-start(bf16[72,1024]{1,0:T(8,128)(2,1)S(1)} %collective-permute-done.36.refs_5_), channel_id=1, source_target_pairs={{0,1},{1,0},{2,3},{3,2},{4,5},{5,4},{6,7},{7,6},{8,9},{9,8},{10,11... | collective-permute-start | bytes 442376 | tf_op jit(solution)/shard_map/ppermute | solution.py:279
  109.2 5.1 %collective-permute-start.29 = (bf16[288,256]{1,0:T(8,128)(2,1)S(1)}, bf16[288,256]{1,0:T(8,128)(2,1)S(1)}, u32[]{:S(2)}, u32[]{:S(2)}) collective-permute-start(bf16[288,256]{1,0:T(8,128)(2,1)S(1)} %pad_maximum_fusion.3), channel_id=1, source_target_pairs={{0,8},{1,9},{2,10},{3,11},{4,12},{5,13},{6,14},{7,15},{8,0},{9,1},... | collective-permute-start | bytes 442376 | tf_op jit(solution)/shard_map/ppermute | solution.py:279
  111.6 5.6 %collective-permute-start.38 = (bf16[72,1024]{1,0:T(8,128)(2,1)S(1)}, bf16[72,1024]{1,0:T(8,128)(2,1)S(1)}, u32[]{:S(2)}, u32[]{:S(2)}) collective-permute-start(bf16[72,1024]{1,0:T(8,128)(2,1)S(1)} %collective-permute-done.37.refs_7_), channel_id=1, source_target_pairs={{0,8},{1,9},{2,10},{3,11},{4,12},{5,13},{6,14},{7,15},{8,0},{9,1},... | collective-permute-start | bytes 442376 | tf_op jit(solution)/shard_map/ppermute | solution.py:279

commit v3 on v2

--- a/solution.py
+++ b/solution.py
@@ -12,6 +12,7 @@
 BF16 = jnp.bfloat16
 CORES = 2
 PAIR = 2
+FIRST_PIECES, LAST_PIECES = 1, 2
 CUTS = (0, 2, 4, 6, 8)
 TILE = 8
 ANY = pl.BlockSpec(memory_space=pl.ANY)
@@ -358,15 +359,21 @@
             panel = permute(panel2[0], shift=CORES)
             passed = panel if passed is None else jnp.where(at_plane[step + 1], panel, passed)
 
-    def gather(pair):
-        parts = {0: pair}
-        for bit in reversed(bits):
+    def gather(kept, pieces):
+        size = feats // pieces
+        parts = {0: [kept]}
+        parts[far] = [permute(kept[:, k * size:(k + 1) * size], mask=far) for k in range(pieces)]
+        for bit in reversed(near):
             for m in list(parts):
-                parts[m ^ bit] = permute(parts[m], mask=bit)
-        return ordered([parts[m] for m in masks])
-
-    first_parts = gather(keep_first)
-    second_parts = gather(keep_second)
+                parts[m ^ bit] = [permute(x, mask=bit) for x in parts[m]]
+        return [parts[m] for m in masks]
+
+    def joined(parts):
+        return ordered([x[0] if len(x) == 1 else jnp.concatenate(x, axis=1) for x in parts])
+
+    first_parts = joined(gather(keep_first, FIRST_PIECES))
+    second_pieces = gather(keep_second, LAST_PIECES)
+    second_parts = joined(second_pieces)
     first_got = permute(jnp.concatenate(first_parts, axis=0), flip=1)
     early = max(count - 1, 1)
     got_early = permute(jnp.concatenate(second_parts[:early], axis=0), flip=1)
@@ -403,8 +410,7 @@
     known = second_parts[:early] + second_parts[:1] * (count - early)
     done = write_call(masks, tuple(range(early)), shapes, parts + [got_early] + first_parts + known)
     if early < count:
-        late = jnp.concatenate(second_parts[early:], axis=0)
-        got_late = permute(late, flip=1)
+        got_late = jnp.concatenate([permute(x, flip=1) for x in second_pieces[-1]], axis=1)
         done = write_call(
             masks,
             tuple(range(early, count)),

time: 119 us -> 121 us (1.017)
  waiting for transfers between devices: 43.9 us -> 48.1 us
  starting transfers between devices: 60.6 us -> 58.6 us
    ppermute x41 -> x44, waiting for transfers between devices: 43.9 us -> 48.1 us  [permute(): return lax.ppermute(x, ('grp', 'row'), route)]
    ppermute x41 -> x44, starting transfers between devices: 60.6 us -> 58.6 us  [permute(): return lax.ppermute(x, ('grp', 'row'), route)]
  transfers between devices with their start and end apart: 41 -> 44, of which waited for: 19 -> 18; matrix products, arithmetic and copies ran while one was open for 0% -> 0% of each run, Pallas kernels for 3% -> 1%
where the time goes in v3:
time: 121 us
  starting transfers between devices  58.6 us (48%)
  waiting for transfers between devices  48.1 us (40%)
  Pallas kernels  10.2 us (8%)
  other arithmetic  2.7 us (2%)
    ppermute x44, starting transfers between devices, permute(): return lax.ppermute(x, ('grp', 'row'), route)  58.6 us
    ppermute x44, waiting for transfers between devices, permute(): return lax.ppermute(x, ('grp', 'row'), route)  48.1 us
    pallas_call x4, Pallas kernels, stage_call(): pl.pallas_call(functools.partial(stage_kernel, layout, owner), out_shape=...  4.12 us
    pallas_call x2, Pallas kernels, write_call(): pl.pallas_call(functools.partial(write_kernel, masks, chosen, len(resume)...  3.13 us
    convert_element_type x1, other arithmetic, sweep(): square = after(precond, swapped).astype(BF16)  2.51 us
  transfers between devices with their start and end apart: 44, of which 18 were waited for; matrix products, arithmetic and copies ran while one was open for 0% of the time, Pallas kernels for 1%

profile of v3, /device:TPU:1, one launch (start us, length us, event | category | flops | bytes accessed | tf_op | source)
XLA Modules:
  0.0 120.7 jit_solution(7160048862351818239)
XLA Ops:
  0.9 2.1 %collective-permute-done.refs_10_.other_ref = bf16[256,1024]{1,0:T(8,128)(2,1)S(1)} collective-permute-done((bf16[256,1024]{1,0:T(8,128)(2,1)}, bf16[256,1024]{1,0:T(8,128)(2,1)S(1)}, u32[]{:S(2)}, u32[]{:S(2)}) %collective-permute-start) | collective-permute-done | bytes 524320 | tf_op jit(solution)/shard_map/ppermute | solution.py:280
  3.0 2.5 %convert_element_type.55.own_ref = bf16[1024,1024]{1,0:T(8,128)(2,1)S(1)} convert(f32[1024,1024]{1,0:T(8,128)} %param.5) | non-fusion elementwise | flops 1048576 | bytes 6291456 | tf_op jit(solution)/shard_map/convert_element_type | solution.py:317
  5.7 2.6 %collective-permute-start.9 = (bf16[256,1024]{1,0:T(8,128)(2,1)S(1)}, bf16[256,1024]{1,0:T(8,128)(2,1)S(1)}, u32[]{:S(2)}, u32[]{:S(2)}) collective-permute-start(bf16[256,1024]{1,0:T(8,128)(2,1)S(1)} %copy-done), channel_id=1, source_target_pairs={{0,1},{1,0},{2,3},{3,2},{4,5},{5,4},{6,7},{7,6},{8,9},{9,8},{10,11... | collective-permute-start | bytes 1572872 | tf_op jit(solution)/shard_map/ppermute | solution.py:280
  8.4 2.4 %collective-permute-start.4 = (bf16[256,256]{1,0:T(8,128)(2,1)S(1)}, bf16[256,256]{1,0:T(8,128)(2,1)S(1)}, u32[]{:S(2)}, u32[]{:S(2)}) collective-permute-start(bf16[256,256]{1,0:T(8,128)(2,1)S(1)} %get-tuple-element.48), channel_id=1, source_target_pairs={{0,4},{1,5},{2,6},{3,7},{4,0},{5,1},{6,2},{7,3},{8,12},{9,13},{10,... | collective-permute-start | bytes 393224 | tf_op jit(solution)/shard_map/ppermute | solution.py:280
  11.1 7.2 %collective-permute-done.1 = bf16[72,256]{1,0:T(8,128)(2,1)S(1)} collective-permute-done((bf16[72,256]{1,0:T(8,128)(2,1)S(1)}, bf16[72,256]{1,0:T(8,128)(2,1)S(1)}, u32[]{:S(2)}, u32[]{:S(2)}) %collective-permute-start.1) | collective-permute-done | bytes 36896 | tf_op jit(solution)/shard_map/ppermute | solution.py:280
  18.3 2.9 %collective-permute-done.2 = bf16[72,256]{1,0:T(8,128)(2,1)S(1)} collective-permute-done((bf16[72,256]{1,0:T(8,128)(2,1)S(1)}, bf16[72,256]{1,0:T(8,128)(2,1)S(1)}, u32[]{:S(2)}, u32[]{:S(2)}) %collective-permute-start.2) | collective-permute-done | bytes 36896 | tf_op jit(solution)/shard_map/ppermute | solution.py:280
  21.3 2.7 %collective-permute-start.6 = (bf16[256,256]{1,0:T(8,128)(2,1)S(1)}, bf16[256,256]{1,0:T(8,128)(2,1)S(1)}, u32[]{:S(2)}, u32[]{:S(2)}) collective-permute-start(bf16[256,256]{1,0:T(8,128)(2,1)S(1)} %get-tuple-element.47), channel_id=1, source_target_pairs={{0,4},{1,5},{2,6},{3,7},{4,0},{5,1},{6,2},{7,3},{8,12},{9,13},{10,... | collective-permute-start | bytes 393224 | tf_op jit(solution)/shard_map/ppermute | solution.py:280
  23.9 2.3 %collective-permute-start.8 = (bf16[256,256]{1,0:T(8,128)(2,1)S(1)}, bf16[256,256]{1,0:T(8,128)(2,1)S(1)}, u32[]{:S(2)}, u32[]{:S(2)}) collective-permute-start(bf16[256,256]{1,0:T(8,128)(2,1)S(1)} %get-tuple-element.45), channel_id=1, source_target_pairs={{0,4},{1,5},{2,6},{3,7},{4,0},{5,1},{6,2},{7,3},{8,12},{9,13},{10,... | collective-permute-start | bytes 393224 | tf_op jit(solution)/shard_map/ppermute | solution.py:280
  26.3 2.4 %collective-permute-start.18 = (bf16[256,1024]{1,0:T(8,128)(2,1)S(1)}, bf16[256,1024]{1,0:T(8,128)(2,1)S(1)}, u32[]{:S(2)}, u32[]{:S(2)}) collective-permute-start(bf16[256,1024]{1,0:T(8,128)(2,1)S(1)} %collective-permute-done.9.refs_5_), channel_id=1, source_target_pairs={{0,8},{1,9},{2,10},{3,11},{4,12},{5,13},{6,14},{7,15},{8,0},{9,1},... | collective-permute-start | bytes 1572872 | tf_op jit(solution)/shard_map/ppermute | solution.py:280
  28.7 6.9 %collective-permute-done.6.refs_2_ = bf16[256,256]{1,0:T(8,128)(2,1)S(1)} collective-permute-done((bf16[256,256]{1,0:T(8,128)(2,1)S(1)}, bf16[256,256]{1,0:T(8,128)(2,1)S(1)}, u32[]{:S(2)}, u32[]{:S(2)}) %collective-permute-start.6) | collective-permute-done | bytes 131104 | tf_op jit(solution)/shard_map/ppermute | solution.py:280
  35.6 2.0 %collective-permute-start.11 = (bf16[256,256]{1,0:T(8,128)(2,1)S(1)}, bf16[256,256]{1,0:T(8,128)(2,1)S(1)}, u32[]{:S(2)}, u32[]{:S(2)}) collective-permute-start(bf16[256,256]{1,0:T(8,128)(2,1)S(1)} %collective-permute-done.6.refs_2_), channel_id=1, source_target_pairs={{0,1},{1,0},{2,3},{3,2},{4,5},{5,4},{6,7},{7,6},{8,9},{9,8},{10,11... | collective-permute-start | bytes 393224 | tf_op jit(solution)/shard_map/ppermute | solution.py:280
  37.6 0.8 collective-permute-done.7.refs_3_
  38.4 2.0 %collective-permute-start.12 = (bf16[256,256]{1,0:T(8,128)(2,1)S(1)}, bf16[256,256]{1,0:T(8,128)(2,1)S(1)}, u32[]{:S(2)}, u32[]{:S(2)}) collective-permute-start(bf16[256,256]{1,0:T(8,128)(2,1)S(1)} %collective-permute-done.7.refs_3_), channel_id=1, source_target_pairs={{0,1},{1,0},{2,3},{3,2},{4,5},{5,4},{6,7},{7,6},{8,9},{9,8},{10,11... | collective-permute-start | bytes 393224 | tf_op jit(solution)/shard_map/ppermute | solution.py:280
  41.2 2.0 %collective-permute-start.13 = (bf16[256,256]{1,0:T(8,128)(2,1)S(1)}, bf16[256,256]{1,0:T(8,128)(2,1)S(1)}, u32[]{:S(2)}, u32[]{:S(2)}) collective-permute-start(bf16[256,256]{1,0:T(8,128)(2,1)S(1)} %collective-permute-done.8.refs_4_), channel_id=1, source_target_pairs={{0,1},{1,0},{2,3},{3,2},{4,5},{5,4},{6,7},{7,6},{8,9},{9,8},{10,11... | collective-permute-start | bytes 393224 | tf_op jit(solution)/shard_map/ppermute | solution.py:280
  43.2 1.1 collective-permute-start.15
  44.4 1.6 %collective-permute-start.17 = (bf16[256,256]{1,0:T(8,128)(2,1)S(1)}, bf16[256,256]{1,0:T(8,128)(2,1)S(1)}, u32[]{:S(2)}, u32[]{:S(2)}) collective-permute-start(bf16[256,256]{1,0:T(8,128)(2,1)S(1)} %collective-permute-done.8.refs_4_), channel_id=1, source_target_pairs={{0,8},{1,9},{2,10},{3,11},{4,12},{5,13},{6,14},{7,15},{8,0},{9,1},... | collective-permute-start | bytes 393224 | tf_op jit(solution)/shard_map/ppermute | solution.py:280
  46.0 1.3 %collective-permute-done.13.refs_9_ = bf16[256,256]{1,0:T(8,128)(2,1)S(1)} collective-permute-done((bf16[256,256]{1,0:T(8,128)(2,1)S(1)}, bf16[256,256]{1,0:T(8,128)(2,1)S(1)}, u32[]{:S(2)}, u32[]{:S(2)}) %collective-permute-start.13) | collective-permute-done | bytes 131104 | tf_op jit(solution)/shard_map/ppermute | solution.py:280
  47.2 1.0 collective-permute-start.20
  48.2 1.2 %collective-permute-start.10 = (bf16[256,256]{1,0:T(8,128)(2,1)S(1)}, bf16[256,256]{1,0:T(8,128)(2,1)S(1)}, u32[]{:S(2)}, u32[]{:S(2)}) collective-permute-start(bf16[256,256]{1,0:T(8,128)(2,1)S(1)} %collective-permute-done.4.refs_1_), channel_id=1, source_target_pairs={{0,1},{1,0},{2,3},{3,2},{4,5},{5,4},{6,7},{7,6},{8,9},{9,8},{10,11... | collective-permute-start | bytes 393224 | tf_op jit(solution)/shard_map/ppermute | solution.py:280
  50.3 3.0 %collective-permute-done.10.refs_6_ = bf16[256,256]{1,0:T(8,128)(2,1)S(1)} collective-permute-done((bf16[256,256]{1,0:T(8,128)(2,1)S(1)}, bf16[256,256]{1,0:T(8,128)(2,1)S(1)}, u32[]{:S(2)}, u32[]{:S(2)}) %collective-permute-start.10) | collective-permute-done | bytes 131104 | tf_op jit(solution)/shard_map/ppermute | solution.py:280
  53.3 0.9 collective-permute-start.19
  54.3 0.9 collective-permute-done.19.refs_16_
  55.7 5.0 %collective-permute-done.23.cb_ref = bf16[72,1024]{1,0:T(8,128)(2,1)S(1)} collective-permute-done((bf16[72,1024]{1,0:T(8,128)(2,1)S(1)}, bf16[72,1024]{1,0:T(8,128)(2,1)S(1)}, u32[]{:S(2)}, u32[]{:S(2)}) %collective-permute-start.23) | collective-permute-done | bytes 147488 | tf_op jit(solution)/shard_map/ppermute | solution.py:280
  60.7 1.2 sweep_stage.4
  62.6 3.9 %collective-permute-done.24.cb_ref = bf16[72,1024]{1,0:T(8,128)(2,1)S(1)} collective-permute-done((bf16[72,1024]{1,0:T(8,128)(2,1)S(1)}, bf16[72,1024]{1,0:T(8,128)(2,1)S(1)}, u32[]{:S(2)}, u32[]{:S(2)}) %collective-permute-start.24) | collective-permute-done | bytes 147488 | tf_op jit(solution)/shard_map/ppermute | solution.py:280
  66.5 1.2 sweep_stage.5
  67.7 3.1 %collective-permute-start.25 = (bf16[72,1024]{1,0:T(8,128)(2,1)S(1)}, bf16[72,1024]{1,0:T(8,128)(2,1)S(1)}, u32[]{:S(2)}, u32[]{:S(2)}) collective-permute-start(bf16[72,1024]{1,0:T(8,128)(2,1)S(1)} %get-tuple-element.32), channel_id=1, source_target_pairs={{0,16},{1,17},{2,18},{3,19},{4,20},{5,21},{6,22},{7,23},{8,24},{9,... | collective-permute-start | bytes 442376 | tf_op jit(solution)/shard_map/ppermute | solution.py:280
  70.8 2.1 %collective-permute-done.25.r_ref = bf16[72,1024]{1,0:T(8,128)(2,1)S(1)} collective-permute-done((bf16[72,1024]{1,0:T(8,128)(2,1)S(1)}, bf16[72,1024]{1,0:T(8,128)(2,1)S(1)}, u32[]{:S(2)}, u32[]{:S(2)}) %collective-permute-start.25) | collective-permute-done | bytes 147488 | tf_op jit(solution)/shard_map/ppermute | solution.py:280
  73.9 3.5 %collective-permute-done.30.cb_ref = bf16[72,1024]{1,0:T(8,128)(2,1)S(1)} collective-permute-done((bf16[72,1024]{1,0:T(8,128)(2,1)S(1)}, bf16[72,1024]{1,0:T(8,128)(2,1)S(1)}, u32[]{:S(2)}, u32[]{:S(2)}) %collective-permute-start.30) | collective-permute-done | bytes 147488 | tf_op jit(solution)/shard_map/ppermute | solution.py:280
  77.4 1.2 sweep_stage.6
  79.6 2.6 %collective-permute-start.31 = (bf16[72,1024]{1,0:T(8,128)(2,1)S(1)}, bf16[72,1024]{1,0:T(8,128)(2,1)S(1)}, u32[]{:S(2)}, u32[]{:S(2)}) collective-permute-start(bf16[72,1024]{1,0:T(8,128)(2,1)S(1)} %broadcast_select_fusion.1.refs_0_), channel_id=1, source_target_pairs={{0,4},{1,5},{2,6},{3,7},{4,0},{5,1},{6,2},{7,3},{8,12},{9,13},{10,... | collective-permute-start | bytes 442376 | tf_op jit(solution)/shard_map/ppermute | solution.py:280
  82.2 0.9 collective-permute-done.35.cb_ref
  83.8 2.3 %collective-permute-start.36 = (bf16[72,512]{1,0:T(8,128)(2,1)S(1)}, bf16[72,512]{1,0:T(8,128)(2,1)S(1)}, u32[]{:S(2)}, u32[]{:S(2)}) collective-permute-start(bf16[72,512]{1,0:T(8,128)(2,1)S(1)} %get-tuple-element.49), channel_id=1, source_target_pairs={{0,4},{1,5},{2,6},{3,7},{4,0},{5,1},{6,2},{7,3},{8,12},{9,13},{10,... | collective-permute-start | bytes 221192 | tf_op jit(solution)/shard_map/ppermute | solution.py:280
  86.3 1.4 %collective-permute-start.27 = (bf16[72,256]{1,0:T(8,128)(2,1)S(1)}, bf16[72,256]{1,0:T(8,128)(2,1)S(1)}, u32[]{:S(2)}, u32[]{:S(2)}) collective-permute-start(bf16[72,256]{1,0:T(8,128)(2,1)S(1)} %get-tuple-element.53), channel_id=1, source_target_pairs={{0,1},{1,0},{2,3},{3,2},{4,5},{5,4},{6,7},{7,6},{8,9},{9,8},{10,11... | collective-permute-start | bytes 110600 | tf_op jit(solution)/shard_map/ppermute | solution.py:280
  87.8 2.2 %collective-permute-start.39 = (bf16[72,512]{1,0:T(8,128)(2,1)S(1)}, bf16[72,512]{1,0:T(8,128)(2,1)S(1)}, u32[]{:S(2)}, u32[]{:S(2)}) collective-permute-start(bf16[72,512]{1,0:T(8,128)(2,1)S(1)} %get-tuple-element.50), channel_id=1, source_target_pairs={{0,4},{1,5},{2,6},{3,7},{4,0},{5,1},{6,2},{7,3},{8,12},{9,13},{10,... | collective-permute-start | bytes 221192 | tf_op jit(solution)/shard_map/ppermute | solution.py:280
  90.0 1.4 %collective-permute-start.33 = (bf16[72,1024]{1,0:T(8,128)(2,1)S(1)}, bf16[72,1024]{1,0:T(8,128)(2,1)S(1)}, u32[]{:S(2)}, u32[]{:S(2)}) collective-permute-start(bf16[72,1024]{1,0:T(8,128)(2,1)S(1)} %collective-permute-done.31.refs_1_), channel_id=1, source_target_pairs={{0,1},{1,0},{2,3},{3,2},{4,5},{5,4},{6,7},{7,6},{8,9},{9,8},{10,11... | collective-permute-start | bytes 442376 | tf_op jit(solution)/shard_map/ppermute | solution.py:280
  91.5 3.6 %collective-permute-done.39 = bf16[72,512]{1,0:T(8,128)(2,1)S(1)} collective-permute-done((bf16[72,512]{1,0:T(8,128)(2,1)S(1)}, bf16[72,512]{1,0:T(8,128)(2,1)S(1)}, u32[]{:S(2)}, u32[]{:S(2)}) %collective-permute-start.39) | collective-permute-done | bytes 73760 | tf_op jit(solution)/shard_map/ppermute | solution.py:280
  95.1 2.0 %collective-permute-start.42 = (bf16[72,1024]{1,0:T(8,128)(2,1)S(1)}, bf16[72,1024]{1,0:T(8,128)(2,1)S(1)}, u32[]{:S(2)}, u32[]{:S(2)}) collective-permute-start(bf16[72,1024]{1,0:T(8,128)(2,1)S(1)} %broadcast_select_fusion.refs_4_.refs_7_), channel_id=1, source_target_pairs={{0,1},{1,0},{2,3},{3,2},{4,5},{5,4},{6,7},{7,6},{8,9},{9,8},{10,11... | collective-permute-start | bytes 442376 | tf_op jit(solution)/shard_map/ppermute | solution.py:280
  97.3 6.9 %collective-permute-start.34 = (bf16[288,1024]{1,0:T(8,128)(2,1)S(1)}, bf16[288,1024]{1,0:T(8,128)(2,1)S(1)}, u32[]{:S(2)}, u32[]{:S(2)}) collective-permute-start(bf16[288,1024]{1,0:T(8,128)(2,1)S(1)} %pad_maximum_fusion), channel_id=1, source_target_pairs={{0,8},{1,9},{2,10},{3,11},{4,12},{5,13},{6,14},{7,15},{8,0},{9,1},... | collective-permute-start | bytes 1769480 | tf_op jit(solution)/shard_map/ppermute | solution.py:280
  104.2 3.7 %collective-permute-start.43 = (bf16[216,1024]{1,0:T(8,128)(2,1)S(1)}, bf16[216,1024]{1,0:T(8,128)(2,1)S(1)}, u32[]{:S(2)}, u32[]{:S(2)}) collective-permute-start(bf16[216,1024]{1,0:T(8,128)(2,1)S(1)} %pad_maximum_fusion.1), channel_id=1, source_target_pairs={{0,8},{1,9},{2,10},{3,11},{4,12},{5,13},{6,14},{7,15},{8,0},{9,1},... | collective-permute-start | bytes 1327112 | tf_op jit(solution)/shard_map/ppermute | solution.py:280
  107.9 1.6 %collective-permute-start.29 = (bf16[288,256]{1,0:T(8,128)(2,1)S(1)}, bf16[288,256]{1,0:T(8,128)(2,1)S(1)}, u32[]{:S(2)}, u32[]{:S(2)}) collective-permute-start(bf16[288,256]{1,0:T(8,128)(2,1)S(1)} %pad_maximum_fusion.3), channel_id=1, source_target_pairs={{0,8},{1,9},{2,10},{3,11},{4,12},{5,13},{6,14},{7,15},{8,0},{9,1},... | collective-permute-start | bytes 442376 | tf_op jit(solution)/shard_map/ppermute | solution.py:280
  111.0 2.2 %collective-permute-done.37 = bf16[72,512]{1,0:T(8,128)(2,1)S(1)} collective-permute-done((bf16[72,512]{1,0:T(8,128)(2,1)S(1)}, bf16[72,512]{1,0:T(8,128)(2,1)S(1)}, u32[]{:S(2)}, u32[]{:S(2)}) %collective-permute-start.37) | collective-permute-done | bytes 73760 | tf_op jit(solution)/shard_map/ppermute | solution.py:280
  113.3 1.5 %collective-permute-start.38 = (bf16[72,512]{1,0:T(8,128)(2,1)S(1)}, bf16[72,512]{1,0:T(8,128)(2,1)S(1)}, u32[]{:S(2)}, u32[]{:S(2)}) collective-permute-start(bf16[72,512]{1,0:T(8,128)(2,1)S(1)} %collective-permute-done.37), channel_id=1, source_target_pairs={{0,8},{1,9},{2,10},{3,11},{4,12},{5,13},{6,14},{7,15},{8,0},{9,1},... | collective-permute-start | bytes 221192 | tf_op jit(solution)/shard_map/ppermute | solution.py:280
  114.8 0.9 collective-permute-start.41
  115.8 0.9 collective-permute-done.41
  116.7 0.9 shard_map.51.after_ref
  117.6 1.9 %write_early.1 = (f32[576,1024]{1,0:T(8,128)}, f32[576,256]{1,0:T(8,128)}) custom-call(bf16[256,1024]{1,0:T(8,128)(2,1)S(1)} %copy-done, f32[576,256]{1,0:T(8,128)S(1)} %shard_map.51.after_ref, bf16[288,1024]{1,0:T(8,128)(2,1)S(1)} %collective-permute-done.34.got_ref, bf16[216,1024]{1,0:T(8,128)(2,1)S(1)} %collective-permute-done.43.got_late_ref, ...), custom_call_target="tpu_custom_call" | custom-call | tf_op jit(solution)/shard_map/write_early/pallas_call | solution.py:174
  119.5 1.2 %write_rest.1 = (f32[576,1024]{1,0:T(8,128)}, f32[576,256]{1,0:T(8,128)}) custom-call(bf16[256,1024]{1,0:T(8,128)(2,1)S(1)} %copy-done, f32[576,256]{1,0:T(8,128)S(1)} %shard_map.51.after_ref, bf16[288,1024]{1,0:T(8,128)(2,1)S(1)} %collective-permute-done.34.got_ref, ...), custom_call_target="tpu_custom_call", output_to_operand_aliasing={{0}: (12, {}), {1}: (13, {})} | custom-call | tf_op jit(solution)/shard_map/write_rest/pallas_call | solution.py:174
  (75 shorter events, 8.5 us)
Async XLA Ops:
  0.8 4.9 %copy-start = (bf16[256,1024]{1,0:T(8,128)(2,1)S(1)}, bf16[256,1024]{1,0:T(8,128)(2,1)}, u32[]{:S(2)}) copy-start(bf16[256,1024]{1,0:T(8,128)(2,1)} %a_ref.1) | copy-start | bytes 1572868
  0.8 9.9 %copy-start.1 = (f32[256,576]{0,1:T(8,128)S(1)}, f32[256,576]{0,1:T(8,128)}, u32[]{:S(2)}) copy-start(f32[256,576]{0,1:T(8,128)} %param.4) | copy-start | bytes 1769476
  0.8 2.2 %collective-permute-start = (bf16[256,1024]{1,0:T(8,128)(2,1)}, bf16[256,1024]{1,0:T(8,128)(2,1)S(1)}, u32[]{:S(2)}, u32[]{:S(2)}) collective-permute-start(bf16[256,1024]{1,0:T(8,128)(2,1)} %a_ref.1), channel_id=1, source_target_pairs={{0,8},{1,9},{2,10},{3,11},{4,12},{5,13},{6,14},{7,15},{8,0},{9,1},... | collective-permute-start | bytes 1572872 | tf_op jit(solution)/shard_map/ppermute | solution.py:280
  5.5 37.7 %collective-permute-start.5 = (bf16[1024,1024]{1,0:T(8,128)(2,1)S(1)}, bf16[1024,1024]{1,0:T(8,128)(2,1)S(1)}, u32[]{:S(2)}, u32[]{:S(2)}) collective-permute-start(bf16[1024,1024]{1,0:T(8,128)(2,1)S(1)} %convert_element_type.55.own_ref), channel_id=1, source_target_pairs={{0,8},{1,9},{2,10},{3,11},{4,12},{5,13},{6,14},{7,15},{8,0},{9,1},... | collective-permute-start | bytes 6291464 | tf_op jit(solution)/shard_map/ppermute | solution.py:280
  5.7 20.6 %collective-permute-start.9 = (bf16[256,1024]{1,0:T(8,128)(2,1)S(1)}, bf16[256,1024]{1,0:T(8,128)(2,1)S(1)}, u32[]{:S(2)}, u32[]{:S(2)}) collective-permute-start(bf16[256,1024]{1,0:T(8,128)(2,1)S(1)} %copy-done), channel_id=1, source_target_pairs={{0,1},{1,0},{2,3},{3,2},{4,5},{5,4},{6,7},{7,6},{8,9},{9,8},{10,11... | collective-permute-start | bytes 1572872 | tf_op jit(solution)/shard_map/ppermute | solution.py:280
  8.4 15.6 %collective-permute-start.4 = (bf16[256,256]{1,0:T(8,128)(2,1)S(1)}, bf16[256,256]{1,0:T(8,128)(2,1)S(1)}, u32[]{:S(2)}, u32[]{:S(2)}) collective-permute-start(bf16[256,256]{1,0:T(8,128)(2,1)S(1)} %get-tuple-element.48), channel_id=1, source_target_pairs={{0,4},{1,5},{2,6},{3,7},{4,0},{5,1},{6,2},{7,3},{8,12},{9,13},{10,... | collective-permute-start | bytes 393224 | tf_op jit(solution)/shard_map/ppermute | solution.py:280
  10.8 7.6 %collective-permute-start.1 = (bf16[72,256]{1,0:T(8,128)(2,1)S(1)}, bf16[72,256]{1,0:T(8,128)(2,1)S(1)}, u32[]{:S(2)}, u32[]{:S(2)}) collective-permute-start(bf16[72,256]{1,0:T(8,128)(2,1)S(1)} %get-tuple-element.42), channel_id=1, source_target_pairs={{0,4},{1,5},{2,6},{3,7},{4,0},{5,1},{6,2},{7,3},{8,12},{9,13},{10,... | collective-permute-start | bytes 110600 | tf_op jit(solution)/shard_map/ppermute | solution.py:280
  10.9 10.4 %collective-permute-start.2 = (bf16[72,256]{1,0:T(8,128)(2,1)S(1)}, bf16[72,256]{1,0:T(8,128)(2,1)S(1)}, u32[]{:S(2)}, u32[]{:S(2)}) collective-permute-start(bf16[72,256]{1,0:T(8,128)(2,1)S(1)} %get-tuple-element.44), channel_id=1, source_target_pairs={{0,1},{1,0},{2,3},{3,2},{4,5},{5,4},{6,7},{7,6},{8,9},{9,8},{10,11... | collective-permute-start | bytes 110600 | tf_op jit(solution)/shard_map/ppermute | solution.py:280
  18.3 5.6 %collective-permute-start.3 = (bf16[72,256]{1,0:T(8,128)(2,1)S(1)}, bf16[72,256]{1,0:T(8,128)(2,1)S(1)}, u32[]{:S(2)}, u32[]{:S(2)}) collective-permute-start(bf16[72,256]{1,0:T(8,128)(2,1)S(1)} %get-tuple-element.43), channel_id=1, source_target_pairs={{0,5},{1,4},{2,7},{3,6},{4,1},{5,0},{6,3},{7,2},{8,13},{9,12},{10,... | collective-permute-start | bytes 110600 | tf_op jit(solution)/shard_map/ppermute | solution.py:280
  21.3 14.3 %collective-permute-start.6 = (bf16[256,256]{1,0:T(8,128)(2,1)S(1)}, bf16[256,256]{1,0:T(8,128)(2,1)S(1)}, u32[]{:S(2)}, u32[]{:S(2)}) collective-permute-start(bf16[256,256]{1,0:T(8,128)(2,1)S(1)} %get-tuple-element.47), channel_id=1, source_target_pairs={{0,4},{1,5},{2,6},{3,7},{4,0},{5,1},{6,2},{7,3},{8,12},{9,13},{10,... | collective-permute-start | bytes 393224 | tf_op jit(solution)/shard_map/ppermute | solution.py:280
  23.9 14.5 %collective-permute-start.7 = (bf16[256,256]{1,0:T(8,128)(2,1)S(1)}, bf16[256,256]{1,0:T(8,128)(2,1)S(1)}, u32[]{:S(2)}, u32[]{:S(2)}) collective-permute-start(bf16[256,256]{1,0:T(8,128)(2,1)S(1)} %get-tuple-element.46), channel_id=1, source_target_pairs={{0,4},{1,5},{2,6},{3,7},{4,0},{5,1},{6,2},{7,3},{8,12},{9,13},{10,... | collective-permute-start | bytes 393224 | tf_op jit(solution)/shard_map/ppermute | solution.py:280
  23.9 17.2 %collective-permute-start.8 = (bf16[256,256]{1,0:T(8,128)(2,1)S(1)}, bf16[256,256]{1,0:T(8,128)(2,1)S(1)}, u32[]{:S(2)}, u32[]{:S(2)}) collective-permute-start(bf16[256,256]{1,0:T(8,128)(2,1)S(1)} %get-tuple-element.45), channel_id=1, source_target_pairs={{0,4},{1,5},{2,6},{3,7},{4,0},{5,1},{6,2},{7,3},{8,12},{9,13},{10,... | collective-permute-start | bytes 393224 | tf_op jit(solution)/shard_map/ppermute | solution.py:280
  26.3 27.9 %collective-permute-start.18 = (bf16[256,1024]{1,0:T(8,128)(2,1)S(1)}, bf16[256,1024]{1,0:T(8,128)(2,1)S(1)}, u32[]{:S(2)}, u32[]{:S(2)}) collective-permute-start(bf16[256,1024]{1,0:T(8,128)(2,1)S(1)} %collective-permute-done.9.refs_5_), channel_id=1, source_target_pairs={{0,8},{1,9},{2,10},{3,11},{4,12},{5,13},{6,14},{7,15},{8,0},{9,1},... | collective-permute-start | bytes 1572872 | tf_op jit(solution)/shard_map/ppermute | solution.py:280
  35.6 8.8 %collective-permute-start.11 = (bf16[256,256]{1,0:T(8,128)(2,1)S(1)}, bf16[256,256]{1,0:T(8,128)(2,1)S(1)}, u32[]{:S(2)}, u32[]{:S(2)}) collective-permute-start(bf16[256,256]{1,0:T(8,128)(2,1)S(1)} %collective-permute-done.6.refs_2_), channel_id=1, source_target_pairs={{0,1},{1,0},{2,3},{3,2},{4,5},{5,4},{6,7},{7,6},{8,9},{9,8},{10,11... | collective-permute-start | bytes 393224 | tf_op jit(solution)/shard_map/ppermute | solution.py:280
  38.4 6.0 %collective-permute-start.12 = (bf16[256,256]{1,0:T(8,128)(2,1)S(1)}, bf16[256,256]{1,0:T(8,128)(2,1)S(1)}, u32[]{:S(2)}, u32[]{:S(2)}) collective-permute-start(bf16[256,256]{1,0:T(8,128)(2,1)S(1)} %collective-permute-done.7.refs_3_), channel_id=1, source_target_pairs={{0,1},{1,0},{2,3},{3,2},{4,5},{5,4},{6,7},{7,6},{8,9},{9,8},{10,11... | collective-permute-start | bytes 393224 | tf_op jit(solution)/shard_map/ppermute | solution.py:280
  41.2 6.1 %collective-permute-start.13 = (bf16[256,256]{1,0:T(8,128)(2,1)S(1)}, bf16[256,256]{1,0:T(8,128)(2,1)S(1)}, u32[]{:S(2)}, u32[]{:S(2)}) collective-permute-start(bf16[256,256]{1,0:T(8,128)(2,1)S(1)} %collective-permute-done.8.refs_4_), channel_id=1, source_target_pairs={{0,1},{1,0},{2,3},{3,2},{4,5},{5,4},{6,7},{7,6},{8,9},{9,8},{10,11... | collective-permute-start | bytes 393224 | tf_op jit(solution)/shard_map/ppermute | solution.py:280
  43.2 5.0 %collective-permute-start.15 = (bf16[256,256]{1,0:T(8,128)(2,1)S(1)}, bf16[256,256]{1,0:T(8,128)(2,1)S(1)}, u32[]{:S(2)}, u32[]{:S(2)}) collective-permute-start(bf16[256,256]{1,0:T(8,128)(2,1)S(1)} %collective-permute-done.6.refs_2_), channel_id=1, source_target_pairs={{0,8},{1,9},{2,10},{3,11},{4,12},{5,13},{6,14},{7,15},{8,0},{9,1},... | collective-permute-start | bytes 393224 | tf_op jit(solution)/shard_map/ppermute | solution.py:280
  44.3 5.1 %collective-permute-start.16 = (bf16[256,256]{1,0:T(8,128)(2,1)S(1)}, bf16[256,256]{1,0:T(8,128)(2,1)S(1)}, u32[]{:S(2)}, u32[]{:S(2)}) collective-permute-start(bf16[256,256]{1,0:T(8,128)(2,1)S(1)} %collective-permute-done.7.refs_3_), channel_id=1, source_target_pairs={{0,8},{1,9},{2,10},{3,11},{4,12},{5,13},{6,14},{7,15},{8,0},{9,1},... | collective-permute-start | bytes 393224 | tf_op jit(solution)/shard_map/ppermute | solution.py:280
  44.4 5.3 %collective-permute-start.17 = (bf16[256,256]{1,0:T(8,128)(2,1)S(1)}, bf16[256,256]{1,0:T(8,128)(2,1)S(1)}, u32[]{:S(2)}, u32[]{:S(2)}) collective-permute-start(bf16[256,256]{1,0:T(8,128)(2,1)S(1)} %collective-permute-done.8.refs_4_), channel_id=1, source_target_pairs={{0,8},{1,9},{2,10},{3,11},{4,12},{5,13},{6,14},{7,15},{8,0},{9,1},... | collective-permute-start | bytes 393224 | tf_op jit(solution)/shard_map/ppermute | solution.py:280
  47.2 2.7 %collective-permute-start.20 = (bf16[256,256]{1,0:T(8,128)(2,1)S(1)}, bf16[256,256]{1,0:T(8,128)(2,1)S(1)}, u32[]{:S(2)}, u32[]{:S(2)}) collective-permute-start(bf16[256,256]{1,0:T(8,128)(2,1)S(1)} %collective-permute-done.11.refs_7_), channel_id=1, source_target_pairs={{0,8},{1,9},{2,10},{3,11},{4,12},{5,13},{6,14},{7,15},{8,0},{9,1},... | collective-permute-start | bytes 393224 | tf_op jit(solution)/shard_map/ppermute | solution.py:280
  48.2 5.1 %collective-permute-start.10 = (bf16[256,256]{1,0:T(8,128)(2,1)S(1)}, bf16[256,256]{1,0:T(8,128)(2,1)S(1)}, u32[]{:S(2)}, u32[]{:S(2)}) collective-permute-start(bf16[256,256]{1,0:T(8,128)(2,1)S(1)} %collective-permute-done.4.refs_1_), channel_id=1, source_target_pairs={{0,1},{1,0},{2,3},{3,2},{4,5},{5,4},{6,7},{7,6},{8,9},{9,8},{10,11... | collective-permute-start | bytes 393224 | tf_op jit(solution)/shard_map/ppermute | solution.py:280
  49.5 4.8 %collective-permute-start.21 = (bf16[256,256]{1,0:T(8,128)(2,1)S(1)}, bf16[256,256]{1,0:T(8,128)(2,1)S(1)}, u32[]{:S(2)}, u32[]{:S(2)}) collective-permute-start(bf16[256,256]{1,0:T(8,128)(2,1)S(1)} %collective-permute-done.12.refs_8_), channel_id=1, source_target_pairs={{0,8},{1,9},{2,10},{3,11},{4,12},{5,13},{6,14},{7,15},{8,0},{9,1},... | collective-permute-start | bytes 393224 | tf_op jit(solution)/shard_map/ppermute | solution.py:280
  49.8 4.5 %collective-permute-start.22 = (bf16[256,256]{1,0:T(8,128)(2,1)S(1)}, bf16[256,256]{1,0:T(8,128)(2,1)S(1)}, u32[]{:S(2)}, u32[]{:S(2)}) collective-permute-start(bf16[256,256]{1,0:T(8,128)(2,1)S(1)} %collective-permute-done.13.refs_9_), channel_id=1, source_target_pairs={{0,8},{1,9},{2,10},{3,11},{4,12},{5,13},{6,14},{7,15},{8,0},{9,1},... | collective-permute-start | bytes 393224 | tf_op jit(solution)/shard_map/ppermute | solution.py:280
  50.0 4.3 %collective-permute-start.14 = (bf16[256,256]{1,0:T(8,128)(2,1)S(1)}, bf16[256,256]{1,0:T(8,128)(2,1)S(1)}, u32[]{:S(2)}, u32[]{:S(2)}) collective-permute-start(bf16[256,256]{1,0:T(8,128)(2,1)S(1)} %collective-permute-done.4.refs_1_), channel_id=1, source_target_pairs={{0,8},{1,9},{2,10},{3,11},{4,12},{5,13},{6,14},{7,15},{8,0},{9,1},... | collective-permute-start | bytes 393224 | tf_op jit(solution)/shard_map/ppermute | solution.py:280
  53.3 1.8 %collective-permute-start.19 = (bf16[256,256]{1,0:T(8,128)(2,1)S(1)}, bf16[256,256]{1,0:T(8,128)(2,1)S(1)}, u32[]{:S(2)}, u32[]{:S(2)}) collective-permute-start(bf16[256,256]{1,0:T(8,128)(2,1)S(1)} %collective-permute-done.10.refs_6_), channel_id=1, source_target_pairs={{0,8},{1,9},{2,10},{3,11},{4,12},{5,13},{6,14},{7,15},{8,0},{9,1},... | collective-permute-start | bytes 393224 | tf_op jit(solution)/shard_map/ppermute | solution.py:280
  55.6 5.1 %collective-permute-start.23 = (bf16[72,1024]{1,0:T(8,128)(2,1)S(1)}, bf16[72,1024]{1,0:T(8,128)(2,1)S(1)}, u32[]{:S(2)}, u32[]{:S(2)}) collective-permute-start(bf16[72,1024]{1,0:T(8,128)(2,1)S(1)} %first_corr.4.ca_ref), channel_id=1, source_target_pairs={{0,2},{1,3},{2,0},{3,1},{4,6},{5,7},{6,4},{7,5},{8,10},{9,11},{10,... | collective-permute-start | bytes 442376 | tf_op jit(solution)/shard_map/ppermute | solution.py:280
  62.4 4.1 %collective-permute-start.24 = (bf16[72,1024]{1,0:T(8,128)(2,1)S(1)}, bf16[72,1024]{1,0:T(8,128)(2,1)S(1)}, u32[]{:S(2)}, u32[]{:S(2)}) collective-permute-start(bf16[72,1024]{1,0:T(8,128)(2,1)S(1)} %first_corr.5.ca_ref), channel_id=1, source_target_pairs={{0,2},{1,3},{2,0},{3,1},{4,6},{5,7},{6,4},{7,5},{8,10},{9,11},{10,... | collective-permute-start | bytes 442376 | tf_op jit(solution)/shard_map/ppermute | solution.py:280
  67.7 5.2 %collective-permute-start.25 = (bf16[72,1024]{1,0:T(8,128)(2,1)S(1)}, bf16[72,1024]{1,0:T(8,128)(2,1)S(1)}, u32[]{:S(2)}, u32[]{:S(2)}) collective-permute-start(bf16[72,1024]{1,0:T(8,128)(2,1)S(1)} %get-tuple-element.32), channel_id=1, source_target_pairs={{0,16},{1,17},{2,18},{3,19},{4,20},{5,21},{6,22},{7,23},{8,24},{9,... | collective-permute-start | bytes 442376 | tf_op jit(solution)/shard_map/ppermute | solution.py:280
  73.3 4.1 %collective-permute-start.30 = (bf16[72,1024]{1,0:T(8,128)(2,1)S(1)}, bf16[72,1024]{1,0:T(8,128)(2,1)S(1)}, u32[]{:S(2)}, u32[]{:S(2)}) collective-permute-start(bf16[72,1024]{1,0:T(8,128)(2,1)S(1)} %first_corr.6.ca_ref), channel_id=1, source_target_pairs={{0,2},{1,3},{2,0},{3,1},{4,6},{5,7},{6,4},{7,5},{8,10},{9,11},{10,... | collective-permute-start | bytes 442376 | tf_op jit(solution)/shard_map/ppermute | solution.py:280
  79.1 4.1 %collective-permute-start.35 = (bf16[72,1024]{1,0:T(8,128)(2,1)S(1)}, bf16[72,1024]{1,0:T(8,128)(2,1)S(1)}, u32[]{:S(2)}, u32[]{:S(2)}) collective-permute-start(bf16[72,1024]{1,0:T(8,128)(2,1)S(1)} %first_corr.7.ca_ref), channel_id=1, source_target_pairs={{0,2},{1,3},{2,0},{3,1},{4,6},{5,7},{6,4},{7,5},{8,10},{9,11},{10,... | collective-permute-start | bytes 442376 | tf_op jit(solution)/shard_map/ppermute | solution.py:280
  79.6 8.2 %collective-permute-start.31 = (bf16[72,1024]{1,0:T(8,128)(2,1)S(1)}, bf16[72,1024]{1,0:T(8,128)(2,1)S(1)}, u32[]{:S(2)}, u32[]{:S(2)}) collective-permute-start(bf16[72,1024]{1,0:T(8,128)(2,1)S(1)} %broadcast_select_fusion.1.refs_0_), channel_id=1, source_target_pairs={{0,4},{1,5},{2,6},{3,7},{4,0},{5,1},{6,2},{7,3},{8,12},{9,13},{10,... | collective-permute-start | bytes 442376 | tf_op jit(solution)/shard_map/ppermute | solution.py:280
  83.8 6.3 %collective-permute-start.36 = (bf16[72,512]{1,0:T(8,128)(2,1)S(1)}, bf16[72,512]{1,0:T(8,128)(2,1)S(1)}, u32[]{:S(2)}, u32[]{:S(2)}) collective-permute-start(bf16[72,512]{1,0:T(8,128)(2,1)S(1)} %get-tuple-element.49), channel_id=1, source_target_pairs={{0,4},{1,5},{2,6},{3,7},{4,0},{5,1},{6,2},{7,3},{8,12},{9,13},{10,... | collective-permute-start | bytes 221192 | tf_op jit(solution)/shard_map/ppermute | solution.py:280
  86.1 21.8 %collective-permute-start.26 = (bf16[72,256]{1,0:T(8,128)(2,1)S(1)}, bf16[72,256]{1,0:T(8,128)(2,1)S(1)}, u32[]{:S(2)}, u32[]{:S(2)}) collective-permute-start(bf16[72,256]{1,0:T(8,128)(2,1)S(1)} %get-tuple-element.54), channel_id=1, source_target_pairs={{0,4},{1,5},{2,6},{3,7},{4,0},{5,1},{6,2},{7,3},{8,12},{9,13},{10,... | collective-permute-start | bytes 110600 | tf_op jit(solution)/shard_map/ppermute | solution.py:280
  86.3 21.6 %collective-permute-start.27 = (bf16[72,256]{1,0:T(8,128)(2,1)S(1)}, bf16[72,256]{1,0:T(8,128)(2,1)S(1)}, u32[]{:S(2)}, u32[]{:S(2)}) collective-permute-start(bf16[72,256]{1,0:T(8,128)(2,1)S(1)} %get-tuple-element.53), channel_id=1, source_target_pairs={{0,1},{1,0},{2,3},{3,2},{4,5},{5,4},{6,7},{7,6},{8,9},{9,8},{10,11... | collective-permute-start | bytes 110600 | tf_op jit(solution)/shard_map/ppermute | solution.py:280
  87.7 9.4 %collective-permute-start.32 = (bf16[72,1024]{1,0:T(8,128)(2,1)S(1)}, bf16[72,1024]{1,0:T(8,128)(2,1)S(1)}, u32[]{:S(2)}, u32[]{:S(2)}) collective-permute-start(bf16[72,1024]{1,0:T(8,128)(2,1)S(1)} %broadcast_select_fusion.1.refs_0_), channel_id=1, source_target_pairs={{0,1},{1,0},{2,3},{3,2},{4,5},{5,4},{6,7},{7,6},{8,9},{9,8},{10,11... | collective-permute-start | bytes 442376 | tf_op jit(solution)/shard_map/ppermute | solution.py:280
  87.8 7.2 %collective-permute-start.39 = (bf16[72,512]{1,0:T(8,128)(2,1)S(1)}, bf16[72,512]{1,0:T(8,128)(2,1)S(1)}, u32[]{:S(2)}, u32[]{:S(2)}) collective-permute-start(bf16[72,512]{1,0:T(8,128)(2,1)S(1)} %get-tuple-element.50), channel_id=1, source_target_pairs={{0,4},{1,5},{2,6},{3,7},{4,0},{5,1},{6,2},{7,3},{8,12},{9,13},{10,... | collective-permute-start | bytes 221192 | tf_op jit(solution)/shard_map/ppermute | solution.py:280
  90.0 7.2 %collective-permute-start.33 = (bf16[72,1024]{1,0:T(8,128)(2,1)S(1)}, bf16[72,1024]{1,0:T(8,128)(2,1)S(1)}, u32[]{:S(2)}, u32[]{:S(2)}) collective-permute-start(bf16[72,1024]{1,0:T(8,128)(2,1)S(1)} %collective-permute-done.31.refs_1_), channel_id=1, source_target_pairs={{0,1},{1,0},{2,3},{3,2},{4,5},{5,4},{6,7},{7,6},{8,9},{9,8},{10,11... | collective-permute-start | bytes 442376 | tf_op jit(solution)/shard_map/ppermute | solution.py:280
  95.1 9.1 %collective-permute-start.42 = (bf16[72,1024]{1,0:T(8,128)(2,1)S(1)}, bf16[72,1024]{1,0:T(8,128)(2,1)S(1)}, u32[]{:S(2)}, u32[]{:S(2)}) collective-permute-start(bf16[72,1024]{1,0:T(8,128)(2,1)S(1)} %broadcast_select_fusion.refs_4_.refs_7_), channel_id=1, source_target_pairs={{0,1},{1,0},{2,3},{3,2},{4,5},{5,4},{6,7},{7,6},{8,9},{9,8},{10,11... | collective-permute-start | bytes 442376 | tf_op jit(solution)/shard_map/ppermute | solution.py:280
  97.1 10.8 %collective-permute-start.28 = (bf16[72,256]{1,0:T(8,128)(2,1)S(1)}, bf16[72,256]{1,0:T(8,128)(2,1)S(1)}, u32[]{:S(2)}, u32[]{:S(2)}) collective-permute-start(bf16[72,256]{1,0:T(8,128)(2,1)S(1)} %get-tuple-element.52), channel_id=1, source_target_pairs={{0,5},{1,4},{2,7},{3,6},{4,1},{5,0},{6,3},{7,2},{8,13},{9,12},{10,... | collective-permute-start | bytes 110600 | tf_op jit(solution)/shard_map/ppermute | solution.py:280
  97.3 19.4 %collective-permute-start.34 = (bf16[288,1024]{1,0:T(8,128)(2,1)S(1)}, bf16[288,1024]{1,0:T(8,128)(2,1)S(1)}, u32[]{:S(2)}, u32[]{:S(2)}) collective-permute-start(bf16[288,1024]{1,0:T(8,128)(2,1)S(1)} %pad_maximum_fusion), channel_id=1, source_target_pairs={{0,8},{1,9},{2,10},{3,11},{4,12},{5,13},{6,14},{7,15},{8,0},{9,1},... | collective-permute-start | bytes 1769480 | tf_op jit(solution)/shard_map/ppermute | solution.py:280
  104.2 13.4 %collective-permute-start.43 = (bf16[216,1024]{1,0:T(8,128)(2,1)S(1)}, bf16[216,1024]{1,0:T(8,128)(2,1)S(1)}, u32[]{:S(2)}, u32[]{:S(2)}) collective-permute-start(bf16[216,1024]{1,0:T(8,128)(2,1)S(1)} %pad_maximum_fusion.1), channel_id=1, source_target_pairs={{0,8},{1,9},{2,10},{3,11},{4,12},{5,13},{6,14},{7,15},{8,0},{9,1},... | collective-permute-start | bytes 1327112 | tf_op jit(solution)/shard_map/ppermute | solution.py:280
  107.9 3.1 %collective-permute-start.29 = (bf16[288,256]{1,0:T(8,128)(2,1)S(1)}, bf16[288,256]{1,0:T(8,128)(2,1)S(1)}, u32[]{:S(2)}, u32[]{:S(2)}) collective-permute-start(bf16[288,256]{1,0:T(8,128)(2,1)S(1)} %pad_maximum_fusion.3), channel_id=1, source_target_pairs={{0,8},{1,9},{2,10},{3,11},{4,12},{5,13},{6,14},{7,15},{8,0},{9,1},... | collective-permute-start | bytes 442376 | tf_op jit(solution)/shard_map/ppermute | solution.py:280
  109.5 3.7 %collective-permute-start.37 = (bf16[72,512]{1,0:T(8,128)(2,1)S(1)}, bf16[72,512]{1,0:T(8,128)(2,1)S(1)}, u32[]{:S(2)}, u32[]{:S(2)}) collective-permute-start(bf16[72,512]{1,0:T(8,128)(2,1)S(1)} %collective-permute-done.36), channel_id=1, source_target_pairs={{0,1},{1,0},{2,3},{3,2},{4,5},{5,4},{6,7},{7,6},{8,9},{9,8},{10,11... | collective-permute-start | bytes 221192 | tf_op jit(solution)/shard_map/ppermute | solution.py:280
  110.3 4.5 %collective-permute-start.40 = (bf16[72,512]{1,0:T(8,128)(2,1)S(1)}, bf16[72,512]{1,0:T(8,128)(2,1)S(1)}, u32[]{:S(2)}, u32[]{:S(2)}) collective-permute-start(bf16[72,512]{1,0:T(8,128)(2,1)S(1)} %collective-permute-done.39), channel_id=1, source_target_pairs={{0,1},{1,0},{2,3},{3,2},{4,5},{5,4},{6,7},{7,6},{8,9},{9,8},{10,11... | collective-permute-start | bytes 221192 | tf_op jit(solution)/shard_map/ppermute | solution.py:280
  113.3 2.5 %collective-permute-start.38 = (bf16[72,512]{1,0:T(8,128)(2,1)S(1)}, bf16[72,512]{1,0:T(8,128)(2,1)S(1)}, u32[]{:S(2)}, u32[]{:S(2)}) collective-permute-start(bf16[72,512]{1,0:T(8,128)(2,1)S(1)} %collective-permute-done.37), channel_id=1, source_target_pairs={{0,8},{1,9},{2,10},{3,11},{4,12},{5,13},{6,14},{7,15},{8,0},{9,1},... | collective-permute-start | bytes 221192 | tf_op jit(solution)/shard_map/ppermute | solution.py:280
  114.8 1.9 %collective-permute-start.41 = (bf16[72,512]{1,0:T(8,128)(2,1)S(1)}, bf16[72,512]{1,0:T(8,128)(2,1)S(1)}, u32[]{:S(2)}, u32[]{:S(2)}) collective-permute-start(bf16[72,512]{1,0:T(8,128)(2,1)S(1)} %collective-permute-done.40), channel_id=1, source_target_pairs={{0,8},{1,9},{2,10},{3,11},{4,12},{5,13},{6,14},{7,15},{8,0},{9,1},... | collective-permute-start | bytes 221192 | tf_op jit(solution)/shard_map/ppermute | solution.py:280

commit v4 on v3

--- a/solution.py
+++ b/solution.py
@@ -62,14 +62,14 @@
 
 def stage_kernel(layout, owner, r_ref, ca_ref, cb_ref, own_ref, other_ref, *refs):
     count = sum(layout)
-    w_ref, rn_ref = refs[2 * count], refs[2 * count + 1:]
+    w_ref, rn_ref, next_ref = refs[2 * count], refs[2 * count + 1:2 * count + 2], refs[2 * count + 2:]
     width = ca_ref.shape[0]
     total = ca_ref[...].astype(F32) + cb_ref[...].astype(F32)
     high = total.astype(BF16)
     low = (total - high.astype(F32)).astype(BF16)
     stacked = jnp.concatenate((high, low), axis=0)
 
-    def run(map_ref, blocks):
+    def run(map_ref, blocks, nexts):
         both = jnp.dot(stacked, map_ref[...], preferred_element_type=F32)
         wb = (both[:width] + both[width:]).astype(BF16)
         w_ref[...] = wb
@@ -85,14 +85,18 @@
                 change = part if change is None else change + part
                 start += size
             rn_ref[0][:, span] = (r_ref[:, span].astype(F32) - change).astype(rn_ref[0].dtype)
+        if next_ref:
+            correlation(rn_ref[0], nexts, next_ref[0])
+
+    own, other = grouped(refs[:count], layout), grouped(refs[count:2 * count], layout)
 
     @pl.when(core_is(owner))
     def _():
-        run(own_ref, grouped(refs[:count], layout))
+        run(own_ref, own, other)
 
     @pl.when(core_is(1 - owner))
     def _():
-        run(other_ref, grouped(refs[count:2 * count], layout))
+        run(other_ref, other, own)
 
 
 def product(w, a_ref):
@@ -241,6 +245,8 @@
         own, other, layout = [panel], [panel], [1]
     else:
         out_shape.append(jax.ShapeDtypeStruct(panel.shape, kind))
+    if kind == F32:
+        out_shape.append(jax.ShapeDtypeStruct((width, feats), BF16))
     return pl.pallas_call(
         functools.partial(stage_kernel, layout, owner),
         out_shape=out_shape,
@@ -305,7 +311,9 @@
     near = bits[:-1]
     count = len(masks)
     edges = [feats * e // CUTS[-1] for e in CUTS]
-    parts_of_a = [features[:, low:high] for low, high in zip(edges[:-1], edges[1:])]
+    parts_of_a = [features[:, :edges[1]]]
+    again = after(features, parts_of_a[0])
+    parts_of_a += [again[:, low:high] for low, high in zip(edges[1:-1], edges[2:])]
 
     held = {0: [features]}
     held[far] = [permute(x, mask=far) for x in parts_of_a]
@@ -347,9 +355,8 @@
         if end and passed is not None:
             blocks = [passed[:, k * rows:(k + 1) * rows] for k in range(count)]
             blocks = [permute(x, mask=m) if m else x for x, m in zip(blocks, masks)]
-        w1, panel1 = stage_call(0, layout, panel, corr, got, squares, mine, theirs, F32)
+        w1, panel1, corr = stage_call(0, layout, panel, corr, got, squares, mine, theirs, F32)
         keep_first = w1 if keep_first is None else jnp.where(at_plane[step], w1, keep_first)
-        corr = first_call(1, layout, panel1, mine, theirs)
         got = permute(corr, mask=PAIR)
         w2, *panel2 = stage_call(
             1, layout, panel1, corr, got, squares, mine, theirs, None if end else BF16

time: 121 us -> 121 us (level)
  starting transfers between devices: 58.6 us -> 59.9 us
    ppermute x44, starting transfers between devices: 58.6 us -> 59.9 us  [permute(): return lax.ppermute(x, ('grp', 'row'), route)]
  transfers between devices with their start and end apart: 44 -> 44, of which waited for: 18 -> 17; matrix products, arithmetic and copies ran while one was open for 0% -> 0% of each run, Pallas kernels for 1% -> 1%
where the time goes in v4:
time: 121 us
  starting transfers between devices  59.9 us (50%)
  waiting for transfers between devices  47.5 us (39%)
  Pallas kernels  9.86 us (8%)
  other arithmetic  2.69 us (2%)
    ppermute x44, starting transfers between devices, permute(): return lax.ppermute(x, ('grp', 'row'), route)  59.9 us
    ppermute x44, waiting for transfers between devices, permute(): return lax.ppermute(x, ('grp', 'row'), route)  47.5 us
    pallas_call x4, Pallas kernels, stage_call(): pl.pallas_call(functools.partial(stage_kernel, layout, owner), out_shape=...  4.84 us
    pallas_call x2, Pallas kernels, write_call(): pl.pallas_call(functools.partial(write_kernel, masks, chosen, len(resume)...  3.13 us
    convert_element_type x1, other arithmetic, sweep(): square = after(precond, swapped).astype(BF16)  2.51 us
  transfers between devices with their start and end apart: 44, of which 17 were waited for; matrix products, arithmetic and copies ran while one was open for 0% of the time, Pallas kernels for 1%

profile of v4, /device:TPU:1, one launch (start us, length us, event | category | flops | bytes accessed | tf_op | source)
XLA Modules:
  0.0 121.2 jit_solution(13660075325685895674)
XLA Ops:
  0.9 2.1 %collective-permute-done.refs_10_.other_ref = bf16[256,1024]{1,0:T(8,128)(2,1)S(1)} collective-permute-done((bf16[256,1024]{1,0:T(8,128)(2,1)}, bf16[256,1024]{1,0:T(8,128)(2,1)S(1)}, u32[]{:S(2)}, u32[]{:S(2)}) %collective-permute-start) | collective-permute-done | bytes 524320 | tf_op jit(solution)/shard_map/ppermute | solution.py:286
  3.0 2.5 %convert_element_type.55.own_ref = bf16[1024,1024]{1,0:T(8,128)(2,1)S(1)} convert(f32[1024,1024]{1,0:T(8,128)} %param.5) | non-fusion elementwise | flops 1048576 | bytes 6291456 | tf_op jit(solution)/shard_map/convert_element_type | solution.py:325
  5.7 2.6 %collective-permute-start.9 = (bf16[256,1024]{1,0:T(8,128)(2,1)S(1)}, bf16[256,1024]{1,0:T(8,128)(2,1)S(1)}, u32[]{:S(2)}, u32[]{:S(2)}) collective-permute-start(bf16[256,1024]{1,0:T(8,128)(2,1)S(1)} %copy-done), channel_id=1, source_target_pairs={{0,1},{1,0},{2,3},{3,2},{4,5},{5,4},{6,7},{7,6},{8,9},{9,8},{10,11... | collective-permute-start | bytes 1572872 | tf_op jit(solution)/shard_map/ppermute | solution.py:286
  8.3 2.4 %collective-permute-start.1 = (bf16[72,256]{1,0:T(8,128)(2,1)S(1)}, bf16[72,256]{1,0:T(8,128)(2,1)S(1)}, u32[]{:S(2)}, u32[]{:S(2)}) collective-permute-start(bf16[72,256]{1,0:T(8,128)(2,1)S(1)} %get-tuple-element.48), channel_id=1, source_target_pairs={{0,4},{1,5},{2,6},{3,7},{4,0},{5,1},{6,2},{7,3},{8,12},{9,13},{10,... | collective-permute-start | bytes 110600 | tf_op jit(solution)/shard_map/ppermute | solution.py:286
  11.1 1.0 collective-permute-done.1
  12.1 2.3 %collective-permute-start.3 = (bf16[72,256]{1,0:T(8,128)(2,1)S(1)}, bf16[72,256]{1,0:T(8,128)(2,1)S(1)}, u32[]{:S(2)}, u32[]{:S(2)}) collective-permute-start(bf16[72,256]{1,0:T(8,128)(2,1)S(1)} %get-tuple-element.49), channel_id=1, source_target_pairs={{0,5},{1,4},{2,7},{3,6},{4,1},{5,0},{6,3},{7,2},{8,13},{9,12},{10,... | collective-permute-start | bytes 110600 | tf_op jit(solution)/shard_map/ppermute | solution.py:286
  14.4 7.6 %collective-permute-done.2 = bf16[72,256]{1,0:T(8,128)(2,1)S(1)} collective-permute-done((bf16[72,256]{1,0:T(8,128)(2,1)S(1)}, bf16[72,256]{1,0:T(8,128)(2,1)S(1)}, u32[]{:S(2)}, u32[]{:S(2)}) %collective-permute-start.2) | collective-permute-done | bytes 36896 | tf_op jit(solution)/shard_map/ppermute | solution.py:286
  22.1 2.3 %collective-permute-start.6 = (bf16[256,256]{1,0:T(8,128)(2,1)S(1)}, bf16[256,256]{1,0:T(8,128)(2,1)S(1)}, u32[]{:S(2)}, u32[]{:S(2)}) collective-permute-start(bf16[256,256]{1,0:T(8,128)(2,1)S(1)} %get-tuple-element.53), channel_id=1, source_target_pairs={{0,4},{1,5},{2,6},{3,7},{4,0},{5,1},{6,2},{7,3},{8,12},{9,13},{10,... | collective-permute-start | bytes 393224 | tf_op jit(solution)/shard_map/ppermute | solution.py:286
  24.4 2.3 %collective-permute-start.8 = (bf16[256,256]{1,0:T(8,128)(2,1)S(1)}, bf16[256,256]{1,0:T(8,128)(2,1)S(1)}, u32[]{:S(2)}, u32[]{:S(2)}) collective-permute-start(bf16[256,256]{1,0:T(8,128)(2,1)S(1)} %get-tuple-element.51), channel_id=1, source_target_pairs={{0,4},{1,5},{2,6},{3,7},{4,0},{5,1},{6,2},{7,3},{8,12},{9,13},{10,... | collective-permute-start | bytes 393224 | tf_op jit(solution)/shard_map/ppermute | solution.py:286
  26.7 1.8 %collective-permute-start.18 = (bf16[256,1024]{1,0:T(8,128)(2,1)S(1)}, bf16[256,1024]{1,0:T(8,128)(2,1)S(1)}, u32[]{:S(2)}, u32[]{:S(2)}) collective-permute-start(bf16[256,1024]{1,0:T(8,128)(2,1)S(1)} %collective-permute-done.9.refs_5_), channel_id=1, source_target_pairs={{0,8},{1,9},{2,10},{3,11},{4,12},{5,13},{6,14},{7,15},{8,0},{9,1},... | collective-permute-start | bytes 1572872 | tf_op jit(solution)/shard_map/ppermute | solution.py:286
  28.5 7.3 %collective-permute-done.6.refs_2_ = bf16[256,256]{1,0:T(8,128)(2,1)S(1)} collective-permute-done((bf16[256,256]{1,0:T(8,128)(2,1)S(1)}, bf16[256,256]{1,0:T(8,128)(2,1)S(1)}, u32[]{:S(2)}, u32[]{:S(2)}) %collective-permute-start.6) | collective-permute-done | bytes 131104 | tf_op jit(solution)/shard_map/ppermute | solution.py:286
  35.8 1.1 collective-permute-start.11
  37.0 1.7 %collective-permute-done.7.refs_3_ = bf16[256,256]{1,0:T(8,128)(2,1)S(1)} collective-permute-done((bf16[256,256]{1,0:T(8,128)(2,1)S(1)}, bf16[256,256]{1,0:T(8,128)(2,1)S(1)}, u32[]{:S(2)}, u32[]{:S(2)}) %collective-permute-start.7) | collective-permute-done | bytes 131104 | tf_op jit(solution)/shard_map/ppermute | solution.py:286
  38.6 1.1 collective-permute-start.12
  39.8 1.7 %collective-permute-done.8.refs_4_ = bf16[256,256]{1,0:T(8,128)(2,1)S(1)} collective-permute-done((bf16[256,256]{1,0:T(8,128)(2,1)S(1)}, bf16[256,256]{1,0:T(8,128)(2,1)S(1)}, u32[]{:S(2)}, u32[]{:S(2)}) %collective-permute-start.8) | collective-permute-done | bytes 131104 | tf_op jit(solution)/shard_map/ppermute | solution.py:286
  41.5 1.1 collective-permute-start.13
  42.6 1.8 %collective-permute-start.15 = (bf16[256,256]{1,0:T(8,128)(2,1)S(1)}, bf16[256,256]{1,0:T(8,128)(2,1)S(1)}, u32[]{:S(2)}, u32[]{:S(2)}) collective-permute-start(bf16[256,256]{1,0:T(8,128)(2,1)S(1)} %collective-permute-done.6.refs_2_), channel_id=1, source_target_pairs={{0,8},{1,9},{2,10},{3,11},{4,12},{5,13},{6,14},{7,15},{8,0},{9,1},... | collective-permute-start | bytes 393224 | tf_op jit(solution)/shard_map/ppermute | solution.py:286
  44.6 2.8 %collective-permute-start.17 = (bf16[256,256]{1,0:T(8,128)(2,1)S(1)}, bf16[256,256]{1,0:T(8,128)(2,1)S(1)}, u32[]{:S(2)}, u32[]{:S(2)}) collective-permute-start(bf16[256,256]{1,0:T(8,128)(2,1)S(1)} %collective-permute-done.8.refs_4_), channel_id=1, source_target_pairs={{0,8},{1,9},{2,10},{3,11},{4,12},{5,13},{6,14},{7,15},{8,0},{9,1},... | collective-permute-start | bytes 393224 | tf_op jit(solution)/shard_map/ppermute | solution.py:286
  47.4 1.4 %collective-permute-start.20 = (bf16[256,256]{1,0:T(8,128)(2,1)S(1)}, bf16[256,256]{1,0:T(8,128)(2,1)S(1)}, u32[]{:S(2)}, u32[]{:S(2)}) collective-permute-start(bf16[256,256]{1,0:T(8,128)(2,1)S(1)} %collective-permute-done.11.refs_7_), channel_id=1, source_target_pairs={{0,8},{1,9},{2,10},{3,11},{4,12},{5,13},{6,14},{7,15},{8,0},{9,1},... | collective-permute-start | bytes 393224 | tf_op jit(solution)/shard_map/ppermute | solution.py:286
  48.8 1.1 collective-permute-start.10
  50.7 3.1 %collective-permute-done.10.refs_6_ = bf16[256,256]{1,0:T(8,128)(2,1)S(1)} collective-permute-done((bf16[256,256]{1,0:T(8,128)(2,1)S(1)}, bf16[256,256]{1,0:T(8,128)(2,1)S(1)}, u32[]{:S(2)}, u32[]{:S(2)}) %collective-permute-start.10) | collective-permute-done | bytes 131104 | tf_op jit(solution)/shard_map/ppermute | solution.py:286
  56.2 5.0 %collective-permute-done.23.cb_ref = bf16[72,1024]{1,0:T(8,128)(2,1)S(1)} collective-permute-done((bf16[72,1024]{1,0:T(8,128)(2,1)S(1)}, bf16[72,1024]{1,0:T(8,128)(2,1)S(1)}, u32[]{:S(2)}, u32[]{:S(2)}) %collective-permute-start.23) | collective-permute-done | bytes 147488 | tf_op jit(solution)/shard_map/ppermute | solution.py:286
  61.3 1.5 %sweep_stage.4 = (bf16[72,1024]{1,0:T(8,128)(2,1)S(1)}, f32[72,1024]{1,0:T(8,128)S(1)}, bf16[72,1024]{1,0:T(8,128)(2,1)S(1)}) custom-call(f32[72,1024]{1,0:T(8,128)S(1)} %pad_maximum_fusion.2.r_ref, bf16[72,1024]{1,0:T(8,128)(2,1)S(1)} %first_corr.2.ca_ref, bf16[72,1024]{1,0:T(8,128)(2,1)S(1)} %collective-permute-done.23.cb_ref, ...), custom_call_target="tpu_custom_call" | custom-call | flops 452984832 | bytes 4194304 | tf_op jit(solution)/shard_map/sweep_stage/pallas_call | solution.py:250
  63.2 3.7 %collective-permute-done.24.cb_ref = bf16[72,1024]{1,0:T(8,128)(2,1)S(1)} collective-permute-done((bf16[72,1024]{1,0:T(8,128)(2,1)S(1)}, bf16[72,1024]{1,0:T(8,128)(2,1)S(1)}, u32[]{:S(2)}, u32[]{:S(2)}) %collective-permute-start.24) | collective-permute-done | bytes 147488 | tf_op jit(solution)/shard_map/ppermute | solution.py:286
  66.9 1.2 sweep_stage.5
  68.1 3.0 %collective-permute-start.25 = (bf16[72,1024]{1,0:T(8,128)(2,1)S(1)}, bf16[72,1024]{1,0:T(8,128)(2,1)S(1)}, u32[]{:S(2)}, u32[]{:S(2)}) collective-permute-start(bf16[72,1024]{1,0:T(8,128)(2,1)S(1)} %get-tuple-element.37), channel_id=1, source_target_pairs={{0,16},{1,17},{2,18},{3,19},{4,20},{5,21},{6,22},{7,23},{8,24},{9,... | collective-permute-start | bytes 442376 | tf_op jit(solution)/shard_map/ppermute | solution.py:286
  71.1 2.1 %collective-permute-done.25.r_ref = bf16[72,1024]{1,0:T(8,128)(2,1)S(1)} collective-permute-done((bf16[72,1024]{1,0:T(8,128)(2,1)S(1)}, bf16[72,1024]{1,0:T(8,128)(2,1)S(1)}, u32[]{:S(2)}, u32[]{:S(2)}) %collective-permute-start.25) | collective-permute-done | bytes 147488 | tf_op jit(solution)/shard_map/ppermute | solution.py:286
  74.4 3.3 %collective-permute-done.30.cb_ref = bf16[72,1024]{1,0:T(8,128)(2,1)S(1)} collective-permute-done((bf16[72,1024]{1,0:T(8,128)(2,1)S(1)}, bf16[72,1024]{1,0:T(8,128)(2,1)S(1)}, u32[]{:S(2)}, u32[]{:S(2)}) %collective-permute-start.30) | collective-permute-done | bytes 147488 | tf_op jit(solution)/shard_map/ppermute | solution.py:286
  77.7 1.5 %sweep_stage.6 = (bf16[72,1024]{1,0:T(8,128)(2,1)S(1)}, f32[72,1024]{1,0:T(8,128)S(1)}, bf16[72,1024]{1,0:T(8,128)(2,1)S(1)}) custom-call(bf16[72,1024]{1,0:T(8,128)(2,1)S(1)} %collective-permute-done.25.r_ref, bf16[72,1024]{1,0:T(8,128)(2,1)S(1)} %first_corr.3.ca_ref, bf16[72,1024]{1,0:T(8,128)(2,1)S(1)} %collective-permute-done.30.cb_ref, ...), custom_call_target="tpu_custom_call" | custom-call | flops 452984832 | bytes 4194304 | tf_op jit(solution)/shard_map/sweep_stage/pallas_call | solution.py:250
  80.0 2.3 %collective-permute-start.31 = (bf16[72,1024]{1,0:T(8,128)(2,1)S(1)}, bf16[72,1024]{1,0:T(8,128)(2,1)S(1)}, u32[]{:S(2)}, u32[]{:S(2)}) collective-permute-start(bf16[72,1024]{1,0:T(8,128)(2,1)S(1)} %broadcast_select_fusion.1.refs_0_), channel_id=1, source_target_pairs={{0,4},{1,5},{2,6},{3,7},{4,0},{5,1},{6,2},{7,3},{8,12},{9,13},{10,... | collective-permute-start | bytes 442376 | tf_op jit(solution)/shard_map/ppermute | solution.py:286
  82.3 1.0 collective-permute-done.35.cb_ref
  83.9 2.2 %collective-permute-start.36 = (bf16[72,512]{1,0:T(8,128)(2,1)S(1)}, bf16[72,512]{1,0:T(8,128)(2,1)S(1)}, u32[]{:S(2)}, u32[]{:S(2)}) collective-permute-start(bf16[72,512]{1,0:T(8,128)(2,1)S(1)} %get-tuple-element.54), channel_id=1, source_target_pairs={{0,4},{1,5},{2,6},{3,7},{4,0},{5,1},{6,2},{7,3},{8,12},{9,13},{10,... | collective-permute-start | bytes 221192 | tf_op jit(solution)/shard_map/ppermute | solution.py:286
  86.4 1.3 %collective-permute-start.27 = (bf16[72,256]{1,0:T(8,128)(2,1)S(1)}, bf16[72,256]{1,0:T(8,128)(2,1)S(1)}, u32[]{:S(2)}, u32[]{:S(2)}) collective-permute-start(bf16[72,256]{1,0:T(8,128)(2,1)S(1)} %get-tuple-element.58), channel_id=1, source_target_pairs={{0,1},{1,0},{2,3},{3,2},{4,5},{5,4},{6,7},{7,6},{8,9},{9,8},{10,11... | collective-permute-start | bytes 110600 | tf_op jit(solution)/shard_map/ppermute | solution.py:286
  87.9 2.2 %collective-permute-start.39 = (bf16[72,512]{1,0:T(8,128)(2,1)S(1)}, bf16[72,512]{1,0:T(8,128)(2,1)S(1)}, u32[]{:S(2)}, u32[]{:S(2)}) collective-permute-start(bf16[72,512]{1,0:T(8,128)(2,1)S(1)} %get-tuple-element.55), channel_id=1, source_target_pairs={{0,4},{1,5},{2,6},{3,7},{4,0},{5,1},{6,2},{7,3},{8,12},{9,13},{10,... | collective-permute-start | bytes 221192 | tf_op jit(solution)/shard_map/ppermute | solution.py:286
  90.1 1.4 %collective-permute-start.33 = (bf16[72,1024]{1,0:T(8,128)(2,1)S(1)}, bf16[72,1024]{1,0:T(8,128)(2,1)S(1)}, u32[]{:S(2)}, u32[]{:S(2)}) collective-permute-start(bf16[72,1024]{1,0:T(8,128)(2,1)S(1)} %collective-permute-done.31.refs_1_), channel_id=1, source_target_pairs={{0,1},{1,0},{2,3},{3,2},{4,5},{5,4},{6,7},{7,6},{8,9},{9,8},{10,11... | collective-permute-start | bytes 442376 | tf_op jit(solution)/shard_map/ppermute | solution.py:286
  91.5 3.7 %collective-permute-done.39 = bf16[72,512]{1,0:T(8,128)(2,1)S(1)} collective-permute-done((bf16[72,512]{1,0:T(8,128)(2,1)S(1)}, bf16[72,512]{1,0:T(8,128)(2,1)S(1)}, u32[]{:S(2)}, u32[]{:S(2)}) %collective-permute-start.39) | collective-permute-done | bytes 73760 | tf_op jit(solution)/shard_map/ppermute | solution.py:286
  95.2 1.2 %collective-permute-start.42 = (bf16[72,1024]{1,0:T(8,128)(2,1)S(1)}, bf16[72,1024]{1,0:T(8,128)(2,1)S(1)}, u32[]{:S(2)}, u32[]{:S(2)}) collective-permute-start(bf16[72,1024]{1,0:T(8,128)(2,1)S(1)} %broadcast_select_fusion.refs_4_.refs_7_), channel_id=1, source_target_pairs={{0,1},{1,0},{2,3},{3,2},{4,5},{5,4},{6,7},{7,6},{8,9},{9,8},{10,11... | collective-permute-start | bytes 442376 | tf_op jit(solution)/shard_map/ppermute | solution.py:286
  96.6 7.6 %collective-permute-start.34 = (bf16[288,1024]{1,0:T(8,128)(2,1)S(1)}, bf16[288,1024]{1,0:T(8,128)(2,1)S(1)}, u32[]{:S(2)}, u32[]{:S(2)}) collective-permute-start(bf16[288,1024]{1,0:T(8,128)(2,1)S(1)} %pad_maximum_fusion), channel_id=1, source_target_pairs={{0,8},{1,9},{2,10},{3,11},{4,12},{5,13},{6,14},{7,15},{8,0},{9,1},... | collective-permute-start | bytes 1769480 | tf_op jit(solution)/shard_map/ppermute | solution.py:286
  104.3 3.6 %collective-permute-start.43 = (bf16[216,1024]{1,0:T(8,128)(2,1)S(1)}, bf16[216,1024]{1,0:T(8,128)(2,1)S(1)}, u32[]{:S(2)}, u32[]{:S(2)}) collective-permute-start(bf16[216,1024]{1,0:T(8,128)(2,1)S(1)} %pad_maximum_fusion.1), channel_id=1, source_target_pairs={{0,8},{1,9},{2,10},{3,11},{4,12},{5,13},{6,14},{7,15},{8,0},{9,1},... | collective-permute-start | bytes 1327112 | tf_op jit(solution)/shard_map/ppermute | solution.py:286
  108.0 2.0 %collective-permute-start.29 = (bf16[288,256]{1,0:T(8,128)(2,1)S(1)}, bf16[288,256]{1,0:T(8,128)(2,1)S(1)}, u32[]{:S(2)}, u32[]{:S(2)}) collective-permute-start(bf16[288,256]{1,0:T(8,128)(2,1)S(1)} %pad_maximum_fusion.3), channel_id=1, source_target_pairs={{0,8},{1,9},{2,10},{3,11},{4,12},{5,13},{6,14},{7,15},{8,0},{9,1},... | collective-permute-start | bytes 442376 | tf_op jit(solution)/shard_map/ppermute | solution.py:286
  110.4 1.1 collective-permute-start.40
  111.5 2.2 %collective-permute-done.37 = bf16[72,512]{1,0:T(8,128)(2,1)S(1)} collective-permute-done((bf16[72,512]{1,0:T(8,128)(2,1)S(1)}, bf16[72,512]{1,0:T(8,128)(2,1)S(1)}, u32[]{:S(2)}, u32[]{:S(2)}) %collective-permute-start.37) | collective-permute-done | bytes 73760 | tf_op jit(solution)/shard_map/ppermute | solution.py:286
  113.7 1.5 %collective-permute-start.38 = (bf16[72,512]{1,0:T(8,128)(2,1)S(1)}, bf16[72,512]{1,0:T(8,128)(2,1)S(1)}, u32[]{:S(2)}, u32[]{:S(2)}) collective-permute-start(bf16[72,512]{1,0:T(8,128)(2,1)S(1)} %collective-permute-done.37), channel_id=1, source_target_pairs={{0,8},{1,9},{2,10},{3,11},{4,12},{5,13},{6,14},{7,15},{8,0},{9,1},... | collective-permute-start | bytes 221192 | tf_op jit(solution)/shard_map/ppermute | solution.py:286
  115.3 0.9 collective-permute-start.41
  116.3 0.9 collective-permute-done.41
  117.2 0.9 shard_map.51.after_ref
  118.1 1.9 %write_early.1 = (f32[576,1024]{1,0:T(8,128)}, f32[576,256]{1,0:T(8,128)}) custom-call(bf16[256,1024]{1,0:T(8,128)(2,1)S(1)} %copy-done, f32[576,256]{1,0:T(8,128)S(1)} %shard_map.51.after_ref, bf16[288,1024]{1,0:T(8,128)(2,1)S(1)} %collective-permute-done.34.got_ref, bf16[216,1024]{1,0:T(8,128)(2,1)S(1)} %collective-permute-done.43.got_late_ref, ...), custom_call_target="tpu_custom_call" | custom-call | tf_op jit(solution)/shard_map/write_early/pallas_call | solution.py:178
  120.0 1.2 %write_rest.1 = (f32[576,1024]{1,0:T(8,128)}, f32[576,256]{1,0:T(8,128)}) custom-call(bf16[256,1024]{1,0:T(8,128)(2,1)S(1)} %copy-done, f32[576,256]{1,0:T(8,128)S(1)} %shard_map.51.after_ref, bf16[288,1024]{1,0:T(8,128)(2,1)S(1)} %collective-permute-done.34.got_ref, ...), custom_call_target="tpu_custom_call", output_to_operand_aliasing={{0}: (12, {}), {1}: (13, {})} | custom-call | tf_op jit(solution)/shard_map/write_rest/pallas_call | solution.py:178
  (74 shorter events, 8.2 us)
Async XLA Ops:
  0.8 4.9 %copy-start = (bf16[256,1024]{1,0:T(8,128)(2,1)S(1)}, bf16[256,1024]{1,0:T(8,128)(2,1)}, u32[]{:S(2)}) copy-start(bf16[256,1024]{1,0:T(8,128)(2,1)} %a_ref.1) | copy-start | bytes 1572868
  0.8 7.5 %copy-start.1 = (f32[256,576]{0,1:T(8,128)S(1)}, f32[256,576]{0,1:T(8,128)}, u32[]{:S(2)}) copy-start(f32[256,576]{0,1:T(8,128)} %param.4) | copy-start | bytes 1769476
  0.8 2.2 %collective-permute-start = (bf16[256,1024]{1,0:T(8,128)(2,1)}, bf16[256,1024]{1,0:T(8,128)(2,1)S(1)}, u32[]{:S(2)}, u32[]{:S(2)}) collective-permute-start(bf16[256,1024]{1,0:T(8,128)(2,1)} %a_ref.1), channel_id=1, source_target_pairs={{0,8},{1,9},{2,10},{3,11},{4,12},{5,13},{6,14},{7,15},{8,0},{9,1},... | collective-permute-start | bytes 1572872 | tf_op jit(solution)/shard_map/ppermute | solution.py:286
  5.5 37.1 %collective-permute-start.5 = (bf16[1024,1024]{1,0:T(8,128)(2,1)S(1)}, bf16[1024,1024]{1,0:T(8,128)(2,1)S(1)}, u32[]{:S(2)}, u32[]{:S(2)}) collective-permute-start(bf16[1024,1024]{1,0:T(8,128)(2,1)S(1)} %convert_element_type.55.own_ref), channel_id=1, source_target_pairs={{0,8},{1,9},{2,10},{3,11},{4,12},{5,13},{6,14},{7,15},{8,0},{9,1},... | collective-permute-start | bytes 6291464 | tf_op jit(solution)/shard_map/ppermute | solution.py:286
  5.7 21.0 %collective-permute-start.9 = (bf16[256,1024]{1,0:T(8,128)(2,1)S(1)}, bf16[256,1024]{1,0:T(8,128)(2,1)S(1)}, u32[]{:S(2)}, u32[]{:S(2)}) collective-permute-start(bf16[256,1024]{1,0:T(8,128)(2,1)S(1)} %copy-done), channel_id=1, source_target_pairs={{0,1},{1,0},{2,3},{3,2},{4,5},{5,4},{6,7},{7,6},{8,9},{9,8},{10,11... | collective-permute-start | bytes 1572872 | tf_op jit(solution)/shard_map/ppermute | solution.py:286
  8.3 3.8 %collective-permute-start.1 = (bf16[72,256]{1,0:T(8,128)(2,1)S(1)}, bf16[72,256]{1,0:T(8,128)(2,1)S(1)}, u32[]{:S(2)}, u32[]{:S(2)}) collective-permute-start(bf16[72,256]{1,0:T(8,128)(2,1)S(1)} %get-tuple-element.48), channel_id=1, source_target_pairs={{0,4},{1,5},{2,6},{3,7},{4,0},{5,1},{6,2},{7,3},{8,12},{9,13},{10,... | collective-permute-start | bytes 110600 | tf_op jit(solution)/shard_map/ppermute | solution.py:286
  10.7 13.7 %collective-permute-start.4 = (bf16[256,256]{1,0:T(8,128)(2,1)S(1)}, bf16[256,256]{1,0:T(8,128)(2,1)S(1)}, u32[]{:S(2)}, u32[]{:S(2)}) collective-permute-start(bf16[256,256]{1,0:T(8,128)(2,1)S(1)} %slice.30), channel_id=1, source_target_pairs={{0,4},{1,5},{2,6},{3,7},{4,0},{5,1},{6,2},{7,3},{8,12},{9,13},{10,... | collective-permute-start | bytes 393224 | tf_op jit(solution)/shard_map/ppermute | solution.py:286
  10.9 11.2 %collective-permute-start.2 = (bf16[72,256]{1,0:T(8,128)(2,1)S(1)}, bf16[72,256]{1,0:T(8,128)(2,1)S(1)}, u32[]{:S(2)}, u32[]{:S(2)}) collective-permute-start(bf16[72,256]{1,0:T(8,128)(2,1)S(1)} %get-tuple-element.50), channel_id=1, source_target_pairs={{0,1},{1,0},{2,3},{3,2},{4,5},{5,4},{6,7},{7,6},{8,9},{9,8},{10,11... | collective-permute-start | bytes 110600 | tf_op jit(solution)/shard_map/ppermute | solution.py:286
  12.1 12.2 %collective-permute-start.3 = (bf16[72,256]{1,0:T(8,128)(2,1)S(1)}, bf16[72,256]{1,0:T(8,128)(2,1)S(1)}, u32[]{:S(2)}, u32[]{:S(2)}) collective-permute-start(bf16[72,256]{1,0:T(8,128)(2,1)S(1)} %get-tuple-element.49), channel_id=1, source_target_pairs={{0,5},{1,4},{2,7},{3,6},{4,1},{5,0},{6,3},{7,2},{8,13},{9,12},{10,... | collective-permute-start | bytes 110600 | tf_op jit(solution)/shard_map/ppermute | solution.py:286
  22.1 13.8 %collective-permute-start.6 = (bf16[256,256]{1,0:T(8,128)(2,1)S(1)}, bf16[256,256]{1,0:T(8,128)(2,1)S(1)}, u32[]{:S(2)}, u32[]{:S(2)}) collective-permute-start(bf16[256,256]{1,0:T(8,128)(2,1)S(1)} %get-tuple-element.53), channel_id=1, source_target_pairs={{0,4},{1,5},{2,6},{3,7},{4,0},{5,1},{6,2},{7,3},{8,12},{9,13},{10,... | collective-permute-start | bytes 393224 | tf_op jit(solution)/shard_map/ppermute | solution.py:286
  24.3 14.3 %collective-permute-start.7 = (bf16[256,256]{1,0:T(8,128)(2,1)S(1)}, bf16[256,256]{1,0:T(8,128)(2,1)S(1)}, u32[]{:S(2)}, u32[]{:S(2)}) collective-permute-start(bf16[256,256]{1,0:T(8,128)(2,1)S(1)} %get-tuple-element.52), channel_id=1, source_target_pairs={{0,4},{1,5},{2,6},{3,7},{4,0},{5,1},{6,2},{7,3},{8,12},{9,13},{10,... | collective-permute-start | bytes 393224 | tf_op jit(solution)/shard_map/ppermute | solution.py:286
  24.4 17.0 %collective-permute-start.8 = (bf16[256,256]{1,0:T(8,128)(2,1)S(1)}, bf16[256,256]{1,0:T(8,128)(2,1)S(1)}, u32[]{:S(2)}, u32[]{:S(2)}) collective-permute-start(bf16[256,256]{1,0:T(8,128)(2,1)S(1)} %get-tuple-element.51), channel_id=1, source_target_pairs={{0,4},{1,5},{2,6},{3,7},{4,0},{5,1},{6,2},{7,3},{8,12},{9,13},{10,... | collective-permute-start | bytes 393224 | tf_op jit(solution)/shard_map/ppermute | solution.py:286
  26.7 28.1 %collective-permute-start.18 = (bf16[256,1024]{1,0:T(8,128)(2,1)S(1)}, bf16[256,1024]{1,0:T(8,128)(2,1)S(1)}, u32[]{:S(2)}, u32[]{:S(2)}) collective-permute-start(bf16[256,1024]{1,0:T(8,128)(2,1)S(1)} %collective-permute-done.9.refs_5_), channel_id=1, source_target_pairs={{0,8},{1,9},{2,10},{3,11},{4,12},{5,13},{6,14},{7,15},{8,0},{9,1},... | collective-permute-start | bytes 1572872 | tf_op jit(solution)/shard_map/ppermute | solution.py:286
  35.8 8.5 %collective-permute-start.11 = (bf16[256,256]{1,0:T(8,128)(2,1)S(1)}, bf16[256,256]{1,0:T(8,128)(2,1)S(1)}, u32[]{:S(2)}, u32[]{:S(2)}) collective-permute-start(bf16[256,256]{1,0:T(8,128)(2,1)S(1)} %collective-permute-done.6.refs_2_), channel_id=1, source_target_pairs={{0,1},{1,0},{2,3},{3,2},{4,5},{5,4},{6,7},{7,6},{8,9},{9,8},{10,11... | collective-permute-start | bytes 393224 | tf_op jit(solution)/shard_map/ppermute | solution.py:286
  38.6 5.9 %collective-permute-start.12 = (bf16[256,256]{1,0:T(8,128)(2,1)S(1)}, bf16[256,256]{1,0:T(8,128)(2,1)S(1)}, u32[]{:S(2)}, u32[]{:S(2)}) collective-permute-start(bf16[256,256]{1,0:T(8,128)(2,1)S(1)} %collective-permute-done.7.refs_3_), channel_id=1, source_target_pairs={{0,1},{1,0},{2,3},{3,2},{4,5},{5,4},{6,7},{7,6},{8,9},{9,8},{10,11... | collective-permute-start | bytes 393224 | tf_op jit(solution)/shard_map/ppermute | solution.py:286
  41.5 5.9 %collective-permute-start.13 = (bf16[256,256]{1,0:T(8,128)(2,1)S(1)}, bf16[256,256]{1,0:T(8,128)(2,1)S(1)}, u32[]{:S(2)}, u32[]{:S(2)}) collective-permute-start(bf16[256,256]{1,0:T(8,128)(2,1)S(1)} %collective-permute-done.8.refs_4_), channel_id=1, source_target_pairs={{0,1},{1,0},{2,3},{3,2},{4,5},{5,4},{6,7},{7,6},{8,9},{9,8},{10,11... | collective-permute-start | bytes 393224 | tf_op jit(solution)/shard_map/ppermute | solution.py:286
  42.6 6.2 %collective-permute-start.15 = (bf16[256,256]{1,0:T(8,128)(2,1)S(1)}, bf16[256,256]{1,0:T(8,128)(2,1)S(1)}, u32[]{:S(2)}, u32[]{:S(2)}) collective-permute-start(bf16[256,256]{1,0:T(8,128)(2,1)S(1)} %collective-permute-done.6.refs_2_), channel_id=1, source_target_pairs={{0,8},{1,9},{2,10},{3,11},{4,12},{5,13},{6,14},{7,15},{8,0},{9,1},... | collective-permute-start | bytes 393224 | tf_op jit(solution)/shard_map/ppermute | solution.py:286
  44.4 5.5 %collective-permute-start.16 = (bf16[256,256]{1,0:T(8,128)(2,1)S(1)}, bf16[256,256]{1,0:T(8,128)(2,1)S(1)}, u32[]{:S(2)}, u32[]{:S(2)}) collective-permute-start(bf16[256,256]{1,0:T(8,128)(2,1)S(1)} %collective-permute-done.7.refs_3_), channel_id=1, source_target_pairs={{0,8},{1,9},{2,10},{3,11},{4,12},{5,13},{6,14},{7,15},{8,0},{9,1},... | collective-permute-start | bytes 393224 | tf_op jit(solution)/shard_map/ppermute | solution.py:286
  44.6 5.6 %collective-permute-start.17 = (bf16[256,256]{1,0:T(8,128)(2,1)S(1)}, bf16[256,256]{1,0:T(8,128)(2,1)S(1)}, u32[]{:S(2)}, u32[]{:S(2)}) collective-permute-start(bf16[256,256]{1,0:T(8,128)(2,1)S(1)} %collective-permute-done.8.refs_4_), channel_id=1, source_target_pairs={{0,8},{1,9},{2,10},{3,11},{4,12},{5,13},{6,14},{7,15},{8,0},{9,1},... | collective-permute-start | bytes 393224 | tf_op jit(solution)/shard_map/ppermute | solution.py:286
  47.4 3.1 %collective-permute-start.20 = (bf16[256,256]{1,0:T(8,128)(2,1)S(1)}, bf16[256,256]{1,0:T(8,128)(2,1)S(1)}, u32[]{:S(2)}, u32[]{:S(2)}) collective-permute-start(bf16[256,256]{1,0:T(8,128)(2,1)S(1)} %collective-permute-done.11.refs_7_), channel_id=1, source_target_pairs={{0,8},{1,9},{2,10},{3,11},{4,12},{5,13},{6,14},{7,15},{8,0},{9,1},... | collective-permute-start | bytes 393224 | tf_op jit(solution)/shard_map/ppermute | solution.py:286
  48.8 5.1 %collective-permute-start.10 = (bf16[256,256]{1,0:T(8,128)(2,1)S(1)}, bf16[256,256]{1,0:T(8,128)(2,1)S(1)}, u32[]{:S(2)}, u32[]{:S(2)}) collective-permute-start(bf16[256,256]{1,0:T(8,128)(2,1)S(1)} %collective-permute-done.4.refs_1_), channel_id=1, source_target_pairs={{0,1},{1,0},{2,3},{3,2},{4,5},{5,4},{6,7},{7,6},{8,9},{9,8},{10,11... | collective-permute-start | bytes 393224 | tf_op jit(solution)/shard_map/ppermute | solution.py:286
  49.9 4.9 %collective-permute-start.21 = (bf16[256,256]{1,0:T(8,128)(2,1)S(1)}, bf16[256,256]{1,0:T(8,128)(2,1)S(1)}, u32[]{:S(2)}, u32[]{:S(2)}) collective-permute-start(bf16[256,256]{1,0:T(8,128)(2,1)S(1)} %collective-permute-done.12.refs_8_), channel_id=1, source_target_pairs={{0,8},{1,9},{2,10},{3,11},{4,12},{5,13},{6,14},{7,15},{8,0},{9,1},... | collective-permute-start | bytes 393224 | tf_op jit(solution)/shard_map/ppermute | solution.py:286
  50.2 4.6 %collective-permute-start.22 = (bf16[256,256]{1,0:T(8,128)(2,1)S(1)}, bf16[256,256]{1,0:T(8,128)(2,1)S(1)}, u32[]{:S(2)}, u32[]{:S(2)}) collective-permute-start(bf16[256,256]{1,0:T(8,128)(2,1)S(1)} %collective-permute-done.13.refs_9_), channel_id=1, source_target_pairs={{0,8},{1,9},{2,10},{3,11},{4,12},{5,13},{6,14},{7,15},{8,0},{9,1},... | collective-permute-start | bytes 393224 | tf_op jit(solution)/shard_map/ppermute | solution.py:286
  50.4 4.4 %collective-permute-start.14 = (bf16[256,256]{1,0:T(8,128)(2,1)S(1)}, bf16[256,256]{1,0:T(8,128)(2,1)S(1)}, u32[]{:S(2)}, u32[]{:S(2)}) collective-permute-start(bf16[256,256]{1,0:T(8,128)(2,1)S(1)} %collective-permute-done.4.refs_1_), channel_id=1, source_target_pairs={{0,8},{1,9},{2,10},{3,11},{4,12},{5,13},{6,14},{7,15},{8,0},{9,1},... | collective-permute-start | bytes 393224 | tf_op jit(solution)/shard_map/ppermute | solution.py:286
  53.8 1.8 %collective-permute-start.19 = (bf16[256,256]{1,0:T(8,128)(2,1)S(1)}, bf16[256,256]{1,0:T(8,128)(2,1)S(1)}, u32[]{:S(2)}, u32[]{:S(2)}) collective-permute-start(bf16[256,256]{1,0:T(8,128)(2,1)S(1)} %collective-permute-done.10.refs_6_), channel_id=1, source_target_pairs={{0,8},{1,9},{2,10},{3,11},{4,12},{5,13},{6,14},{7,15},{8,0},{9,1},... | collective-permute-start | bytes 393224 | tf_op jit(solution)/shard_map/ppermute | solution.py:286
  56.2 5.1 %collective-permute-start.23 = (bf16[72,1024]{1,0:T(8,128)(2,1)S(1)}, bf16[72,1024]{1,0:T(8,128)(2,1)S(1)}, u32[]{:S(2)}, u32[]{:S(2)}) collective-permute-start(bf16[72,1024]{1,0:T(8,128)(2,1)S(1)} %first_corr.2.ca_ref), channel_id=1, source_target_pairs={{0,2},{1,3},{2,0},{3,1},{4,6},{5,7},{6,4},{7,5},{8,10},{9,11},{10,... | collective-permute-start | bytes 442376 | tf_op jit(solution)/shard_map/ppermute | solution.py:286
  62.8 4.1 %collective-permute-start.24 = (bf16[72,1024]{1,0:T(8,128)(2,1)S(1)}, bf16[72,1024]{1,0:T(8,128)(2,1)S(1)}, u32[]{:S(2)}, u32[]{:S(2)}) collective-permute-start(bf16[72,1024]{1,0:T(8,128)(2,1)S(1)} %get-tuple-element.36.ca_ref), channel_id=1, source_target_pairs={{0,2},{1,3},{2,0},{3,1},{4,6},{5,7},{6,4},{7,5},{8,10},{9,11},{10,... | collective-permute-start | bytes 442376 | tf_op jit(solution)/shard_map/ppermute | solution.py:286
  68.1 5.1 %collective-permute-start.25 = (bf16[72,1024]{1,0:T(8,128)(2,1)S(1)}, bf16[72,1024]{1,0:T(8,128)(2,1)S(1)}, u32[]{:S(2)}, u32[]{:S(2)}) collective-permute-start(bf16[72,1024]{1,0:T(8,128)(2,1)S(1)} %get-tuple-element.37), channel_id=1, source_target_pairs={{0,16},{1,17},{2,18},{3,19},{4,20},{5,21},{6,22},{7,23},{8,24},{9,... | collective-permute-start | bytes 442376 | tf_op jit(solution)/shard_map/ppermute | solution.py:286
  73.6 4.1 %collective-permute-start.30 = (bf16[72,1024]{1,0:T(8,128)(2,1)S(1)}, bf16[72,1024]{1,0:T(8,128)(2,1)S(1)}, u32[]{:S(2)}, u32[]{:S(2)}) collective-permute-start(bf16[72,1024]{1,0:T(8,128)(2,1)S(1)} %first_corr.3.ca_ref), channel_id=1, source_target_pairs={{0,2},{1,3},{2,0},{3,1},{4,6},{5,7},{6,4},{7,5},{8,10},{9,11},{10,... | collective-permute-start | bytes 442376 | tf_op jit(solution)/shard_map/ppermute | solution.py:286
  79.3 4.1 %collective-permute-start.35 = (bf16[72,1024]{1,0:T(8,128)(2,1)S(1)}, bf16[72,1024]{1,0:T(8,128)(2,1)S(1)}, u32[]{:S(2)}, u32[]{:S(2)}) collective-permute-start(bf16[72,1024]{1,0:T(8,128)(2,1)S(1)} %get-tuple-element.42.ca_ref), channel_id=1, source_target_pairs={{0,2},{1,3},{2,0},{3,1},{4,6},{5,7},{6,4},{7,5},{8,10},{9,11},{10,... | collective-permute-start | bytes 442376 | tf_op jit(solution)/shard_map/ppermute | solution.py:286
  80.0 7.9 %collective-permute-start.31 = (bf16[72,1024]{1,0:T(8,128)(2,1)S(1)}, bf16[72,1024]{1,0:T(8,128)(2,1)S(1)}, u32[]{:S(2)}, u32[]{:S(2)}) collective-permute-start(bf16[72,1024]{1,0:T(8,128)(2,1)S(1)} %broadcast_select_fusion.1.refs_0_), channel_id=1, source_target_pairs={{0,4},{1,5},{2,6},{3,7},{4,0},{5,1},{6,2},{7,3},{8,12},{9,13},{10,... | collective-permute-start | bytes 442376 | tf_op jit(solution)/shard_map/ppermute | solution.py:286
  83.9 6.2 %collective-permute-start.36 = (bf16[72,512]{1,0:T(8,128)(2,1)S(1)}, bf16[72,512]{1,0:T(8,128)(2,1)S(1)}, u32[]{:S(2)}, u32[]{:S(2)}) collective-permute-start(bf16[72,512]{1,0:T(8,128)(2,1)S(1)} %get-tuple-element.54), channel_id=1, source_target_pairs={{0,4},{1,5},{2,6},{3,7},{4,0},{5,1},{6,2},{7,3},{8,12},{9,13},{10,... | collective-permute-start | bytes 221192 | tf_op jit(solution)/shard_map/ppermute | solution.py:286
  86.2 21.8 %collective-permute-start.26 = (bf16[72,256]{1,0:T(8,128)(2,1)S(1)}, bf16[72,256]{1,0:T(8,128)(2,1)S(1)}, u32[]{:S(2)}, u32[]{:S(2)}) collective-permute-start(bf16[72,256]{1,0:T(8,128)(2,1)S(1)} %get-tuple-element.59), channel_id=1, source_target_pairs={{0,4},{1,5},{2,6},{3,7},{4,0},{5,1},{6,2},{7,3},{8,12},{9,13},{10,... | collective-permute-start | bytes 110600 | tf_op jit(solution)/shard_map/ppermute | solution.py:286
  86.4 21.5 %collective-permute-start.27 = (bf16[72,256]{1,0:T(8,128)(2,1)S(1)}, bf16[72,256]{1,0:T(8,128)(2,1)S(1)}, u32[]{:S(2)}, u32[]{:S(2)}) collective-permute-start(bf16[72,256]{1,0:T(8,128)(2,1)S(1)} %get-tuple-element.58), channel_id=1, source_target_pairs={{0,1},{1,0},{2,3},{3,2},{4,5},{5,4},{6,7},{7,6},{8,9},{9,8},{10,11... | collective-permute-start | bytes 110600 | tf_op jit(solution)/shard_map/ppermute | solution.py:286
  87.8 8.7 %collective-permute-start.32 = (bf16[72,1024]{1,0:T(8,128)(2,1)S(1)}, bf16[72,1024]{1,0:T(8,128)(2,1)S(1)}, u32[]{:S(2)}, u32[]{:S(2)}) collective-permute-start(bf16[72,1024]{1,0:T(8,128)(2,1)S(1)} %broadcast_select_fusion.1.refs_0_), channel_id=1, source_target_pairs={{0,1},{1,0},{2,3},{3,2},{4,5},{5,4},{6,7},{7,6},{8,9},{9,8},{10,11... | collective-permute-start | bytes 442376 | tf_op jit(solution)/shard_map/ppermute | solution.py:286
  87.9 7.3 %collective-permute-start.39 = (bf16[72,512]{1,0:T(8,128)(2,1)S(1)}, bf16[72,512]{1,0:T(8,128)(2,1)S(1)}, u32[]{:S(2)}, u32[]{:S(2)}) collective-permute-start(bf16[72,512]{1,0:T(8,128)(2,1)S(1)} %get-tuple-element.55), channel_id=1, source_target_pairs={{0,4},{1,5},{2,6},{3,7},{4,0},{5,1},{6,2},{7,3},{8,12},{9,13},{10,... | collective-permute-start | bytes 221192 | tf_op jit(solution)/shard_map/ppermute | solution.py:286
  90.1 6.5 %collective-permute-start.33 = (bf16[72,1024]{1,0:T(8,128)(2,1)S(1)}, bf16[72,1024]{1,0:T(8,128)(2,1)S(1)}, u32[]{:S(2)}, u32[]{:S(2)}) collective-permute-start(bf16[72,1024]{1,0:T(8,128)(2,1)S(1)} %collective-permute-done.31.refs_1_), channel_id=1, source_target_pairs={{0,1},{1,0},{2,3},{3,2},{4,5},{5,4},{6,7},{7,6},{8,9},{9,8},{10,11... | collective-permute-start | bytes 442376 | tf_op jit(solution)/shard_map/ppermute | solution.py:286
  95.2 9.0 %collective-permute-start.42 = (bf16[72,1024]{1,0:T(8,128)(2,1)S(1)}, bf16[72,1024]{1,0:T(8,128)(2,1)S(1)}, u32[]{:S(2)}, u32[]{:S(2)}) collective-permute-start(bf16[72,1024]{1,0:T(8,128)(2,1)S(1)} %broadcast_select_fusion.refs_4_.refs_7_), channel_id=1, source_target_pairs={{0,1},{1,0},{2,3},{3,2},{4,5},{5,4},{6,7},{7,6},{8,9},{9,8},{10,11... | collective-permute-start | bytes 442376 | tf_op jit(solution)/shard_map/ppermute | solution.py:286
  96.5 11.5 %collective-permute-start.28 = (bf16[72,256]{1,0:T(8,128)(2,1)S(1)}, bf16[72,256]{1,0:T(8,128)(2,1)S(1)}, u32[]{:S(2)}, u32[]{:S(2)}) collective-permute-start(bf16[72,256]{1,0:T(8,128)(2,1)S(1)} %get-tuple-element.57), channel_id=1, source_target_pairs={{0,5},{1,4},{2,7},{3,6},{4,1},{5,0},{6,3},{7,2},{8,13},{9,12},{10,... | collective-permute-start | bytes 110600 | tf_op jit(solution)/shard_map/ppermute | solution.py:286
  96.6 20.5 %collective-permute-start.34 = (bf16[288,1024]{1,0:T(8,128)(2,1)S(1)}, bf16[288,1024]{1,0:T(8,128)(2,1)S(1)}, u32[]{:S(2)}, u32[]{:S(2)}) collective-permute-start(bf16[288,1024]{1,0:T(8,128)(2,1)S(1)} %pad_maximum_fusion), channel_id=1, source_target_pairs={{0,8},{1,9},{2,10},{3,11},{4,12},{5,13},{6,14},{7,15},{8,0},{9,1},... | collective-permute-start | bytes 1769480 | tf_op jit(solution)/shard_map/ppermute | solution.py:286
  104.3 13.7 %collective-permute-start.43 = (bf16[216,1024]{1,0:T(8,128)(2,1)S(1)}, bf16[216,1024]{1,0:T(8,128)(2,1)S(1)}, u32[]{:S(2)}, u32[]{:S(2)}) collective-permute-start(bf16[216,1024]{1,0:T(8,128)(2,1)S(1)} %pad_maximum_fusion.1), channel_id=1, source_target_pairs={{0,8},{1,9},{2,10},{3,11},{4,12},{5,13},{6,14},{7,15},{8,0},{9,1},... | collective-permute-start | bytes 1327112 | tf_op jit(solution)/shard_map/ppermute | solution.py:286
  108.0 3.5 %collective-permute-start.29 = (bf16[288,256]{1,0:T(8,128)(2,1)S(1)}, bf16[288,256]{1,0:T(8,128)(2,1)S(1)}, u32[]{:S(2)}, u32[]{:S(2)}) collective-permute-start(bf16[288,256]{1,0:T(8,128)(2,1)S(1)} %pad_maximum_fusion.3), channel_id=1, source_target_pairs={{0,8},{1,9},{2,10},{3,11},{4,12},{5,13},{6,14},{7,15},{8,0},{9,1},... | collective-permute-start | bytes 442376 | tf_op jit(solution)/shard_map/ppermute | solution.py:286
  110.0 3.7 %collective-permute-start.37 = (bf16[72,512]{1,0:T(8,128)(2,1)S(1)}, bf16[72,512]{1,0:T(8,128)(2,1)S(1)}, u32[]{:S(2)}, u32[]{:S(2)}) collective-permute-start(bf16[72,512]{1,0:T(8,128)(2,1)S(1)} %collective-permute-done.36), channel_id=1, source_target_pairs={{0,1},{1,0},{2,3},{3,2},{4,5},{5,4},{6,7},{7,6},{8,9},{9,8},{10,11... | collective-permute-start | bytes 221192 | tf_op jit(solution)/shard_map/ppermute | solution.py:286
  110.4 4.9 %collective-permute-start.40 = (bf16[72,512]{1,0:T(8,128)(2,1)S(1)}, bf16[72,512]{1,0:T(8,128)(2,1)S(1)}, u32[]{:S(2)}, u32[]{:S(2)}) collective-permute-start(bf16[72,512]{1,0:T(8,128)(2,1)S(1)} %collective-permute-done.39), channel_id=1, source_target_pairs={{0,1},{1,0},{2,3},{3,2},{4,5},{5,4},{6,7},{7,6},{8,9},{9,8},{10,11... | collective-permute-start | bytes 221192 | tf_op jit(solution)/shard_map/ppermute | solution.py:286
  113.7 2.5 %collective-permute-start.38 = (bf16[72,512]{1,0:T(8,128)(2,1)S(1)}, bf16[72,512]{1,0:T(8,128)(2,1)S(1)}, u32[]{:S(2)}, u32[]{:S(2)}) collective-permute-start(bf16[72,512]{1,0:T(8,128)(2,1)S(1)} %collective-permute-done.37), channel_id=1, source_target_pairs={{0,8},{1,9},{2,10},{3,11},{4,12},{5,13},{6,14},{7,15},{8,0},{9,1},... | collective-permute-start | bytes 221192 | tf_op jit(solution)/shard_map/ppermute | solution.py:286
  115.3 1.9 %collective-permute-start.41 = (bf16[72,512]{1,0:T(8,128)(2,1)S(1)}, bf16[72,512]{1,0:T(8,128)(2,1)S(1)}, u32[]{:S(2)}, u32[]{:S(2)}) collective-permute-start(bf16[72,512]{1,0:T(8,128)(2,1)S(1)} %collective-permute-done.40), channel_id=1, source_target_pairs={{0,8},{1,9},{2,10},{3,11},{4,12},{5,13},{6,14},{7,15},{8,0},{9,1},... | collective-permute-start | bytes 221192 | tf_op jit(solution)/shard_map/ppermute | solution.py:286
